TPU v7x, 256 devices: a whole 4x4x8 slice. The times are simulated.
256 devices in a mesh: tm: 64 (over z, y, core), state: 4 (over x).
Axes of the slice: x: 4, y: 4, z: 8, core: 2. Of those that a mesh axis runs over, the one named last changes fastest.
Arguments:
- updated_spread: float32 [256, 512, 512], P('tm', 'state'), may hold values from -1 to 1, as said below
- inverse_prior_spread: float32 [256, 512, 512], P('tm', 'state'), may hold values from -1 to 1, as said below
- dynamics_tiles: float32 [256, 8, 64, 128], P('tm', 'state'), may hold values from -0.15625 to 0.15625
- tile_column_ids: int32 [256, 8, 2], P('tm'), may hold values from 0 to 7, all different within a row
- updated_average: float32 [256, 512], P('tm', 'state'), may hold values from -1.5 to 1.5
- prior_average: float32 [256, 512], P('tm', 'state'), may hold values from -1.5 to 1.5
Outputs:
- smoothed_mean: float32 [256, 512], P('tm', 'state')
Inputs may be any that keep to these rules, and one draw needn't show every extreme that they name: `updated_spread`: each filtered covariance is exactly symmetric. `inverse_prior_spread`: each predicted precision is exactly symmetric. `tile_column_ids`: the 2 block columns listed for one block row differ.
All inputs are finite; a program needn't handle non-finite values.
Results may differ from a plain program's by a relative error of at most 0.0003.
Values sent between devices are 32-bit elements; how exact they have to be, the bound alone decides.
No kernel may reach another device: no remote copies, remote signals or barrier semaphores. Data moves between devices by JAX's collectives and lax.ppermute only.
A program may use at most 192 MiB of HBM per device.

v0:
```python
import jax
import jax.numpy as jnp
from jax import lax
from jax.sharding import PartitionSpec as P

finest_accuracy = lax.Precision.HIGHEST


def carried_in(shard, axis, combine, identity):
    length, place = (lax.axis_size(axis), lax.axis_index(axis))
    everything = jax.tree.map(lambda part: lax.all_gather(part, axis), shard)
    start = jax.tree.map(
        lambda part, zero: jnp.broadcast_to(jnp.asarray(zero, part.dtype), part.shape),
        shard,
        identity,
    )

    def lap(k, before):
        at = length - 1 - k
        reached = at > place
        new = combine(before, jax.tree.map(lambda part: part[at], everything))
        return jax.tree.map(lambda a, b: jnp.where(reached, a, b), new, before)

    return lax.fori_loop(0, length, lap, start)


def pick_rows(blocks_of, indices):
    return jnp.take(blocks_of, indices.reshape(-1), axis=0)


def on_device(
    updated_spread,
    inverse_prior_spread,
    dynamics_tiles,
    tile_column_ids,
    updated_average,
    prior_average,
):
    steps_here, share, state_width = updated_spread.shape
    blocks_here = dynamics_tiles.shape[1]
    block_size = dynamics_tiles.shape[2]
    nonzero_count = tile_column_ids.shape[2]
    block_count = state_width // block_size
    state_pos = lax.axis_index("state")
    time_pos = lax.axis_index("tm")
    last_mask = (time_pos == lax.axis_size("tm") - 1) & (jnp.arange(steps_here) == steps_here - 1)
    cov_full, mean_full, pmean_full = (
        lax.all_gather(updated_spread, "state", axis=1, tiled=True),
        lax.all_gather(updated_average, "state", axis=1, tiled=True),
        lax.all_gather(prior_average, "state", axis=1, tiled=True),
    )
    own_columns = lax.dynamic_slice_in_dim(tile_column_ids, state_pos * blocks_here, blocks_here, 1)
    cov_blocks = cov_full.reshape(steps_here, block_count, block_size, state_width)
    chosen = jax.vmap(pick_rows)(cov_blocks, own_columns)
    chosen = chosen.reshape(steps_here, blocks_here, nonzero_count * block_size, state_width)
    mixed_rows = jnp.einsum("krau,krus->kras", dynamics_tiles, chosen, precision=finest_accuracy)
    sparse_apply = updated_spread + mixed_rows.reshape(steps_here, share, state_width)
    partial_value = jnp.einsum(
        "mad,mab->mdb", sparse_apply, inverse_prior_spread, precision=finest_accuracy
    )
    gain_full = lax.psum(partial_value, "state")
    offsets = mean_full - jnp.einsum("ksj,kj->ks", gain_full, pmean_full, precision=finest_accuracy)
    gain_full = jnp.where(last_mask[:, None, None], jnp.zeros_like(gain_full), gain_full)
    offsets = jnp.where(last_mask[:, None], mean_full, offsets)
    block_gain = gain_full[steps_here - 1]
    block_start_position = offsets[steps_here - 1]
    for position in range(steps_here - 2, -1, -1):
        block_start_position = offsets[position] + jnp.dot(
            gain_full[position], block_start_position, precision=finest_accuracy
        )
        block_gain = jnp.dot(gain_full[position], block_gain, precision=finest_accuracy)

    def combine(earlier, latter):
        return (
            jnp.dot(latter[0], earlier[0], precision=finest_accuracy),
            jnp.dot(latter[0], earlier[1], precision=finest_accuracy) + latter[1],
        )

    identity = (jnp.eye(state_width, dtype=jnp.float32), jnp.zeros((state_width,), jnp.float32))
    boundary_value = carried_in((block_gain, block_start_position), "tm", combine, identity)[1]
    current = boundary_value
    pieces = []
    for position in range(steps_here - 1, -1, -1):
        current = (
            jnp.dot(gain_full[position], current, precision=finest_accuracy) + offsets[position]
        )
        pieces.append(current)
    refined_result = jnp.stack(pieces[::-1])
    return lax.dynamic_slice_in_dim(refined_result, state_pos * share, share, 1)


def solution(mesh):
    return jax.shard_map(
        on_device,
        mesh=mesh,
        in_specs=(
            P("tm", "state", None),
            P("tm", "state", None),
            P("tm", "state", None, None),
            P("tm", None, None),
            P("tm", "state"),
            P("tm", "state"),
        ),
        out_specs=P("tm", "state"),
        check_vma=False,
    )
```

profile of v0, /device:TPU:1, one launch (start us, length us, event | category | flops | bytes accessed | tf_op | source)
XLA Modules:
  0.0 582.1 jit_solution(9812976212404710192)
XLA Ops:
  8.7 55.1 %all-gather.6.cloned.1.call-done = f32[4,512,512]{2,1,0:T(8,128)} async-done(((f32[4,128,512]{2,1,0:T(8,128)}), f32[4,512,512]{2,1,0:T(8,128)}) %all-gather.6.cloned.1.call-update) | async-done | bytes 4194320 | tf_op jit(solution)/shard_map/all_gather | solution.py:48
  63.8 2.9 gather_fusion
  69.5 5.0 fusion.30
  74.6 98.4 %all-reduce.2.cloned.1.call-done = f32[4,512,512]{2,1,0:T(8,128)} async-done(((f32[4,512,512]{2,1,0:T(8,128)}), f32[4,512,512]{2,1,0:T(8,128)}) %all-reduce.2.cloned.1.call-update) | async-done | bytes 4194320 | tf_op jit(solution)/shard_map/psum | solution.py:61
  173.0 3.0 broadcast_select_fusion.1
  179.8 2.9 fusion.12
  182.7 8.2 %all_gather.25 = f32[4,512]{1,0:T(4,128)S(1)} all-gather(f32[4,128]{1,0:T(4,128)S(1)} %copy-done.4), channel_id=1, replica_groups=mesh['tm'=64,'state'=4] {'state'}, dimensions={1}, use_global_device_ids=true | all-gather | bytes 10240 | tf_op jit(solution)/shard_map/all_gather | solution.py:50
  190.9 8.3 %all_gather.24 = f32[4,512]{1,0:T(4,128)S(1)} all-gather(f32[4,128]{1,0:T(4,128)S(1)} %copy-done.5), channel_id=1, replica_groups=mesh['tm'=64,'state'=4] {'state'}, dimensions={1}, use_global_device_ids=true | all-gather | bytes 10240 | tf_op jit(solution)/shard_map/all_gather | solution.py:49
  199.2 5.8 fusion.18
  208.1 55.8 %all-gather.2 = f32[64,1,512]{2,1,0:T(1,128)S(1)} all-gather(f32[1,1,512]{2,1,0:T(1,128)S(1)} %bitcast.119), channel_id=3, replica_groups=mesh['tm'=64,'state'=4] {'tm'}, dimensions={0}, use_global_device_ids=true | all-gather | bytes 133120 | tf_op jit(solution)/shard_map/all_gather | solution.py:11
  263.9 155.7 %all-gather.8.cloned.1.call-done = f32[32768,512]{1,0:T(8,128)} async-done(((f32[512,512]{1,0:T(8,128)}), f32[32768,512]{1,0:T(8,128)}) %all-gather.8.cloned.1.call-update) | async-done | bytes 67108880 | tf_op jit(solution)/shard_map/all_gather | solution.py:11
  419.6 146.4 %while.16 = (s32[]{:T(128)}, f32[512]{0:T(512)S(1)}, s32[]{:T(128)}, f32[64,512,512]{2,1,0:T(8,128)}, f32[64,512]{1,0:T(8,128)S(1)}, /*index=5*/s32[]{:T(128)}, s32[]{:T(128)}, s32[]{:T(128)}, s32[]{:T(128)}) while((s32[]{:T(128)}, f32[512]{0:T(512)S(1)}, s32[]{:T(128)}, f32[64,512,512]{2,1,0:T(8,128)}, f32[64,512]{1,0:T(8,128)S(1)}, ...), condition=%wide.region_2.3_spmd.clone, body=%wide.region_1.2_spmd.clone.sunk | while | flops 3147784 | bytes 1069224 | solution.py:24
  421.9 2.2 fusion.49
  426.5 2.2 fusion.49
  428.8 2.2 fusion.49
  431.1 2.2 fusion.49
  435.7 2.2 fusion.49
  437.9 2.2 fusion.49
  440.2 2.2 fusion.49
  442.5 2.2 fusion.49
  444.8 2.2 fusion.49
  447.1 2.2 fusion.49
  449.4 2.2 fusion.49
  451.7 2.2 fusion.49
  454.0 2.2 fusion.49
  456.3 2.2 fusion.49
  458.5 2.2 fusion.49
  460.8 2.2 fusion.49
  463.1 2.2 fusion.49
  465.4 2.2 fusion.49
  470.0 2.2 fusion.49
  472.3 2.2 fusion.49
  474.6 2.2 fusion.49
  479.1 2.2 fusion.49
  481.4 2.2 fusion.49
  483.7 2.2 fusion.49
  486.0 2.2 fusion.49
  488.3 2.2 fusion.49
  490.6 2.2 fusion.49
  492.9 2.2 fusion.49
  495.1 2.2 fusion.49
  497.4 2.2 fusion.49
  499.7 2.2 fusion.49
  502.0 2.2 fusion.49
  504.3 2.2 fusion.49
  506.6 2.2 fusion.49
  508.9 2.2 fusion.49
  513.4 2.2 fusion.49
  515.7 2.2 fusion.49
  518.0 2.2 fusion.49
  522.6 2.2 fusion.49
  524.9 2.2 fusion.49
  527.2 2.2 fusion.49
  529.5 2.2 fusion.49
  531.8 2.2 fusion.49
  534.0 2.2 fusion.49
  536.3 2.2 fusion.49
  538.6 2.2 fusion.49
  540.9 2.2 fusion.49
  543.2 2.2 fusion.49
  545.5 2.2 fusion.49
  568.2 2.2 fusion.16
  570.5 2.2 fusion.13
  572.7 2.2 fusion.10
  (255 shorter events, 50.0 us)
Async XLA Ops:
  6.5 62.9 %copy-start = (f32[4,128,512]{2,1,0:T(8,128)S(1)}, f32[4,128,512]{2,1,0:T(8,128)}, u32[]{:S(2)}) copy-start(f32[4,128,512]{2,1,0:T(8,128)} %param.9) | copy-start | bytes 3145732
  6.5 60.1 %copy-start.3 = (f32[4,2,64,128]{3,2,1,0:T(8,128)S(1)}, f32[4,2,64,128]{3,2,1,0:T(8,128)}, u32[]{:S(2)}) copy-start(f32[4,2,64,128]{3,2,1,0:T(8,128)} %param.10) | copy-start | bytes 786436
  6.5 57.2 %all-gather.6.cloned.1.call-start = ((), (), s32[]{:S(2)}) async-start(), calls=%async_computation | async-start | bytes 5242880 | tf_op jit(solution)/shard_map/all_gather | solution.py:48
  7.3 165.7 %all-reduce.2.cloned.1.call-start = ((), (), s32[]{:S(2)}) async-start(), calls=%async_computation.1 | async-start | bytes 8388608 | tf_op jit(solution)/shard_map/psum | solution.py:61
  74.5 345.1 %all-gather.8.cloned.1.call-start = ((), (), s32[]{:S(2)}) async-start(), calls=%async_computation.2 | async-start | bytes 68157440 | tf_op jit(solution)/shard_map/all_gather | solution.py:11
  176.0 3.7 copy-start.1
  177.9 4.8 copy-start.4
  177.9 13.0 %copy-start.5 = (f32[4,128]{1,0:T(4,128)S(1)}, f32[4,128]{1,0:T(4,128)}, u32[]{:S(2)}) copy-start(f32[4,128]{1,0:T(4,128)} %param.12) | copy-start | bytes 6148
  182.7 22.3 %copy-start.2 = (f32[4,512,512]{2,1,0:T(8,128)S(1)}, f32[4,512,512]{2,1,0:T(8,128)}, u32[]{:S(2)}) copy-start(f32[4,512,512]{2,1,0:T(8,128)} %copy-done.1) | copy-start | bytes 12582916
Sparse Core Ops, SparseCore 0:
  9.2 54.5 all-gather.5
  74.6 98.2 all-reduce.1
  182.8 236.7 all-gather.7
where the time goes:
time: 585 us; the launch traced here: 582 us
  waiting for transfers between devices  310 us (53%)
  matrix products  172 us (29%)
  blocking collectives  72.3 us (12%)
  between operations  13.3 us (2%)
  other arithmetic  6.31 us (1%)
    all_gather x1, waiting for transfers between devices, carried_in(): everything = jax.tree.map(lambda part: lax.all_gather(part, axis), shard)  156 us
    dot_general x64, matrix products, combine(): jnp.dot(latter[0], earlier[1], precision=finest_accuracy) + latter[1]  141 us
    psum x1, waiting for transfers between devices, on_device(): gain_full = lax.psum(partial_value, 'state')  98.4 us
    all_gather x1, blocking collectives, carried_in(): everything = jax.tree.map(lambda part: lax.all_gather(part, axis), shard)  55.8 us
    all_gather x1, waiting for transfers between devices, on_device(): lax.all_gather(updated_spread, 'state', axis=1, tiled=True)  55.1 us
  transfers between devices with their start and end apart: 3, of which 3 were waited for; matrix products, arithmetic and copies ran while one was open for 2% of the time, Pallas kernels for 0%

commit v1 on v0

v1 whole, which is shorter than its diff:
```python
import jax
import jax.numpy as jnp
from jax import lax
from jax.experimental import pallas as pl
from jax.experimental.pallas import tpu as pltpu
from jax.sharding import PartitionSpec as P

NZ, NY, NC, NX = 8, 4, 2, 4
W = 512
B = 128
HALF = 256
PAN = HALF + 8
FULL = W + 8
AXES = ("tm", "state")
F32 = jnp.float32
VMEM_LIMIT = 56 * 1024 * 1024


def joint(move):
    pairs = []
    for z in range(NZ):
        for y in range(NY):
            for c in range(NC):
                for x in range(NX):
                    y2, c2, x2 = move(y, c, x)
                    source = ((z * NY + y) * NC + c) * NX + x
                    pairs.append((source, ((z * NY + y2) * NC + c2) * NX + x2))
    return pairs


def spread_move(p):
    def move(y, c, x):
        q = (x + p) % 4
        return y, q % 2, 2 * c + q // 2

    return move


def collect_move(r):
    def move(y, c, x):
        return y, x // 2, 2 * c + (x + r) % 2

    return move


SWAP = joint(lambda y, c, x: (y, 1 - c, x))
SPREAD = [joint(spread_move(p)) for p in range(4)]
COLLECT = [joint(collect_move(r)) for r in range(2)]
SHIFT_X = {k: joint(lambda y, c, x, k=k: (y, c, (x + k) % 4)) for k in (1, 2, 3)}
SHIFT_Y = {k: joint(lambda y, c, x, k=k: ((y + k) % 4, c, x)) for k in (1, 2, 3)}


def move(value, pairs):
    return lax.ppermute(value, AXES, pairs)


def split(a):
    high = a.astype(jnp.bfloat16)
    return high, (a - high.astype(F32)).astype(jnp.bfloat16)


def dot(a, b):
    return jnp.dot(a, b, preferred_element_type=F32)


def mm3(a, b):
    return dot(a[0], b[0]) + (dot(a[0], b[1]) + dot(a[1], b[0]))


def rows_times(row8, matrix):
    column = jnp.transpose(row8)[:, 0:1]
    product = (matrix * column).reshape(matrix.shape[0] // 8, 8, matrix.shape[1])
    total = jnp.sum(jnp.sum(product, axis=0), axis=0, keepdims=True)
    return jnp.broadcast_to(total, (8, matrix.shape[1]))


def block(i):
    return pl.ds(pl.multiple_of(i * B, B), B)


def place():
    tm = lax.axis_index("tm")
    return lax.axis_index("state"), lax.rem(tm // 2, 4), tm // 8, lax.rem(tm, 2)


def next_block(x, skip):
    one = lax.rem(x + 1, 4)
    return jnp.where(one == skip, lax.rem(x + 2, 4), one)


def pack_kernel(p_ref, r_ref, t_ref, m_ref, q_ref, pay0, pay1, pay2, pay3, local_ref, other_ref):
    x, _, _, c = place()
    for p, pay in enumerate((pay0, pay1, pay2, pay3)):
        j = lax.rem(x + p, 4)
        after = next_block(x, 2 * c + j // 2)
        for row, ref in ((0, p_ref), (B, r_ref)):
            pay[row : row + B, 0:B] = ref[j, :, block(x)]
            pay[row : row + B, B : 2 * B] = ref[j, :, block(after)]
        pay[256:320, 0:B] = t_ref[j, 0]
        pay[256:320, B : 2 * B] = t_ref[j, 1]
        pay[320:328, 0:B] = jnp.broadcast_to(m_ref[pl.ds(j, 1), :], (8, B))
        pay[320:328, B : 2 * B] = jnp.broadcast_to(q_ref[pl.ds(j, 1), :], (8, B))
    mine = 2 * lax.rem(x, 2) + c
    theirs = 2 * lax.rem(x, 2) + 1 - c
    local_ref[0:B, :] = p_ref[mine]
    local_ref[B : 2 * B, :] = r_ref[mine]
    other_ref[0:B, :] = p_ref[theirs]
    other_ref[B : 2 * B, :] = r_ref[theirs]


def step_kernel(ids_own, ids_other, pay0, pay1, pay2, pay3, local_ref, other_ref, out_ref, pf, rf, inc, vec):
    x, y, z, c = place()
    j = 2 * lax.rem(x, 2) + c
    same = (x // 2) == c
    low = lax.broadcasted_iota(jnp.int32, (64, B), 1) < 64
    for p, pay in enumerate((pay0, pay1, pay2, pay3)):
        source = lax.rem(j - p + 4, 4)
        after = next_block(source, x)
        for row, full in ((0, pf), (B, rf)):
            full[block(source), block(source)] = pay[row : row + B, 0:B]
            beside = pay[row : row + B, B : 2 * B]
            full[block(source), block(after)] = beside
            full[block(after), block(source)] = jnp.transpose(beside)
        for half in range(2):
            r = 2 * source + half
            at = j * 16 + r * 2
            first = jnp.where(same, ids_own[at], ids_other[at])
            second = jnp.where(same, ids_own[at + 1], ids_other[at + 1])
            tiles = pay[256:320, half * B : (half + 1) * B]
            turned = jnp.concatenate([tiles[:, 64:], tiles[:, :64]], axis=1)
            straight_to = jnp.where(low, first, second)
            turned_to = jnp.where(low, second, first)
            for g in range(4):
                here = jnp.where(low, 2 * g, 2 * g + 1)
                value = jnp.where(
                    straight_to == here, tiles, jnp.where(turned_to == here, turned, 0.0)
                )
                inc[pl.ds(pl.multiple_of(r * 64, 64), 64), g * B : (g + 1) * B] = value
        vec[0:8, block(source)] = pay[320:328, 0:B]
        vec[8:16, block(source)] = pay[320:328, B : 2 * B]
    for row, full in ((0, pf), (B, rf)):
        full[block(x), :] = jnp.where(
            same, local_ref[row : row + B, :], other_ref[row : row + B, :]
        )
        for d in (1, 2, 3):
            v = lax.rem(x + d, 4)
            full[block(v), block(x)] = jnp.transpose(full[block(x), block(v)])
    mixed = pf[...] + mm3(split(inc[...]), split(pf[...]))
    mixed = split(mixed)
    precision = split(rf[...])
    lead = split(mm3(split(vec[8:16, :]), precision))
    last = (z == NZ - 1) & (y == NY - 1) & (x == NX - 1) & (c == NC - 1)
    gain = mm3(precision, mixed)
    out_ref[0:W, :] = jnp.where(last, 0.0, gain)
    out_ref[W:FULL, :] = vec[0:8, :] - jnp.where(last, 0.0, mm3(lead, mixed))


def pair_kernel(own_ref, other_ref, out_ref):
    _, _, _, c = place()

    def compose(first, second):
        rows = jnp.concatenate(
            [first[pl.ds(pl.multiple_of(c * HALF, HALF), HALF), :], first[W:FULL, :]], axis=0
        )
        value = mm3(split(rows), split(second[0:W, :]))
        out_ref[0:HALF, :] = value[0:HALF]
        out_ref[HALF:PAN, :] = value[HALF:PAN] + second[W:FULL, :]

    @pl.when(c == 0)
    def _():
        compose(other_ref, own_ref)

    @pl.when(c == 1)
    def _():
        compose(own_ref, other_ref)


def fetch(panels, held, sems, index, c):
    copies = []
    for n, ref in enumerate(panels):
        k, mine = n // 2, n % 2
        half = c if mine == 0 else 1 - c
        slot = lax.rem(index - k + 4, 4)
        copy = pltpu.make_async_copy(ref, held.at[slot, half], sems.at[n])
        copy.start()
        copies.append(copy)
    return copies


def chain_kernel(along, whole, *refs):
    panels, out_ref, held, sems = refs[:8], refs[8], refs[9], refs[10]
    x, y, _, c = place()
    for copy in fetch(panels, held, sems, x if along == "x" else y, c):
        copy.wait()
    tail = held[3, 0, HALF:PAN, :]
    if whole:
        rows = jnp.concatenate([held[3, 0, 0:HALF, :], held[3, 1, 0:HALF, :], tail], axis=0)
    else:
        rows = jnp.concatenate([held[3, c, 0:HALF, :], tail], axis=0)
    size = W if whole else HALF
    for t in (2, 1, 0):
        left = split(rows)
        top = split(held[t, 0, 0:HALF, :])
        bottom = split(held[t, 1, 0:HALF, :])
        value = mm3((left[0][:, :HALF], left[1][:, :HALF]), top) + mm3(
            (left[0][:, HALF:], left[1][:, HALF:]), bottom
        )
        rows = jnp.concatenate([value[0:size], value[size:] + held[t, 0, HALF:PAN, :]], axis=0)
    out_ref[...] = rows


def plane_kernel(map_ref, carried_ref, came_ref, carried_out, out_ref):
    carried = carried_ref[...] + came_ref[...]
    carried_out[...] = carried
    out_ref[...] = rows_times(carried, map_ref[0:W, :]) + map_ref[W:FULL, :]


def down_kernel(carried_ref, came_ref, own_ref, other_ref, *refs):
    panels_y, panels_x = refs[0:8], refs[8:16]
    send0, send1, held_y, held_x, values, sems = refs[16:22]
    x, y, _, c = place()
    copies = fetch(panels_y, held_y, sems.at[0], y, c) + fetch(panels_x, held_x, sems.at[1], x, c)
    for copy in copies:
        copy.wait()
    carried = carried_ref[...] + came_ref[...]
    for held, index in ((held_y, y), (held_x, x)):
        for t in (3, 2, 1):
            matrix = jnp.concatenate([held[t, 0, 0:HALF, :], held[t, 1, 0:HALF, :]], axis=0)
            value = rows_times(carried, matrix) + held[t, 0, HALF:PAN, :]
            carried = jnp.where(t > index, value, carried)
    own_last = c == 1
    late = jnp.where(own_last, own_ref[...], other_ref[...])
    early = jnp.where(own_last, other_ref[...], own_ref[...])
    after = rows_times(carried, late[0:W]) + late[W:FULL]
    before = rows_times(after, early[0:W]) + early[W:FULL]
    top = lax.broadcasted_iota(jnp.int32, (8, W), 0) == 0
    values[...] = jnp.where(top, before, after)
    for r, send in enumerate((send0, send1)):
        send[...] = values[:, block(2 * c + lax.rem(x + r, 2))]


def shape(*dims):
    return jax.ShapeDtypeStruct(dims, F32)


PARAMS = pltpu.CompilerParams(vmem_limit_bytes=VMEM_LIMIT)
IN_VMEM = pl.BlockSpec(memory_space=pltpu.VMEM)
IN_SMEM = pl.BlockSpec(memory_space=pltpu.SMEM)
ANYWHERE = pl.BlockSpec(memory_space=pl.ANY)


def gather_panels(panel, shifts):
    panels = [panel, move(panel, SWAP)]
    for k in (1, 2, 3):
        came = move(panel, shifts[k])
        panels += [came, move(came, SWAP)]
    return panels


def chain(along, whole, panels):
    def kernel(*refs):
        chain_kernel(along, whole, *refs)

    return pl.pallas_call(
        kernel,
        out_shape=shape(FULL if whole else PAN, W),
        in_specs=[ANYWHERE] * 8,
        out_specs=IN_VMEM,
        scratch_shapes=[pltpu.VMEM((4, 2, PAN, W), F32), pltpu.SemaphoreType.DMA((8,))],
        compiler_params=PARAMS,
        name="chain_" + along,
    )(*panels)


def on_device(spread, inverse, tiles, ids, mean, prior):
    ids_own = ids.reshape(-1)
    ids_other = move(ids_own, SWAP)
    *pays, local, other = pl.pallas_call(
        pack_kernel,
        out_shape=[shape(328, HALF)] * 4 + [shape(2 * B, W)] * 2,
        in_specs=[IN_VMEM] * 5,
        out_specs=[IN_VMEM] * 6,
        compiler_params=PARAMS,
        name="pack",
    )(spread, inverse, tiles, mean, prior)
    got = [move(pay, SPREAD[p]) for p, pay in enumerate(pays)]
    other = move(other, SWAP)
    step = pl.pallas_call(
        step_kernel,
        out_shape=shape(FULL, W),
        in_specs=[IN_SMEM] * 2 + [IN_VMEM] * 6,
        out_specs=IN_VMEM,
        scratch_shapes=[pltpu.VMEM((W, W), F32)] * 3 + [pltpu.VMEM((16, W), F32)],
        compiler_params=PARAMS,
        name="step",
    )(ids_own, ids_other, *got, local, other)
    twin = move(step, SWAP)
    pair = pl.pallas_call(
        pair_kernel,
        out_shape=shape(PAN, W),
        in_specs=[IN_VMEM] * 2,
        out_specs=IN_VMEM,
        compiler_params=PARAMS,
        name="pair",
    )(step, twin)
    panels_x = gather_panels(pair, SHIFT_X)
    row_map = chain("x", False, panels_x)
    panels_y = gather_panels(row_map, SHIFT_Y)
    plane_map = chain("y", True, panels_y)
    carried = jnp.zeros((8, W), F32)
    came = jnp.zeros((8, W), F32)
    for i in range(NZ - 1):
        carried, out = pl.pallas_call(
            plane_kernel,
            out_shape=[shape(8, W)] * 2,
            in_specs=[IN_VMEM] * 3,
            out_specs=[IN_VMEM] * 2,
            compiler_params=PARAMS,
            name="plane",
        )(plane_map, carried, came)
        came = lax.ppermute(out, "tm", [(t, t - 8) for t in range(64) if t // 8 == 7 - i])
    sends = pl.pallas_call(
        down_kernel,
        out_shape=[shape(8, B)] * 2,
        in_specs=[IN_VMEM] * 4 + [ANYWHERE] * 16,
        out_specs=[IN_VMEM] * 2,
        scratch_shapes=[pltpu.VMEM((4, 2, PAN, W), F32)] * 2
        + [pltpu.VMEM((8, W), F32), pltpu.SemaphoreType.DMA((2, 8))],
        compiler_params=PARAMS,
        name="down",
    )(carried, came, step, twin, *panels_y, *panels_x)
    even, odd = (move(send, COLLECT[r])[0:2] for r, send in enumerate(sends))
    flip = lax.rem(lax.axis_index("state"), 2) == 1
    return jnp.concatenate([jnp.where(flip, odd, even), jnp.where(flip, even, odd)], axis=0)


def solution(mesh):
    return jax.shard_map(
        on_device,
        mesh=mesh,
        in_specs=(
            P("tm", "state", None),
            P("tm", "state", None),
            P("tm", "state", None, None),
            P("tm", None, None),
            P("tm", "state"),
            P("tm", "state"),
        ),
        out_specs=P("tm", "state"),
        check_vma=False,
    )
```

time: 585 us -> 190 us (0.32)
  waiting for transfers between devices: 310 us -> 92.1 us
  matrix products: 172 us -> 0 us
  blocking collectives: 72.3 us -> 0 us
  Pallas kernels: 0 us -> 45.4 us
  starting transfers between devices: 0.08 us -> 42.7 us
  between operations: 13.3 us -> 0.38 us
    all_gather x2 -> x0, waiting for transfers between devices: 211 us -> none  [the longest x1 156 us: carried_in(): everything = jax.tree.map(lambda part: lax.all_gather(part, axis), shard)]
    dot_general x77 -> x0, matrix products: 172 us -> none  [the longest x64 141 us: combine(): jnp.dot(latter[0], earlier[1], precision=finest_accuracy) + latter[1]]
    psum x1 -> x0, waiting for transfers between devices: 98.4 us -> none  [on_device(): gain_full = lax.psum(partial_value, 'state')]
    ppermute x0 -> x30, waiting for transfers between devices: none -> 92.1 us  [the longest x23 67.9 us: move(): return lax.ppermute(value, AXES, pairs)]
    all_gather x3 -> x0, blocking collectives: 72.3 us -> none  [the longest x1 55.8 us: carried_in(): everything = jax.tree.map(lambda part: lax.all_gather(part, axis), shard)]
    pallas_call x0 -> x13, Pallas kernels: none -> 45.4 us  [the longest x7 14.8 us: on_device(): pl.pallas_call(plane_kernel, out_shape=[shape(8, W)] * 2, in_specs=[IN_VM...]
    ppermute x0 -> x30, starting transfers between devices: none -> 42.7 us  [the longest x23 37.5 us: move(): return lax.ppermute(value, AXES, pairs)]
    unnamed x13 -> x61, local copies, waits for them, and re-layouts: 0.04 us -> 7.98 us
  transfers between devices with their start and end apart: 3 -> 30, of which waited for: 3 -> 14; matrix products, arithmetic and copies ran while one was open for 2% -> 0% of each run, Pallas kernels for 0% -> 0%
where the time goes in v1:
time: 190 us
  waiting for transfers between devices  92.1 us (48%)
  Pallas kernels  45.4 us (24%)
  starting transfers between devices  42.7 us (22%)
  local copies, waits for them, and re-layouts  8.69 us (5%)
    ppermute x23, waiting for transfers between devices, move(): return lax.ppermute(value, AXES, pairs)  67.9 us
    ppermute x23, starting transfers between devices, move(): return lax.ppermute(value, AXES, pairs)  37.5 us
    ppermute x7, waiting for transfers between devices, on_device(): lax.ppermute(out, 'tm', [(t, t - 8) for t in range(64) if t // 8 == 7 - i])  24.2 us
    pallas_call x7, Pallas kernels, on_device(): pl.pallas_call(plane_kernel, out_shape=[shape(8, W)] * 2, in_specs=[IN_VM...  14.8 us
    pallas_call x2, Pallas kernels, chain(): pl.pallas_call(kernel, out_shape=shape(FULL if whole else PAN, W), in_spe...  10.7 us
    pallas_call x1, Pallas kernels, on_device(): pl.pallas_call(down_kernel, out_shape=[shape(8, B)] * 2, in_specs=[IN_VME...  8.07 us
    unnamed x61, local copies, waits for them, and re-layouts  7.98 us
    pallas_call x1, Pallas kernels, on_device(): pl.pallas_call(step_kernel, out_shape=shape(FULL, W), in_specs=[IN_SMEM]...  5.54 us
  transfers between devices with their start and end apart: 30, of which 14 were waited for; matrix products, arithmetic and copies ran while one was open for 0% of the time, Pallas kernels for 0%

profile of v1, /device:TPU:1, one launch (start us, length us, event | category | flops | bytes accessed | tf_op | source)
XLA Modules:
  0.0 189.8 jit_solution(17051471495220135900)
XLA Ops:
  0.0 3.3 %pack.1 = (f32[328,256]{1,0:T(8,128)}, f32[328,256]{1,0:T(8,128)}, f32[328,256]{1,0:T(8,128)}, f32[328,256]{1,0:T(8,128)}, f32[256,512]{1,0:T(8,128)}, /*index=5*/f32[256,512]{1,0:T(8,128)}) custom-call(f32[4,128,512]{2,1,0:T(8,128)} %p_ref.1, f32[4,128,512]{2,1,0:T(8,128)} %r_ref.1, f32[4,2,64,128]{3,2,1,0:T(8,128)} %t_ref.1, f32[4,128]{1,0:T(4,128)} %m_ref.1, ...), custom_call_target="tpu_custom_call" | custom-call | tf_op jit(solution)/shard_map/pack/pallas_call | solution.py:278
  3.3 3.2 %collective-permute-start.5 = (f32[256,512]{1,0:T(8,128)}, f32[256,512]{1,0:T(8,128)S(1)}, u32[]{:S(2)}, u32[]{:S(2)}) collective-permute-start(f32[256,512]{1,0:T(8,128)} %get-tuple-element.32), channel_id=1, source_target_pairs={{0,4},{1,5},{2,6},{3,7},{4,0},{5,1},{6,2},{7,3},{8,12},{9,13},{10,... | collective-permute-start | bytes 1572872 | tf_op jit(solution)/shard_map/ppermute | solution.py:54
  6.8 3.3 %collective-permute-start.1 = (f32[328,256]{1,0:T(8,128)}, f32[328,256]{1,0:T(8,128)S(1)}, u32[]{:S(2)}, u32[]{:S(2)}) collective-permute-start(f32[328,256]{1,0:T(8,128)} %get-tuple-element.27), channel_id=1, source_target_pairs={{0,0},{1,4},{2,1},{3,5},{4,2},{5,6},{6,3},{7,7},{8,8},{9,12},{10,9... | collective-permute-start | bytes 1007624 | tf_op jit(solution)/shard_map/ppermute | solution.py:54
  10.2 2.8 %collective-permute-start.2 = (f32[328,256]{1,0:T(8,128)}, f32[328,256]{1,0:T(8,128)S(1)}, u32[]{:S(2)}, u32[]{:S(2)}) collective-permute-start(f32[328,256]{1,0:T(8,128)} %get-tuple-element.28), channel_id=1, source_target_pairs={{0,4},{1,1},{2,5},{3,0},{4,6},{5,3},{6,7},{7,2},{8,12},{9,9},{10,1... | collective-permute-start | bytes 1007624 | tf_op jit(solution)/shard_map/ppermute | solution.py:54
  13.0 0.8 collective-permute-start.3
  13.8 1.9 %collective-permute-start.4 = (f32[328,256]{1,0:T(8,128)}, f32[328,256]{1,0:T(8,128)S(1)}, u32[]{:S(2)}, u32[]{:S(2)}) collective-permute-start(f32[328,256]{1,0:T(8,128)} %get-tuple-element.30), channel_id=1, source_target_pairs={{0,5},{1,0},{2,4},{3,1},{4,7},{5,2},{6,6},{7,3},{8,13},{9,8},{10,1... | collective-permute-start | bytes 1007624 | tf_op jit(solution)/shard_map/ppermute | solution.py:54
  15.7 1.0 collective-permute-done.1.pay0
  16.8 5.9 %collective-permute-done.2.pay1 = f32[328,256]{1,0:T(8,128)S(1)} collective-permute-done((f32[328,256]{1,0:T(8,128)}, f32[328,256]{1,0:T(8,128)S(1)}, u32[]{:S(2)}, u32[]{:S(2)}) %collective-permute-start.2) | collective-permute-done | bytes 335904 | tf_op jit(solution)/shard_map/ppermute | solution.py:54
  22.7 6.9 %collective-permute-done.3.pay2 = f32[328,256]{1,0:T(8,128)S(1)} collective-permute-done((f32[328,256]{1,0:T(8,128)}, f32[328,256]{1,0:T(8,128)S(1)}, u32[]{:S(2)}, u32[]{:S(2)}) %collective-permute-start.3) | collective-permute-done | bytes 335904 | tf_op jit(solution)/shard_map/ppermute | solution.py:54
  29.6 0.7 copy-done.18
  30.6 5.5 %step.1.own_ref = f32[520,512]{1,0:T(8,128)} custom-call(s32[64]{0:T(128)} %copy-done.28, s32[64]{0:T(128)} %copy-done.29, f32[328,256]{1,0:T(8,128)} %copy-done.16, f32[328,256]{1,0:T(8,128)} %copy-done.17, f32[328,256]{1,0:T(8,128)} %copy-done.18, f32[328,256]{1,0:T(8,128)} %copy-done.19, f32[256,512]{1,0:T(8,128)} %get-tuple-element.31.local_ref, ...), custom_call_target="tpu_custom_call" | custom-call | tf_op jit(solution)/shard_map/step/pallas_call | solution.py:288
  36.1 2.9 %collective-permute-done.6.other_ref = f32[520,512]{1,0:T(8,128)S(1)} collective-permute-done((f32[520,512]{1,0:T(8,128)}, f32[520,512]{1,0:T(8,128)S(1)}, u32[]{:S(2)}, u32[]{:S(2)}) %collective-permute-start.6) | collective-permute-done | bytes 1064992 | tf_op jit(solution)/shard_map/ppermute | solution.py:54
  39.0 1.0 copy-done
  40.0 3.0 %pair.1.refs_0_.refs_8_ = f32[264,512]{1,0:T(8,128)} custom-call(f32[520,512]{1,0:T(8,128)} %step.1.own_ref, f32[520,512]{1,0:T(8,128)} %copy-done), custom_call_target="tpu_custom_call" | custom-call | tf_op jit(solution)/shard_map/pair/pallas_call | solution.py:298
  43.0 2.1 %collective-permute-start.12 = (f32[264,512]{1,0:T(8,128)}, f32[264,512]{1,0:T(8,128)S(1)}, u32[]{:S(2)}, u32[]{:S(2)}) collective-permute-start(f32[264,512]{1,0:T(8,128)} %pair.1.refs_0_.refs_8_), channel_id=1, source_target_pairs={{0,3},{1,0},{2,1},{3,2},{4,7},{5,4},{6,5},{7,6},{8,11},{9,8},{10,9... | collective-permute-start | bytes 1622024 | tf_op jit(solution)/shard_map/ppermute | solution.py:54
  45.6 0.7 collective-permute-start.7
  46.4 12.1 %collective-permute-done.10.refs_4_.refs_12_ = f32[264,512]{1,0:T(8,128)S(1)} collective-permute-done((f32[264,512]{1,0:T(8,128)}, f32[264,512]{1,0:T(8,128)S(1)}, u32[]{:S(2)}, u32[]{:S(2)}) %collective-permute-start.10) | collective-permute-done | bytes 540704 | tf_op jit(solution)/shard_map/ppermute | solution.py:54
  58.5 1.5 collective-permute-start.11
  60.0 9.8 %collective-permute-done.12.refs_6_.refs_14_ = f32[264,512]{1,0:T(8,128)S(1)} collective-permute-done((f32[264,512]{1,0:T(8,128)}, f32[264,512]{1,0:T(8,128)S(1)}, u32[]{:S(2)}, u32[]{:S(2)}) %collective-permute-start.12) | collective-permute-done | bytes 540704 | tf_op jit(solution)/shard_map/ppermute | solution.py:54
  69.8 0.9 collective-permute-start.13
  71.0 1.3 collective-permute-done.13.refs_7_.refs_15_
  72.3 0.8 collective-permute-done.9.refs_3_.refs_11_
  73.1 0.8 copy-done.7
  73.9 4.8 %chain_x.1.refs_0_ = f32[264,512]{1,0:T(8,128)} custom-call(f32[264,512]{1,0:T(8,128)} %pair.1.refs_0_.refs_8_, f32[264,512]{1,0:T(8,128)} %copy-done.4, f32[264,512]{1,0:T(8,128)} %copy-done.3, f32[264,512]{1,0:T(8,128)} %copy-done.7, f32[264,512]{1,0:T(8,128)} %copy-done.1, f32[264,512]{1,0:T(8,128)} %copy-done.5, f32[264,512]{1,0:T(8,128)} %copy-done.2, ...), custom_call_target="tpu_custom_call" | custom-call | tf_op jit(solution)/shard_map/chain_x/pallas_call | solution.py:264
  78.7 1.1 collective-permute-start.15
  79.8 2.6 %collective-permute-start.17 = (f32[264,512]{1,0:T(8,128)}, f32[264,512]{1,0:T(8,128)S(1)}, u32[]{:S(2)}, u32[]{:S(2)}) collective-permute-start(f32[264,512]{1,0:T(8,128)} %chain_x.1.refs_0_), channel_id=1, source_target_pairs={{0,16},{1,17},{2,18},{3,19},{4,20},{5,21},{6,22},{7,23},{8,24},{9,... | collective-permute-start | bytes 1622024 | tf_op jit(solution)/shard_map/ppermute | solution.py:54
  82.5 1.1 collective-permute-start.19
  83.5 1.2 collective-permute-start.14
  84.7 9.1 %collective-permute-done.15.refs_2_ = f32[264,512]{1,0:T(8,128)S(1)} collective-permute-done((f32[264,512]{1,0:T(8,128)}, f32[264,512]{1,0:T(8,128)S(1)}, u32[]{:S(2)}, u32[]{:S(2)}) %collective-permute-start.15) | collective-permute-done | bytes 540704 | tf_op jit(solution)/shard_map/ppermute | solution.py:54
  93.9 1.2 collective-permute-start.16
  95.1 11.2 %collective-permute-done.17.refs_4_ = f32[264,512]{1,0:T(8,128)S(1)} collective-permute-done((f32[264,512]{1,0:T(8,128)}, f32[264,512]{1,0:T(8,128)S(1)}, u32[]{:S(2)}, u32[]{:S(2)}) %collective-permute-start.17) | collective-permute-done | bytes 540704 | tf_op jit(solution)/shard_map/ppermute | solution.py:54
  106.3 1.2 collective-permute-start.18
  107.6 1.4 collective-permute-done.18.refs_5_
  109.1 0.8 collective-permute-done.20.refs_7_
  109.9 0.8 copy-done.14
  110.7 6.0 %chain_y.1.map_ref = f32[520,512]{1,0:T(8,128)} custom-call(f32[264,512]{1,0:T(8,128)} %chain_x.1.refs_0_, f32[264,512]{1,0:T(8,128)} %copy-done.11, f32[264,512]{1,0:T(8,128)} %copy-done.8, f32[264,512]{1,0:T(8,128)} %copy-done.12, f32[264,512]{1,0:T(8,128)} %copy-done.9, f32[264,512]{1,0:T(8,128)} %copy-done.13, f32[264,512]{1,0:T(8,128)} %copy-done.10, ...), custom_call_target="tpu_custom_call" | custom-call | tf_op jit(solution)/shard_map/chain_y/pallas_call | solution.py:264
  116.6 0.6 broadcast_1_carried_ref_came_ref.2.carried_ref.came_ref
  117.2 2.1 %plane.7 = (f32[8,512]{1,0:T(8,128)}, f32[8,512]{1,0:T(8,128)}) custom-call(f32[520,512]{1,0:T(8,128)} %chain_y.1.map_ref, f32[8,512]{1,0:T(8,128)} %broadcast_1_carried_ref_came_ref.2.carried_ref.came_ref, f32[8,512]{1,0:T(8,128)} %broadcast_1_carried_ref_came_ref.2.carried_ref.came_ref), custom_call_target="tpu_custom_call" | custom-call | tf_op jit(solution)/shard_map/plane/pallas_call | solution.py:313
  119.4 0.7 collective-permute-start.21
  120.0 0.6 copy-done.22
  120.6 2.1 %plane.8 = (f32[8,512]{1,0:T(8,128)}, f32[8,512]{1,0:T(8,128)}) custom-call(f32[520,512]{1,0:T(8,128)} %chain_y.1.map_ref, f32[8,512]{1,0:T(8,128)} %get-tuple-element.33.carried_ref, f32[8,512]{1,0:T(8,128)} %copy-done.22), custom_call_target="tpu_custom_call" | custom-call | tf_op jit(solution)/shard_map/plane/pallas_call | solution.py:313
  122.7 0.7 collective-permute-start.22
  123.4 0.6 copy-done.23
  124.0 2.1 %plane.9 = (f32[8,512]{1,0:T(8,128)}, f32[8,512]{1,0:T(8,128)}) custom-call(f32[520,512]{1,0:T(8,128)} %chain_y.1.map_ref, f32[8,512]{1,0:T(8,128)} %get-tuple-element.35.carried_ref, f32[8,512]{1,0:T(8,128)} %copy-done.23), custom_call_target="tpu_custom_call" | custom-call | tf_op jit(solution)/shard_map/plane/pallas_call | solution.py:313
  126.1 0.7 collective-permute-start.23
  126.8 0.6 copy-done.24
  127.4 2.1 %plane.10 = (f32[8,512]{1,0:T(8,128)}, f32[8,512]{1,0:T(8,128)}) custom-call(f32[520,512]{1,0:T(8,128)} %chain_y.1.map_ref, f32[8,512]{1,0:T(8,128)} %get-tuple-element.37.carried_ref, f32[8,512]{1,0:T(8,128)} %copy-done.24), custom_call_target="tpu_custom_call" | custom-call | tf_op jit(solution)/shard_map/plane/pallas_call | solution.py:313
  129.5 0.7 collective-permute-start.24
  130.2 0.6 copy-done.25
  130.8 2.1 %plane.11 = (f32[8,512]{1,0:T(8,128)}, f32[8,512]{1,0:T(8,128)}) custom-call(f32[520,512]{1,0:T(8,128)} %chain_y.1.map_ref, f32[8,512]{1,0:T(8,128)} %get-tuple-element.39.carried_ref, f32[8,512]{1,0:T(8,128)} %copy-done.25), custom_call_target="tpu_custom_call" | custom-call | tf_op jit(solution)/shard_map/plane/pallas_call | solution.py:313
  132.9 0.7 collective-permute-start.25
  133.6 0.6 copy-done.26
  134.2 2.1 %plane.12 = (f32[8,512]{1,0:T(8,128)}, f32[8,512]{1,0:T(8,128)}) custom-call(f32[520,512]{1,0:T(8,128)} %chain_y.1.map_ref, f32[8,512]{1,0:T(8,128)} %get-tuple-element.41.carried_ref, f32[8,512]{1,0:T(8,128)} %copy-done.26), custom_call_target="tpu_custom_call" | custom-call | tf_op jit(solution)/shard_map/plane/pallas_call | solution.py:313
  136.3 0.7 collective-permute-start.26
  137.0 0.6 copy-done.21
  137.6 2.1 %plane.13 = (f32[8,512]{1,0:T(8,128)}, f32[8,512]{1,0:T(8,128)}) custom-call(f32[520,512]{1,0:T(8,128)} %chain_y.1.map_ref, f32[8,512]{1,0:T(8,128)} %get-tuple-element.43.carried_ref, f32[8,512]{1,0:T(8,128)} %copy-done.21), custom_call_target="tpu_custom_call" | custom-call | tf_op jit(solution)/shard_map/plane/pallas_call | solution.py:313
  139.7 1.3 collective-permute-start.27
  141.0 24.2 %collective-permute-done.27.came_ref = f32[8,512]{1,0:T(8,128)S(1)} collective-permute-done((f32[8,512]{1,0:T(8,128)}, f32[8,512]{1,0:T(8,128)S(1)}, u32[]{:S(2)}, u32[]{:S(2)}) %collective-permute-start.27) | collective-permute-done | bytes 16416 | tf_op jit(solution)/shard_map/ppermute | solution.py:321
  165.2 0.6 copy-done.20
  165.8 8.1 %down.1 = (f32[8,128]{1,0:T(8,128)}, f32[8,128]{1,0:T(8,128)}) custom-call(f32[8,512]{1,0:T(8,128)} %get-tuple-element.45.carried_ref, f32[8,512]{1,0:T(8,128)} %copy-done.20, f32[520,512]{1,0:T(8,128)} %step.1.own_ref, f32[520,512]{1,0:T(8,128)} %copy-done, f32[264,512]{1,0:T(8,128)} %chain_x.1.refs_0_, f32[264,512]{1,0:T(8,128)} %copy-done.11, ...), custom_call_target="tpu_custom_call" | custom-call | tf_op jit(solution)/shard_map/down/pallas_call | solution.py:322
  173.8 8.8 %collective-permute-start.28 = (f32[8,128]{1,0:T(8,128)}, f32[8,128]{1,0:T(8,128)S(1)}, u32[]{:S(2)}, u32[]{:S(2)}) collective-permute-start(f32[8,128]{1,0:T(8,128)} %get-tuple-element.47), channel_id=1, source_target_pairs={{0,1},{1,0},{2,5},{3,4},{4,3},{5,2},{6,7},{7,6},{8,9},{9,8},{10,13... | collective-permute-start | bytes 12296 | tf_op jit(solution)/shard_map/ppermute | solution.py:54
  182.6 1.9 %collective-permute-start.29 = (f32[8,128]{1,0:T(8,128)}, f32[8,128]{1,0:T(8,128)S(1)}, u32[]{:S(2)}, u32[]{:S(2)}) collective-permute-start(f32[8,128]{1,0:T(8,128)} %get-tuple-element.48), channel_id=1, source_target_pairs={{0,0},{1,1},{2,4},{3,5},{4,2},{5,3},{6,6},{7,7},{8,8},{9,9},{10,12... | collective-permute-start | bytes 12296 | tf_op jit(solution)/shard_map/ppermute | solution.py:54
  184.6 4.7 %collective-permute-done.29 = f32[8,128]{1,0:T(8,128)S(1)} collective-permute-done((f32[8,128]{1,0:T(8,128)}, f32[8,128]{1,0:T(8,128)S(1)}, u32[]{:S(2)}, u32[]{:S(2)}) %collective-permute-start.29) | collective-permute-done | bytes 4128 | tf_op jit(solution)/shard_map/ppermute | solution.py:54
  189.3 0.6 pad_maximum_fusion
  (74 shorter events, 1.8 us)
Async XLA Ops:
  0.0 6.5 %copy-start.27 = (s32[4,8,2]{1,2,0:T(2,128)S(1)}, s32[4,8,2]{1,2,0:T(2,128)}, u32[]{:S(2)}) copy-start(s32[4,8,2]{1,2,0:T(2,128)} %param.9) | copy-start | bytes 772
  3.3 26.3 %collective-permute-start.5 = (f32[256,512]{1,0:T(8,128)}, f32[256,512]{1,0:T(8,128)S(1)}, u32[]{:S(2)}, u32[]{:S(2)}) collective-permute-start(f32[256,512]{1,0:T(8,128)} %get-tuple-element.32), channel_id=1, source_target_pairs={{0,4},{1,5},{2,6},{3,7},{4,0},{5,1},{6,2},{7,3},{8,12},{9,13},{10,... | collective-permute-start | bytes 1572872 | tf_op jit(solution)/shard_map/ppermute | solution.py:54
  6.7 22.8 %copy-start.28 = (s32[64]{0:T(128)}, s32[64]{0:T(128)S(1)}, u32[]{:S(2)}) copy-start(s32[64]{0:T(128)S(1)} %reshape.3.ids_own) | copy-start | bytes 772
  6.7 7.1 %collective-permute-start = (s32[64]{0:T(128)S(1)}, s32[64]{0:T(128)S(1)}, u32[]{:S(2)}, u32[]{:S(2)}) collective-permute-start(s32[64]{0:T(128)S(1)} %reshape.3.ids_own), channel_id=1, source_target_pairs={{0,4},{1,5},{2,6},{3,7},{4,0},{5,1},{6,2},{7,3},{8,12},{9,13},{10,... | collective-permute-start | bytes 776 | tf_op jit(solution)/shard_map/ppermute | solution.py:54
  6.8 9.9 %collective-permute-start.1 = (f32[328,256]{1,0:T(8,128)}, f32[328,256]{1,0:T(8,128)S(1)}, u32[]{:S(2)}, u32[]{:S(2)}) collective-permute-start(f32[328,256]{1,0:T(8,128)} %get-tuple-element.27), channel_id=1, source_target_pairs={{0,0},{1,4},{2,1},{3,5},{4,2},{5,6},{6,3},{7,7},{8,8},{9,12},{10,9... | collective-permute-start | bytes 1007624 | tf_op jit(solution)/shard_map/ppermute | solution.py:54
  10.2 12.5 %collective-permute-start.2 = (f32[328,256]{1,0:T(8,128)}, f32[328,256]{1,0:T(8,128)S(1)}, u32[]{:S(2)}, u32[]{:S(2)}) collective-permute-start(f32[328,256]{1,0:T(8,128)} %get-tuple-element.28), channel_id=1, source_target_pairs={{0,4},{1,1},{2,5},{3,0},{4,6},{5,3},{6,7},{7,2},{8,12},{9,9},{10,1... | collective-permute-start | bytes 1007624 | tf_op jit(solution)/shard_map/ppermute | solution.py:54
  13.0 16.6 %collective-permute-start.3 = (f32[328,256]{1,0:T(8,128)}, f32[328,256]{1,0:T(8,128)S(1)}, u32[]{:S(2)}, u32[]{:S(2)}) collective-permute-start(f32[328,256]{1,0:T(8,128)} %get-tuple-element.29), channel_id=1, source_target_pairs={{0,1},{1,5},{2,0},{3,4},{4,3},{5,7},{6,2},{7,6},{8,9},{9,13},{10,8... | collective-permute-start | bytes 1007624 | tf_op jit(solution)/shard_map/ppermute | solution.py:54
  13.8 15.8 %copy-start.29 = (s32[64]{0:T(128)}, s32[64]{0:T(128)S(1)}, u32[]{:S(2)}) copy-start(s32[64]{0:T(128)S(1)} %collective-permute-done.ids_other) | copy-start | bytes 772
  13.8 15.7 %collective-permute-start.4 = (f32[328,256]{1,0:T(8,128)}, f32[328,256]{1,0:T(8,128)S(1)}, u32[]{:S(2)}, u32[]{:S(2)}) collective-permute-start(f32[328,256]{1,0:T(8,128)} %get-tuple-element.30), channel_id=1, source_target_pairs={{0,5},{1,0},{2,4},{3,1},{4,7},{5,2},{6,6},{7,3},{8,13},{9,8},{10,1... | collective-permute-start | bytes 1007624 | tf_op jit(solution)/shard_map/ppermute | solution.py:54
  16.7 12.8 %copy-start.16 = (f32[328,256]{1,0:T(8,128)}, f32[328,256]{1,0:T(8,128)S(1)}, u32[]{:S(2)}) copy-start(f32[328,256]{1,0:T(8,128)S(1)} %collective-permute-done.1.pay0) | copy-start | bytes 1007620
  22.7 6.9 %copy-start.17 = (f32[328,256]{1,0:T(8,128)}, f32[328,256]{1,0:T(8,128)S(1)}, u32[]{:S(2)}) copy-start(f32[328,256]{1,0:T(8,128)S(1)} %collective-permute-done.2.pay1) | copy-start | bytes 1007620
  29.5 0.7 copy-start.18
  29.5 0.8 copy-start.19
  29.6 1.0 copy-start.15
  36.1 2.9 %collective-permute-start.6 = (f32[520,512]{1,0:T(8,128)}, f32[520,512]{1,0:T(8,128)S(1)}, u32[]{:S(2)}, u32[]{:S(2)}) collective-permute-start(f32[520,512]{1,0:T(8,128)} %step.1.own_ref), channel_id=1, source_target_pairs={{0,4},{1,5},{2,6},{3,7},{4,0},{5,1},{6,2},{7,3},{8,12},{9,13},{10,... | collective-permute-start | bytes 3194888 | tf_op jit(solution)/shard_map/ppermute | solution.py:54
  39.0 1.0 copy-start
  43.0 15.5 %collective-permute-start.10 = (f32[264,512]{1,0:T(8,128)}, f32[264,512]{1,0:T(8,128)S(1)}, u32[]{:S(2)}, u32[]{:S(2)}) collective-permute-start(f32[264,512]{1,0:T(8,128)} %pair.1.refs_0_.refs_8_), channel_id=1, source_target_pairs={{0,2},{1,3},{2,0},{3,1},{4,6},{5,7},{6,4},{7,5},{8,10},{9,11},{10,... | collective-permute-start | bytes 1622024 | tf_op jit(solution)/shard_map/ppermute | solution.py:54
  43.0 26.8 %collective-permute-start.12 = (f32[264,512]{1,0:T(8,128)}, f32[264,512]{1,0:T(8,128)S(1)}, u32[]{:S(2)}, u32[]{:S(2)}) collective-permute-start(f32[264,512]{1,0:T(8,128)} %pair.1.refs_0_.refs_8_), channel_id=1, source_target_pairs={{0,3},{1,0},{2,1},{3,2},{4,7},{5,4},{6,5},{7,6},{8,11},{9,8},{10,9... | collective-permute-start | bytes 1622024 | tf_op jit(solution)/shard_map/ppermute | solution.py:54
  45.1 25.6 %collective-permute-start.8 = (f32[264,512]{1,0:T(8,128)}, f32[264,512]{1,0:T(8,128)S(1)}, u32[]{:S(2)}, u32[]{:S(2)}) collective-permute-start(f32[264,512]{1,0:T(8,128)} %pair.1.refs_0_.refs_8_), channel_id=1, source_target_pairs={{0,1},{1,2},{2,3},{3,0},{4,5},{5,6},{6,7},{7,4},{8,9},{9,10},{10,1... | collective-permute-start | bytes 1622024 | tf_op jit(solution)/shard_map/ppermute | solution.py:54
  45.6 25.3 %collective-permute-start.7 = (f32[264,512]{1,0:T(8,128)}, f32[264,512]{1,0:T(8,128)S(1)}, u32[]{:S(2)}, u32[]{:S(2)}) collective-permute-start(f32[264,512]{1,0:T(8,128)} %pair.1.refs_0_.refs_8_), channel_id=1, source_target_pairs={{0,4},{1,5},{2,6},{3,7},{4,0},{5,1},{6,2},{7,3},{8,12},{9,13},{10,... | collective-permute-start | bytes 1622024 | tf_op jit(solution)/shard_map/ppermute | solution.py:54
  58.5 14.5 %copy-start.1 = (f32[264,512]{1,0:T(8,128)}, f32[264,512]{1,0:T(8,128)S(1)}, u32[]{:S(2)}) copy-start(f32[264,512]{1,0:T(8,128)S(1)} %collective-permute-done.10.refs_4_.refs_12_) | copy-start | bytes 1622020
  58.5 12.5 %collective-permute-start.11 = (f32[264,512]{1,0:T(8,128)S(1)}, f32[264,512]{1,0:T(8,128)S(1)}, u32[]{:S(2)}, u32[]{:S(2)}) collective-permute-start(f32[264,512]{1,0:T(8,128)S(1)} %collective-permute-done.10.refs_4_.refs_12_), channel_id=1, source_target_pairs={{0,4},{1,5},{2,6},{3,7},{4,0},{5,1},{6,2},{7,3},{8,12},{9,13},{10,... | collective-permute-start | bytes 1622024 | tf_op jit(solution)/shard_map/ppermute | solution.py:54
  69.8 3.3 %copy-start.2 = (f32[264,512]{1,0:T(8,128)}, f32[264,512]{1,0:T(8,128)S(1)}, u32[]{:S(2)}) copy-start(f32[264,512]{1,0:T(8,128)S(1)} %collective-permute-done.12.refs_6_.refs_14_) | copy-start | bytes 1622020
  69.8 2.5 %collective-permute-start.13 = (f32[264,512]{1,0:T(8,128)S(1)}, f32[264,512]{1,0:T(8,128)S(1)}, u32[]{:S(2)}, u32[]{:S(2)}) collective-permute-start(f32[264,512]{1,0:T(8,128)S(1)} %collective-permute-done.12.refs_6_.refs_14_), channel_id=1, source_target_pairs={{0,4},{1,5},{2,6},{3,7},{4,0},{5,1},{6,2},{7,3},{8,12},{9,13},{10,... | collective-permute-start | bytes 1622024 | tf_op jit(solution)/shard_map/ppermute | solution.py:54
  70.7 2.3 %copy-start.3 = (f32[264,512]{1,0:T(8,128)}, f32[264,512]{1,0:T(8,128)S(1)}, u32[]{:S(2)}) copy-start(f32[264,512]{1,0:T(8,128)S(1)} %collective-permute-done.8.refs_2_.refs_10_) | copy-start | bytes 1622020
  70.7 2.3 %collective-permute-start.9 = (f32[264,512]{1,0:T(8,128)S(1)}, f32[264,512]{1,0:T(8,128)S(1)}, u32[]{:S(2)}, u32[]{:S(2)}) collective-permute-start(f32[264,512]{1,0:T(8,128)S(1)} %collective-permute-done.8.refs_2_.refs_10_), channel_id=1, source_target_pairs={{0,4},{1,5},{2,6},{3,7},{4,0},{5,1},{6,2},{7,3},{8,12},{9,13},{10,... | collective-permute-start | bytes 1622024 | tf_op jit(solution)/shard_map/ppermute | solution.py:54
  71.0 2.1 %copy-start.4 = (f32[264,512]{1,0:T(8,128)}, f32[264,512]{1,0:T(8,128)S(1)}, u32[]{:S(2)}) copy-start(f32[264,512]{1,0:T(8,128)S(1)} %collective-permute-done.7.refs_1_.refs_9_) | copy-start | bytes 1622020
  71.0 2.1 %copy-start.5 = (f32[264,512]{1,0:T(8,128)}, f32[264,512]{1,0:T(8,128)S(1)}, u32[]{:S(2)}) copy-start(f32[264,512]{1,0:T(8,128)S(1)} %collective-permute-done.11.refs_5_.refs_13_) | copy-start | bytes 1622020
  72.3 0.9 copy-start.6
  73.1 0.8 copy-start.7
  78.7 15.2 %collective-permute-start.15 = (f32[264,512]{1,0:T(8,128)}, f32[264,512]{1,0:T(8,128)S(1)}, u32[]{:S(2)}, u32[]{:S(2)}) collective-permute-start(f32[264,512]{1,0:T(8,128)} %chain_x.1.refs_0_), channel_id=1, source_target_pairs={{0,8},{1,9},{2,10},{3,11},{4,12},{5,13},{6,14},{7,15},{8,16},{9,17... | collective-permute-start | bytes 1622024 | tf_op jit(solution)/shard_map/ppermute | solution.py:54
  79.8 26.4 %collective-permute-start.17 = (f32[264,512]{1,0:T(8,128)}, f32[264,512]{1,0:T(8,128)S(1)}, u32[]{:S(2)}, u32[]{:S(2)}) collective-permute-start(f32[264,512]{1,0:T(8,128)} %chain_x.1.refs_0_), channel_id=1, source_target_pairs={{0,16},{1,17},{2,18},{3,19},{4,20},{5,21},{6,22},{7,23},{8,24},{9,... | collective-permute-start | bytes 1622024 | tf_op jit(solution)/shard_map/ppermute | solution.py:54
  82.5 25.0 %collective-permute-start.19 = (f32[264,512]{1,0:T(8,128)}, f32[264,512]{1,0:T(8,128)S(1)}, u32[]{:S(2)}, u32[]{:S(2)}) collective-permute-start(f32[264,512]{1,0:T(8,128)} %chain_x.1.refs_0_), channel_id=1, source_target_pairs={{0,24},{1,25},{2,26},{3,27},{4,28},{5,29},{6,30},{7,31},{8,0},{9,1... | collective-permute-start | bytes 1622024 | tf_op jit(solution)/shard_map/ppermute | solution.py:54
  83.5 24.1 %collective-permute-start.14 = (f32[264,512]{1,0:T(8,128)}, f32[264,512]{1,0:T(8,128)S(1)}, u32[]{:S(2)}, u32[]{:S(2)}) collective-permute-start(f32[264,512]{1,0:T(8,128)} %chain_x.1.refs_0_), channel_id=1, source_target_pairs={{0,4},{1,5},{2,6},{3,7},{4,0},{5,1},{6,2},{7,3},{8,12},{9,13},{10,... | collective-permute-start | bytes 1622024 | tf_op jit(solution)/shard_map/ppermute | solution.py:54
  93.9 16.0 %copy-start.8 = (f32[264,512]{1,0:T(8,128)}, f32[264,512]{1,0:T(8,128)S(1)}, u32[]{:S(2)}) copy-start(f32[264,512]{1,0:T(8,128)S(1)} %collective-permute-done.15.refs_2_) | copy-start | bytes 1622020
  93.9 13.7 %collective-permute-start.16 = (f32[264,512]{1,0:T(8,128)S(1)}, f32[264,512]{1,0:T(8,128)S(1)}, u32[]{:S(2)}, u32[]{:S(2)}) collective-permute-start(f32[264,512]{1,0:T(8,128)S(1)} %collective-permute-done.15.refs_2_), channel_id=1, source_target_pairs={{0,4},{1,5},{2,6},{3,7},{4,0},{5,1},{6,2},{7,3},{8,12},{9,13},{10,... | collective-permute-start | bytes 1622024 | tf_op jit(solution)/shard_map/ppermute | solution.py:54
  106.3 3.5 %copy-start.9 = (f32[264,512]{1,0:T(8,128)}, f32[264,512]{1,0:T(8,128)S(1)}, u32[]{:S(2)}) copy-start(f32[264,512]{1,0:T(8,128)S(1)} %collective-permute-done.17.refs_4_) | copy-start | bytes 1622020
  106.3 2.8 %collective-permute-start.18 = (f32[264,512]{1,0:T(8,128)S(1)}, f32[264,512]{1,0:T(8,128)S(1)}, u32[]{:S(2)}, u32[]{:S(2)}) collective-permute-start(f32[264,512]{1,0:T(8,128)S(1)} %collective-permute-done.17.refs_4_), channel_id=1, source_target_pairs={{0,4},{1,5},{2,6},{3,7},{4,0},{5,1},{6,2},{7,3},{8,12},{9,13},{10,... | collective-permute-start | bytes 1622024 | tf_op jit(solution)/shard_map/ppermute | solution.py:54
  107.5 2.3 %copy-start.10 = (f32[264,512]{1,0:T(8,128)}, f32[264,512]{1,0:T(8,128)S(1)}, u32[]{:S(2)}) copy-start(f32[264,512]{1,0:T(8,128)S(1)} %collective-permute-done.19.refs_6_) | copy-start | bytes 1622020
  107.5 2.3 %collective-permute-start.20 = (f32[264,512]{1,0:T(8,128)S(1)}, f32[264,512]{1,0:T(8,128)S(1)}, u32[]{:S(2)}, u32[]{:S(2)}) collective-permute-start(f32[264,512]{1,0:T(8,128)S(1)} %collective-permute-done.19.refs_6_), channel_id=1, source_target_pairs={{0,4},{1,5},{2,6},{3,7},{4,0},{5,1},{6,2},{7,3},{8,12},{9,13},{10,... | collective-permute-start | bytes 1622024 | tf_op jit(solution)/shard_map/ppermute | solution.py:54
  107.6 2.2 %copy-start.11 = (f32[264,512]{1,0:T(8,128)}, f32[264,512]{1,0:T(8,128)S(1)}, u32[]{:S(2)}) copy-start(f32[264,512]{1,0:T(8,128)S(1)} %collective-permute-done.14.refs_1_) | copy-start | bytes 1622020
  107.6 2.2 %copy-start.12 = (f32[264,512]{1,0:T(8,128)}, f32[264,512]{1,0:T(8,128)S(1)}, u32[]{:S(2)}) copy-start(f32[264,512]{1,0:T(8,128)S(1)} %collective-permute-done.16.refs_3_) | copy-start | bytes 1622020
  109.1 0.8 copy-start.13
  109.9 0.8 copy-start.14
  119.4 0.7 collective-permute-start.21
  120.0 0.6 copy-start.22
  122.7 0.7 collective-permute-start.22
  123.4 0.6 copy-start.23
  126.1 0.7 collective-permute-start.23
  126.8 0.6 copy-start.24
  129.5 0.7 collective-permute-start.24
  130.2 0.6 copy-start.25
  132.9 0.7 collective-permute-start.25
  133.6 0.6 copy-start.26
  136.3 0.7 collective-permute-start.26
  137.0 0.6 copy-start.21
  139.7 25.5 %collective-permute-start.27 = (f32[8,512]{1,0:T(8,128)}, f32[8,512]{1,0:T(8,128)S(1)}, u32[]{:S(2)}, u32[]{:S(2)}) collective-permute-start(f32[8,512]{1,0:T(8,128)} %get-tuple-element.46), channel_id=1, source_target_pairs={{32,0},{36,4},{40,8},{44,12},{48,16},{52,20},{56,24},{60,28},{33,1... | collective-permute-start | bytes 49160 | tf_op jit(solution)/shard_map/ppermute | solution.py:321
  165.2 0.6 copy-start.20
  173.8 10.7 %collective-permute-start.28 = (f32[8,128]{1,0:T(8,128)}, f32[8,128]{1,0:T(8,128)S(1)}, u32[]{:S(2)}, u32[]{:S(2)}) collective-permute-start(f32[8,128]{1,0:T(8,128)} %get-tuple-element.47), channel_id=1, source_target_pairs={{0,1},{1,0},{2,5},{3,4},{4,3},{5,2},{6,7},{7,6},{8,9},{9,8},{10,13... | collective-permute-start | bytes 12296 | tf_op jit(solution)/shard_map/ppermute | solution.py:54
  182.6 6.6 %collective-permute-start.29 = (f32[8,128]{1,0:T(8,128)}, f32[8,128]{1,0:T(8,128)S(1)}, u32[]{:S(2)}, u32[]{:S(2)}) collective-permute-start(f32[8,128]{1,0:T(8,128)} %get-tuple-element.48), channel_id=1, source_target_pairs={{0,0},{1,1},{2,4},{3,5},{4,2},{5,3},{6,6},{7,7},{8,8},{9,9},{10,12... | collective-permute-start | bytes 12296 | tf_op jit(solution)/shard_map/ppermute | solution.py:54

commit v2 on v1

--- a/solution.py
+++ b/solution.py
@@ -10,10 +10,11 @@
 B = 128
 HALF = 256
 PAN = HALF + 8
+LOW = B + 8
 FULL = W + 8
 AXES = ("tm", "state")
 F32 = jnp.float32
-VMEM_LIMIT = 56 * 1024 * 1024
+VMEM_LIMIT = 24 * 1024 * 1024
 
 
 def joint(move):
@@ -88,24 +89,38 @@
     return jnp.where(one == skip, lax.rem(x + 2, 4), one)
 
 
-def pack_kernel(p_ref, r_ref, t_ref, m_ref, q_ref, pay0, pay1, pay2, pay3, local_ref, other_ref):
+def pack_kernel(p_ref, r_ref, t_ref, m_ref, q_ref, pay0, pay1, pay2, pay3, local_ref, other_ref, means, sems):
     x, _, _, c = place()
+    copies = []
+
+    def start(source, target):
+        copy = pltpu.make_async_copy(source, target, sems.at[len(copies)])
+        copy.start()
+        copies.append(copy)
+
+    start(m_ref, means.at[0])
+    start(q_ref, means.at[1])
     for p, pay in enumerate((pay0, pay1, pay2, pay3)):
         j = lax.rem(x + p, 4)
         after = next_block(x, 2 * c + j // 2)
         for row, ref in ((0, p_ref), (B, r_ref)):
-            pay[row : row + B, 0:B] = ref[j, :, block(x)]
-            pay[row : row + B, B : 2 * B] = ref[j, :, block(after)]
-        pay[256:320, 0:B] = t_ref[j, 0]
-        pay[256:320, B : 2 * B] = t_ref[j, 1]
-        pay[320:328, 0:B] = jnp.broadcast_to(m_ref[pl.ds(j, 1), :], (8, B))
-        pay[320:328, B : 2 * B] = jnp.broadcast_to(q_ref[pl.ds(j, 1), :], (8, B))
+            start(ref.at[j, :, block(x)], pay.at[row : row + B, 0:B])
+            start(ref.at[j, :, block(after)], pay.at[row : row + B, B : 2 * B])
+        start(t_ref.at[j, 0], pay.at[256:320, 0:B])
+        start(t_ref.at[j, 1], pay.at[256:320, B : 2 * B])
     mine = 2 * lax.rem(x, 2) + c
     theirs = 2 * lax.rem(x, 2) + 1 - c
-    local_ref[0:B, :] = p_ref[mine]
-    local_ref[B : 2 * B, :] = r_ref[mine]
-    other_ref[0:B, :] = p_ref[theirs]
-    other_ref[B : 2 * B, :] = r_ref[theirs]
+    for row, ref in ((0, p_ref), (B, r_ref)):
+        start(ref.at[mine], local_ref.at[row : row + B])
+        start(ref.at[theirs], other_ref.at[row : row + B])
+    copies[0].wait()
+    copies[1].wait()
+    for p, pay in enumerate((pay0, pay1, pay2, pay3)):
+        j = lax.rem(x + p, 4)
+        pay[320:328, 0:B] = jnp.broadcast_to(means[0, pl.ds(j, 1), :], (8, B))
+        pay[320:328, B : 2 * B] = jnp.broadcast_to(means[1, pl.ds(j, 1), :], (8, B))
+    for copy in copies[2:]:
+        copy.wait()
 
 
 def step_kernel(ids_own, ids_other, pay0, pay1, pay2, pay3, local_ref, other_ref, out_ref, pf, rf, inc, vec):
@@ -155,7 +170,7 @@
     out_ref[W:FULL, :] = vec[0:8, :] - jnp.where(last, 0.0, mm3(lead, mixed))
 
 
-def pair_kernel(own_ref, other_ref, out_ref):
+def pair_kernel(own_ref, other_ref, top_ref, low_ref):
     _, _, _, c = place()
 
     def compose(first, second):
@@ -163,8 +178,9 @@
             [first[pl.ds(pl.multiple_of(c * HALF, HALF), HALF), :], first[W:FULL, :]], axis=0
         )
         value = mm3(split(rows), split(second[0:W, :]))
-        out_ref[0:HALF, :] = value[0:HALF]
-        out_ref[HALF:PAN, :] = value[HALF:PAN] + second[W:FULL, :]
+        top_ref[...] = value[0:B]
+        low_ref[0:B, :] = value[B:HALF]
+        low_ref[B:LOW, :] = value[HALF:PAN] + second[W:FULL, :]
 
     @pl.when(c == 0)
     def _():
@@ -178,17 +194,18 @@
 def fetch(panels, held, sems, index, c):
     copies = []
     for n, ref in enumerate(panels):
-        k, mine = n // 2, n % 2
+        k, mine, low = n // 4, n // 2 % 2, n % 2
         half = c if mine == 0 else 1 - c
         slot = lax.rem(index - k + 4, 4)
-        copy = pltpu.make_async_copy(ref, held.at[slot, half], sems.at[n])
+        rows = pl.ds(B, LOW) if low else pl.ds(0, B)
+        copy = pltpu.make_async_copy(ref, held.at[slot, half, rows], sems.at[n])
         copy.start()
         copies.append(copy)
     return copies
 
 
 def chain_kernel(along, whole, *refs):
-    panels, out_ref, held, sems = refs[:8], refs[8], refs[9], refs[10]
+    panels, outs, held, sems = refs[:16], refs[16:-2], refs[-2], refs[-1]
     x, y, _, c = place()
     for copy in fetch(panels, held, sems, x if along == "x" else y, c):
         copy.wait()
@@ -206,7 +223,11 @@
             (left[0][:, HALF:], left[1][:, HALF:]), bottom
         )
         rows = jnp.concatenate([value[0:size], value[size:] + held[t, 0, HALF:PAN, :]], axis=0)
-    out_ref[...] = rows
+    if whole:
+        outs[0][...] = rows
+    else:
+        outs[0][...] = rows[0:B]
+        outs[1][...] = rows[B:]
 
 
 def plane_kernel(map_ref, carried_ref, came_ref, carried_out, out_ref):
@@ -216,8 +237,8 @@
 
 
 def down_kernel(carried_ref, came_ref, own_ref, other_ref, *refs):
-    panels_y, panels_x = refs[0:8], refs[8:16]
-    send0, send1, held_y, held_x, values, sems = refs[16:22]
+    panels_y, panels_x = refs[0:16], refs[16:32]
+    send0, send1, held_y, held_x, values, sems = refs[32:38]
     x, y, _, c = place()
     copies = fetch(panels_y, held_y, sems.at[0], y, c) + fetch(panels_x, held_x, sems.at[1], x, c)
     for copy in copies:
@@ -246,14 +267,22 @@
 PARAMS = pltpu.CompilerParams(vmem_limit_bytes=VMEM_LIMIT)
 IN_VMEM = pl.BlockSpec(memory_space=pltpu.VMEM)
 IN_SMEM = pl.BlockSpec(memory_space=pltpu.SMEM)
+IN_HBM = pl.BlockSpec(memory_space=pltpu.HBM)
 ANYWHERE = pl.BlockSpec(memory_space=pl.ANY)
 
 
-def gather_panels(panel, shifts):
-    panels = [panel, move(panel, SWAP)]
-    for k in (1, 2, 3):
-        came = move(panel, shifts[k])
-        panels += [came, move(came, SWAP)]
+def both(value):
+    return [value, move(value, SWAP)]
+
+
+def gather_panels(top, low, shifts):
+    left_top, right_low = move(top, shifts[1]), move(low, shifts[3])
+    left_low, right_top = move(low, shifts[1]), move(top, shifts[3])
+    far_top, far_low = move(left_top, shifts[1]), move(right_low, shifts[3])
+    panels = []
+    for pair in ((top, low), (left_top, left_low), (far_top, far_low), (right_top, right_low)):
+        own, other = zip(*(both(value) for value in pair))
+        panels += [*own, *other]
     return panels
 
 
@@ -263,13 +292,17 @@
 
     return pl.pallas_call(
         kernel,
-        out_shape=shape(FULL if whole else PAN, W),
-        in_specs=[ANYWHERE] * 8,
-        out_specs=IN_VMEM,
-        scratch_shapes=[pltpu.VMEM((4, 2, PAN, W), F32), pltpu.SemaphoreType.DMA((8,))],
+        out_shape=shape(FULL, W) if whole else [shape(B, W), shape(LOW, W)],
+        in_specs=[ANYWHERE] * 16,
+        out_specs=IN_VMEM if whole else [IN_VMEM] * 2,
+        scratch_shapes=[pltpu.VMEM((4, 2, PAN, W), F32), pltpu.SemaphoreType.DMA((16,))],
         compiler_params=PARAMS,
         name="chain_" + along,
     )(*panels)
+
+
+def in_hbm(value):
+    return pltpu.with_memory_space_constraint(value, pltpu.HBM)
 
 
 def on_device(spread, inverse, tiles, ids, mean, prior):
@@ -278,11 +311,12 @@
     *pays, local, other = pl.pallas_call(
         pack_kernel,
         out_shape=[shape(328, HALF)] * 4 + [shape(2 * B, W)] * 2,
-        in_specs=[IN_VMEM] * 5,
+        in_specs=[IN_HBM] * 5,
         out_specs=[IN_VMEM] * 6,
+        scratch_shapes=[pltpu.VMEM((2, 4, B), F32), pltpu.SemaphoreType.DMA((30,))],
         compiler_params=PARAMS,
         name="pack",
-    )(spread, inverse, tiles, mean, prior)
+    )(*(in_hbm(a) for a in (spread, inverse, tiles, mean, prior)))
     got = [move(pay, SPREAD[p]) for p, pay in enumerate(pays)]
     other = move(other, SWAP)
     step = pl.pallas_call(
@@ -297,15 +331,15 @@
     twin = move(step, SWAP)
     pair = pl.pallas_call(
         pair_kernel,
-        out_shape=shape(PAN, W),
+        out_shape=[shape(B, W), shape(LOW, W)],
         in_specs=[IN_VMEM] * 2,
-        out_specs=IN_VMEM,
+        out_specs=[IN_VMEM] * 2,
         compiler_params=PARAMS,
         name="pair",
     )(step, twin)
-    panels_x = gather_panels(pair, SHIFT_X)
+    panels_x = gather_panels(*pair, SHIFT_X)
     row_map = chain("x", False, panels_x)
-    panels_y = gather_panels(row_map, SHIFT_Y)
+    panels_y = gather_panels(*row_map, SHIFT_Y)
     plane_map = chain("y", True, panels_y)
     carried = jnp.zeros((8, W), F32)
     came = jnp.zeros((8, W), F32)
@@ -322,10 +356,10 @@
     sends = pl.pallas_call(
         down_kernel,
         out_shape=[shape(8, B)] * 2,
-        in_specs=[IN_VMEM] * 4 + [ANYWHERE] * 16,
+        in_specs=[IN_VMEM] * 4 + [ANYWHERE] * 32,
         out_specs=[IN_VMEM] * 2,
         scratch_shapes=[pltpu.VMEM((4, 2, PAN, W), F32)] * 2
-        + [pltpu.VMEM((8, W), F32), pltpu.SemaphoreType.DMA((2, 8))],
+        + [pltpu.VMEM((8, W), F32), pltpu.SemaphoreType.DMA((2, 16))],
         compiler_params=PARAMS,
         name="down",
     )(carried, came, step, twin, *panels_y, *panels_x)

time: 190 us -> 142 us (0.75)
  Pallas kernels: 45.4 us -> 17.3 us
  waiting for transfers between devices: 92.1 us -> 65.3 us
  starting transfers between devices: 42.7 us -> 57.7 us
  local copies, waits for them, and re-layouts: 8.69 us -> 0.21 us
    ppermute x23 -> x37, waiting for transfers between devices: 67.9 us -> 42.5 us  [move(): return lax.ppermute(value, AXES, pairs)]
    ppermute x23 -> x37, starting transfers between devices: 37.5 us -> 52.4 us  [move(): return lax.ppermute(value, AXES, pairs)]
    pallas_call x7, Pallas kernels: 14.8 us -> 1.86 us  [on_device(): pl.pallas_call(plane_kernel, out_shape=[shape(8, W)] * 2, in_specs=[IN_VM...]
    unnamed x61 -> x3, local copies, waits for them, and re-layouts: 7.98 us -> 0.1 us
    pallas_call x3, Pallas kernels: 13.7 us -> 6.32 us  [the longest x2 5.69 us: chain(): pl.pallas_call(kernel, out_shape=shape(FULL, W) if whole else [shape(B, W...]
    pallas_call x1, Pallas kernels: 8.07 us -> 3.66 us  [on_device(): pl.pallas_call(down_kernel, out_shape=[shape(8, B)] * 2, in_specs=[IN_VME...]
    pallas_call x1, Pallas kernels: 5.54 us -> 3.43 us  [on_device(): pl.pallas_call(step_kernel, out_shape=shape(FULL, W), in_specs=[IN_SMEM]...]
  transfers between devices with their start and end apart: 30 -> 44, of which waited for: 14 -> 19; matrix products, arithmetic and copies ran while one was open for 0% -> 0% of each run, Pallas kernels for 0% -> 0%
where the time goes in v2:
time: 142 us; the launch traced here: 141 us
  waiting for transfers between devices  65.3 us (46%)
  starting transfers between devices  57.7 us (41%)
  Pallas kernels  17.3 us (12%)
    ppermute x37, starting transfers between devices, move(): return lax.ppermute(value, AXES, pairs)  52.4 us
    ppermute x37, waiting for transfers between devices, move(): return lax.ppermute(value, AXES, pairs)  42.5 us
    ppermute x7, waiting for transfers between devices, on_device(): lax.ppermute(out, 'tm', [(t, t - 8) for t in range(64) if t // 8 == 7 - i])  22.8 us
    pallas_call x2, Pallas kernels, chain(): pl.pallas_call(kernel, out_shape=shape(FULL, W) if whole else [shape(B, W...  5.69 us
    ppermute x7, starting transfers between devices, on_device(): lax.ppermute(out, 'tm', [(t, t - 8) for t in range(64) if t // 8 == 7 - i])  5.26 us
    pallas_call x1, Pallas kernels, on_device(): pl.pallas_call(down_kernel, out_shape=[shape(8, B)] * 2, in_specs=[IN_VME...  3.66 us
    pallas_call x1, Pallas kernels, on_device(): pl.pallas_call(step_kernel, out_shape=shape(FULL, W), in_specs=[IN_SMEM]...  3.43 us
  transfers between devices with their start and end apart: 44, of which 19 were waited for; matrix products, arithmetic and copies ran while one was open for 0% of the time, Pallas kernels for 0%

profile of v2, /device:TPU:1, one launch (start us, length us, event | category | flops | bytes accessed | tf_op | source)
XLA Modules:
  0.0 141.4 jit_solution(15712406554538098997)
XLA Ops:
  0.0 2.0 %pack.1 = (f32[328,256]{1,0:T(8,128)S(1)}, f32[328,256]{1,0:T(8,128)S(1)}, f32[328,256]{1,0:T(8,128)S(1)}, f32[328,256]{1,0:T(8,128)S(1)}, f32[256,512]{1,0:T(8,128)S(1)}, /*index=5*/f32[256,512]{1,0:T(8,128)S(1)}) custom-call(f32[4,128,512]{2,1,0:T(8,128)} %p_ref.1, f32[4,128,512]{2,1,0:T(8,128)} %r_ref.1, f32[4,2,64,128]{3,2,1,0:T(8,128)} %t_ref.1, ...), custom_call_target="tpu_custom_call" | custom-call | tf_op jit(solution)/shard_map/pack/pallas_call | solution.py:311
  2.0 3.3 %collective-permute-start.5 = (f32[256,512]{1,0:T(8,128)S(1)}, f32[256,512]{1,0:T(8,128)S(1)}, u32[]{:S(2)}, u32[]{:S(2)}) collective-permute-start(f32[256,512]{1,0:T(8,128)S(1)} %get-tuple-element.36), channel_id=1, source_target_pairs={{0,4},{1,5},{2,6},{3,7},{4,0},{5,1},{6,2},{7,3},{8,12},{9,13},{10,... | collective-permute-start | bytes 1572872 | tf_op jit(solution)/shard_map/ppermute | solution.py:55
  5.7 3.3 %collective-permute-start.1 = (f32[328,256]{1,0:T(8,128)S(1)}, f32[328,256]{1,0:T(8,128)S(1)}, u32[]{:S(2)}, u32[]{:S(2)}) collective-permute-start(f32[328,256]{1,0:T(8,128)S(1)} %get-tuple-element.31), channel_id=1, source_target_pairs={{0,0},{1,4},{2,1},{3,5},{4,2},{5,6},{6,3},{7,7},{8,8},{9,12},{10,9... | collective-permute-start | bytes 1007624 | tf_op jit(solution)/shard_map/ppermute | solution.py:55
  9.0 2.8 %collective-permute-start.2 = (f32[328,256]{1,0:T(8,128)S(1)}, f32[328,256]{1,0:T(8,128)S(1)}, u32[]{:S(2)}, u32[]{:S(2)}) collective-permute-start(f32[328,256]{1,0:T(8,128)S(1)} %get-tuple-element.32), channel_id=1, source_target_pairs={{0,4},{1,1},{2,5},{3,0},{4,6},{5,3},{6,7},{7,2},{8,12},{9,9},{10,1... | collective-permute-start | bytes 1007624 | tf_op jit(solution)/shard_map/ppermute | solution.py:55
  11.9 2.2 %collective-permute-start.4 = (f32[328,256]{1,0:T(8,128)S(1)}, f32[328,256]{1,0:T(8,128)S(1)}, u32[]{:S(2)}, u32[]{:S(2)}) collective-permute-start(f32[328,256]{1,0:T(8,128)S(1)} %get-tuple-element.34), channel_id=1, source_target_pairs={{0,5},{1,0},{2,4},{3,1},{4,7},{5,2},{6,6},{7,3},{8,13},{9,8},{10,1... | collective-permute-start | bytes 1007624 | tf_op jit(solution)/shard_map/ppermute | solution.py:55
  14.1 1.3 collective-permute-done.1.pay0
  15.4 5.8 %collective-permute-done.2.pay1 = f32[328,256]{1,0:T(8,128)S(1)} collective-permute-done((f32[328,256]{1,0:T(8,128)S(1)}, f32[328,256]{1,0:T(8,128)S(1)}, u32[]{:S(2)}, u32[]{:S(2)}) %collective-permute-start.2) | collective-permute-done | bytes 335904 | tf_op jit(solution)/shard_map/ppermute | solution.py:55
  21.1 6.1 %collective-permute-done.3.pay2 = f32[328,256]{1,0:T(8,128)S(1)} collective-permute-done((f32[328,256]{1,0:T(8,128)S(1)}, f32[328,256]{1,0:T(8,128)S(1)}, u32[]{:S(2)}, u32[]{:S(2)}) %collective-permute-start.3) | collective-permute-done | bytes 335904 | tf_op jit(solution)/shard_map/ppermute | solution.py:55
  27.3 3.4 %step.1.own_ref = f32[520,512]{1,0:T(8,128)S(1)} custom-call(s32[64]{0:T(128)S(1)} %reshape.3.ids_own, s32[64]{0:T(128)S(1)} %collective-permute-done.ids_other, f32[328,256]{1,0:T(8,128)S(1)} %collective-permute-done.1.pay0, f32[328,256]{1,0:T(8,128)S(1)} %collective-permute-done.2.pay1, f32[328,256]{1,0:T(8,128)S(1)} %collective-permute-done.3.pay2, ...), custom_call_target="tpu_custom_call" | custom-call | tf_op jit(solution)/shard_map/step/pallas_call | solution.py:322
  30.7 2.7 %collective-permute-done.6.other_ref = f32[520,512]{1,0:T(8,128)S(1)} collective-permute-done((f32[520,512]{1,0:T(8,128)S(1)}, f32[520,512]{1,0:T(8,128)S(1)}, u32[]{:S(2)}, u32[]{:S(2)}) %collective-permute-start.6) | collective-permute-done | bytes 1064992 | tf_op jit(solution)/shard_map/ppermute | solution.py:55
  33.4 0.6 pair.1
  34.0 2.7 %collective-permute-start.14 = (f32[136,512]{1,0:T(8,128)S(1)}, f32[136,512]{1,0:T(8,128)S(1)}, u32[]{:S(2)}, u32[]{:S(2)}) collective-permute-start(f32[136,512]{1,0:T(8,128)S(1)} %get-tuple-element.38.refs_1_.refs_17_), channel_id=1, source_target_pairs={{0,3},{1,0},{2,1},{3,2},{4,7},{5,4},{6,5},{7,6},{8,11},{9,8},{10,9... | collective-permute-start | bytes 835592 | tf_op jit(solution)/shard_map/ppermute | solution.py:55
  36.7 2.7 %collective-permute-start.18 = (f32[128,512]{1,0:T(8,128)S(1)}, f32[128,512]{1,0:T(8,128)S(1)}, u32[]{:S(2)}, u32[]{:S(2)}) collective-permute-start(f32[128,512]{1,0:T(8,128)S(1)} %get-tuple-element.37.refs_0_.refs_16_), channel_id=1, source_target_pairs={{0,3},{1,0},{2,1},{3,2},{4,7},{5,4},{6,5},{7,6},{8,11},{9,8},{10,9... | collective-permute-start | bytes 786440 | tf_op jit(solution)/shard_map/ppermute | solution.py:55
  39.4 1.0 collective-permute-start.7
  40.4 5.0 %collective-permute-done.9.refs_4_.refs_20_ = f32[128,512]{1,0:T(8,128)S(1)} collective-permute-done((f32[128,512]{1,0:T(8,128)S(1)}, f32[128,512]{1,0:T(8,128)S(1)}, u32[]{:S(2)}, u32[]{:S(2)}) %collective-permute-start.9) | collective-permute-done | bytes 262176 | tf_op jit(solution)/shard_map/ppermute | solution.py:55
  45.4 2.2 %collective-permute-start.8 = (f32[136,512]{1,0:T(8,128)S(1)}, f32[136,512]{1,0:T(8,128)S(1)}, u32[]{:S(2)}, u32[]{:S(2)}) collective-permute-start(f32[136,512]{1,0:T(8,128)S(1)} %get-tuple-element.38.refs_1_.refs_17_), channel_id=1, source_target_pairs={{0,4},{1,5},{2,6},{3,7},{4,0},{5,1},{6,2},{7,3},{8,12},{9,13},{10,... | collective-permute-start | bytes 835592 | tf_op jit(solution)/shard_map/ppermute | solution.py:55
  47.6 0.7 collective-permute-done.18.refs_12_.refs_28_
  48.3 0.8 collective-permute-start.13
  49.0 0.8 collective-permute-start.11
  49.8 1.6 %collective-permute-done.10.refs_5_.refs_21_ = f32[136,512]{1,0:T(8,128)S(1)} collective-permute-done((f32[136,512]{1,0:T(8,128)S(1)}, f32[136,512]{1,0:T(8,128)S(1)}, u32[]{:S(2)}, u32[]{:S(2)}) %collective-permute-start.10) | collective-permute-done | bytes 278560 | tf_op jit(solution)/shard_map/ppermute | solution.py:55
  51.4 1.3 collective-permute-start.20
  52.7 3.2 %collective-permute-done.15.refs_9_.refs_25_ = f32[136,512]{1,0:T(8,128)S(1)} collective-permute-done((f32[136,512]{1,0:T(8,128)S(1)}, f32[136,512]{1,0:T(8,128)S(1)}, u32[]{:S(2)}, u32[]{:S(2)}) %collective-permute-start.15) | collective-permute-done | bytes 278560 | tf_op jit(solution)/shard_map/ppermute | solution.py:55
  55.8 0.8 collective-permute-start.17
  56.6 0.2 collective-permute-done.13.refs_8_.refs_24_
  56.8 2.2 %collective-permute-start.19 = (f32[128,512]{1,0:T(8,128)S(1)}, f32[128,512]{1,0:T(8,128)S(1)}, u32[]{:S(2)}, u32[]{:S(2)}) collective-permute-start(f32[128,512]{1,0:T(8,128)S(1)} %collective-permute-done.18.refs_12_.refs_28_), channel_id=1, source_target_pairs={{0,4},{1,5},{2,6},{3,7},{4,0},{5,1},{6,2},{7,3},{8,12},{9,13},{10,... | collective-permute-start | bytes 786440 | tf_op jit(solution)/shard_map/ppermute | solution.py:55
  59.0 1.2 collective-permute-done.19.refs_14_.refs_30_
  60.1 0.4 collective-permute-done.16.refs_10_.refs_26_
  60.5 2.3 %chain_x.1 = (f32[128,512]{1,0:T(8,128)S(1)}, f32[136,512]{1,0:T(8,128)S(1)}) custom-call(f32[128,512]{1,0:T(8,128)S(1)} %get-tuple-element.37.refs_0_.refs_16_, f32[136,512]{1,0:T(8,128)S(1)} %get-tuple-element.38.refs_1_.refs_17_, f32[128,512]{1,0:T(8,128)S(1)} %collective-permute-done.7.refs_2_.refs_18_, ...), custom_call_target="tpu_custom_call" | custom-call | tf_op jit(solution)/shard_map/chain_x/pallas_call | solution.py:293
  62.8 2.8 %collective-permute-start.28 = (f32[136,512]{1,0:T(8,128)S(1)}, f32[136,512]{1,0:T(8,128)S(1)}, u32[]{:S(2)}, u32[]{:S(2)}) collective-permute-start(f32[136,512]{1,0:T(8,128)S(1)} %get-tuple-element.40.refs_1_), channel_id=1, source_target_pairs={{0,24},{1,25},{2,26},{3,27},{4,28},{5,29},{6,30},{7,31},{8,0},{9,1... | collective-permute-start | bytes 835592 | tf_op jit(solution)/shard_map/ppermute | solution.py:55
  65.6 2.7 %collective-permute-start.32 = (f32[128,512]{1,0:T(8,128)S(1)}, f32[128,512]{1,0:T(8,128)S(1)}, u32[]{:S(2)}, u32[]{:S(2)}) collective-permute-start(f32[128,512]{1,0:T(8,128)S(1)} %get-tuple-element.39.refs_0_), channel_id=1, source_target_pairs={{0,24},{1,25},{2,26},{3,27},{4,28},{5,29},{6,30},{7,31},{8,0},{9,1... | collective-permute-start | bytes 786440 | tf_op jit(solution)/shard_map/ppermute | solution.py:55
  68.3 1.2 collective-permute-start.21
  69.5 4.5 %collective-permute-done.23.refs_4_ = f32[128,512]{1,0:T(8,128)S(1)} collective-permute-done((f32[128,512]{1,0:T(8,128)S(1)}, f32[128,512]{1,0:T(8,128)S(1)}, u32[]{:S(2)}, u32[]{:S(2)}) %collective-permute-start.23) | collective-permute-done | bytes 262176 | tf_op jit(solution)/shard_map/ppermute | solution.py:55
  74.0 2.6 %collective-permute-start.22 = (f32[136,512]{1,0:T(8,128)S(1)}, f32[136,512]{1,0:T(8,128)S(1)}, u32[]{:S(2)}, u32[]{:S(2)}) collective-permute-start(f32[136,512]{1,0:T(8,128)S(1)} %get-tuple-element.40.refs_1_), channel_id=1, source_target_pairs={{0,4},{1,5},{2,6},{3,7},{4,0},{5,1},{6,2},{7,3},{8,12},{9,13},{10,... | collective-permute-start | bytes 835592 | tf_op jit(solution)/shard_map/ppermute | solution.py:55
  76.7 0.2 collective-permute-done.32.refs_12_
  76.9 1.2 collective-permute-start.27
  78.2 1.6 %collective-permute-start.25 = (f32[128,512]{1,0:T(8,128)S(1)}, f32[128,512]{1,0:T(8,128)S(1)}, u32[]{:S(2)}, u32[]{:S(2)}) collective-permute-start(f32[128,512]{1,0:T(8,128)S(1)} %collective-permute-done.23.refs_4_), channel_id=1, source_target_pairs={{0,4},{1,5},{2,6},{3,7},{4,0},{5,1},{6,2},{7,3},{8,12},{9,13},{10,... | collective-permute-start | bytes 786440 | tf_op jit(solution)/shard_map/ppermute | solution.py:55
  79.7 0.3 collective-permute-done.24.refs_5_
  80.0 1.5 %collective-permute-start.26 = (f32[136,512]{1,0:T(8,128)S(1)}, f32[136,512]{1,0:T(8,128)S(1)}, u32[]{:S(2)}, u32[]{:S(2)}) collective-permute-start(f32[136,512]{1,0:T(8,128)S(1)} %collective-permute-done.24.refs_5_), channel_id=1, source_target_pairs={{0,4},{1,5},{2,6},{3,7},{4,0},{5,1},{6,2},{7,3},{8,12},{9,13},{10,... | collective-permute-start | bytes 835592 | tf_op jit(solution)/shard_map/ppermute | solution.py:55
  81.5 3.4 %collective-permute-done.29.refs_9_ = f32[136,512]{1,0:T(8,128)S(1)} collective-permute-done((f32[136,512]{1,0:T(8,128)S(1)}, f32[136,512]{1,0:T(8,128)S(1)}, u32[]{:S(2)}, u32[]{:S(2)}) %collective-permute-start.29) | collective-permute-done | bytes 278560 | tf_op jit(solution)/shard_map/ppermute | solution.py:55
  85.0 0.8 collective-permute-start.31
  85.8 1.8 %collective-permute-start.33 = (f32[128,512]{1,0:T(8,128)S(1)}, f32[128,512]{1,0:T(8,128)S(1)}, u32[]{:S(2)}, u32[]{:S(2)}) collective-permute-start(f32[128,512]{1,0:T(8,128)S(1)} %collective-permute-done.32.refs_12_), channel_id=1, source_target_pairs={{0,4},{1,5},{2,6},{3,7},{4,0},{5,1},{6,2},{7,3},{8,12},{9,13},{10,... | collective-permute-start | bytes 786440 | tf_op jit(solution)/shard_map/ppermute | solution.py:55
  87.6 1.2 collective-permute-done.33.refs_14_
  88.8 0.4 collective-permute-done.30.refs_10_
  89.1 3.4 %chain_y.1.map_ref = f32[520,512]{1,0:T(8,128)S(1)} custom-call(f32[128,512]{1,0:T(8,128)S(1)} %get-tuple-element.39.refs_0_, f32[136,512]{1,0:T(8,128)S(1)} %get-tuple-element.40.refs_1_, f32[128,512]{1,0:T(8,128)S(1)} %collective-permute-done.21.refs_2_, f32[136,512]{1,0:T(8,128)S(1)} %collective-permute-done.22.refs_3_, ...), custom_call_target="tpu_custom_call" | custom-call | tf_op jit(solution)/shard_map/chain_y/pallas_call | solution.py:293
  92.5 0.3 plane.7
  92.8 0.7 collective-permute-start.35
  93.5 0.3 plane.8
  93.7 0.7 collective-permute-start.36
  94.4 0.3 plane.9
  94.7 0.7 collective-permute-start.37
  95.4 0.3 plane.10
  95.6 0.7 collective-permute-start.38
  96.3 0.3 plane.11
  96.6 0.7 collective-permute-start.39
  97.3 0.3 plane.12
  97.5 0.7 collective-permute-start.40
  98.2 0.3 plane.13
  98.5 1.3 collective-permute-start.41
  99.8 22.8 %collective-permute-done.41.came_ref = f32[8,512]{1,0:T(8,128)S(1)} collective-permute-done((f32[8,512]{1,0:T(8,128)S(1)}, f32[8,512]{1,0:T(8,128)S(1)}, u32[]{:S(2)}, u32[]{:S(2)}) %collective-permute-start.41) | collective-permute-done | bytes 16416 | tf_op jit(solution)/shard_map/ppermute | solution.py:355
  122.5 3.7 %down.1 = (f32[8,128]{1,0:T(8,128)S(1)}, f32[8,128]{1,0:T(8,128)S(1)}) custom-call(f32[8,512]{1,0:T(8,128)S(1)} %get-tuple-element.53.carried_ref, f32[8,512]{1,0:T(8,128)S(1)} %collective-permute-done.41.came_ref, f32[520,512]{1,0:T(8,128)S(1)} %step.1.own_ref, f32[520,512]{1,0:T(8,128)S(1)} %collective-permute-done.6.other_ref, ...), custom_call_target="tpu_custom_call" | custom-call | tf_op jit(solution)/shard_map/down/pallas_call | solution.py:356
  126.2 8.2 %collective-permute-start.42 = (f32[8,128]{1,0:T(8,128)S(1)}, f32[8,128]{1,0:T(8,128)S(1)}, u32[]{:S(2)}, u32[]{:S(2)}) collective-permute-start(f32[8,128]{1,0:T(8,128)S(1)} %get-tuple-element.55), channel_id=1, source_target_pairs={{0,1},{1,0},{2,5},{3,4},{4,3},{5,2},{6,7},{7,6},{8,9},{9,8},{10,13... | collective-permute-start | bytes 12296 | tf_op jit(solution)/shard_map/ppermute | solution.py:55
  134.4 1.9 %collective-permute-start.43 = (f32[8,128]{1,0:T(8,128)S(1)}, f32[8,128]{1,0:T(8,128)S(1)}, u32[]{:S(2)}, u32[]{:S(2)}) collective-permute-start(f32[8,128]{1,0:T(8,128)S(1)} %get-tuple-element.56), channel_id=1, source_target_pairs={{0,0},{1,1},{2,4},{3,5},{4,2},{5,3},{6,6},{7,7},{8,8},{9,9},{10,12... | collective-permute-start | bytes 12296 | tf_op jit(solution)/shard_map/ppermute | solution.py:55
  136.3 4.5 %collective-permute-done.43 = f32[8,128]{1,0:T(8,128)S(1)} collective-permute-done((f32[8,128]{1,0:T(8,128)S(1)}, f32[8,128]{1,0:T(8,128)S(1)}, u32[]{:S(2)}, u32[]{:S(2)}) %collective-permute-start.43) | collective-permute-done | bytes 4128 | tf_op jit(solution)/shard_map/ppermute | solution.py:55
  140.8 0.6 pad_maximum_fusion
  (44 shorter events, 0.5 us)
Async XLA Ops:
  0.0 5.4 %copy-start = (s32[4,8,2]{1,2,0:T(2,128)S(1)}, s32[4,8,2]{1,2,0:T(2,128)}, u32[]{:S(2)}) copy-start(s32[4,8,2]{1,2,0:T(2,128)} %param.9) | copy-start | bytes 772
  2.0 25.3 %collective-permute-start.5 = (f32[256,512]{1,0:T(8,128)S(1)}, f32[256,512]{1,0:T(8,128)S(1)}, u32[]{:S(2)}, u32[]{:S(2)}) collective-permute-start(f32[256,512]{1,0:T(8,128)S(1)} %get-tuple-element.36), channel_id=1, source_target_pairs={{0,4},{1,5},{2,6},{3,7},{4,0},{5,1},{6,2},{7,3},{8,12},{9,13},{10,... | collective-permute-start | bytes 1572872 | tf_op jit(solution)/shard_map/ppermute | solution.py:55
  5.6 6.3 %collective-permute-start = (s32[64]{0:T(128)S(1)}, s32[64]{0:T(128)S(1)}, u32[]{:S(2)}, u32[]{:S(2)}) collective-permute-start(s32[64]{0:T(128)S(1)} %reshape.3.ids_own), channel_id=1, source_target_pairs={{0,4},{1,5},{2,6},{3,7},{4,0},{5,1},{6,2},{7,3},{8,12},{9,13},{10,... | collective-permute-start | bytes 776 | tf_op jit(solution)/shard_map/ppermute | solution.py:55
  5.7 9.7 %collective-permute-start.1 = (f32[328,256]{1,0:T(8,128)S(1)}, f32[328,256]{1,0:T(8,128)S(1)}, u32[]{:S(2)}, u32[]{:S(2)}) collective-permute-start(f32[328,256]{1,0:T(8,128)S(1)} %get-tuple-element.31), channel_id=1, source_target_pairs={{0,0},{1,4},{2,1},{3,5},{4,2},{5,6},{6,3},{7,7},{8,8},{9,12},{10,9... | collective-permute-start | bytes 1007624 | tf_op jit(solution)/shard_map/ppermute | solution.py:55
  9.0 12.2 %collective-permute-start.2 = (f32[328,256]{1,0:T(8,128)S(1)}, f32[328,256]{1,0:T(8,128)S(1)}, u32[]{:S(2)}, u32[]{:S(2)}) collective-permute-start(f32[328,256]{1,0:T(8,128)S(1)} %get-tuple-element.32), channel_id=1, source_target_pairs={{0,4},{1,1},{2,5},{3,0},{4,6},{5,3},{6,7},{7,2},{8,12},{9,9},{10,1... | collective-permute-start | bytes 1007624 | tf_op jit(solution)/shard_map/ppermute | solution.py:55
  11.8 15.5 %collective-permute-start.3 = (f32[328,256]{1,0:T(8,128)S(1)}, f32[328,256]{1,0:T(8,128)S(1)}, u32[]{:S(2)}, u32[]{:S(2)}) collective-permute-start(f32[328,256]{1,0:T(8,128)S(1)} %get-tuple-element.33), channel_id=1, source_target_pairs={{0,1},{1,5},{2,0},{3,4},{4,3},{5,7},{6,2},{7,6},{8,9},{9,13},{10,8... | collective-permute-start | bytes 1007624 | tf_op jit(solution)/shard_map/ppermute | solution.py:55
  11.9 15.4 %collective-permute-start.4 = (f32[328,256]{1,0:T(8,128)S(1)}, f32[328,256]{1,0:T(8,128)S(1)}, u32[]{:S(2)}, u32[]{:S(2)}) collective-permute-start(f32[328,256]{1,0:T(8,128)S(1)} %get-tuple-element.34), channel_id=1, source_target_pairs={{0,5},{1,0},{2,4},{3,1},{4,7},{5,2},{6,6},{7,3},{8,13},{9,8},{10,1... | collective-permute-start | bytes 1007624 | tf_op jit(solution)/shard_map/ppermute | solution.py:55
  30.7 2.7 %collective-permute-start.6 = (f32[520,512]{1,0:T(8,128)S(1)}, f32[520,512]{1,0:T(8,128)S(1)}, u32[]{:S(2)}, u32[]{:S(2)}) collective-permute-start(f32[520,512]{1,0:T(8,128)S(1)} %step.1.own_ref), channel_id=1, source_target_pairs={{0,4},{1,5},{2,6},{3,7},{4,0},{5,1},{6,2},{7,3},{8,12},{9,13},{10,... | collective-permute-start | bytes 3194888 | tf_op jit(solution)/shard_map/ppermute | solution.py:55
  34.0 13.5 %collective-permute-start.14 = (f32[136,512]{1,0:T(8,128)S(1)}, f32[136,512]{1,0:T(8,128)S(1)}, u32[]{:S(2)}, u32[]{:S(2)}) collective-permute-start(f32[136,512]{1,0:T(8,128)S(1)} %get-tuple-element.38.refs_1_.refs_17_), channel_id=1, source_target_pairs={{0,3},{1,0},{2,1},{3,2},{4,7},{5,4},{6,5},{7,6},{8,11},{9,8},{10,9... | collective-permute-start | bytes 835592 | tf_op jit(solution)/shard_map/ppermute | solution.py:55
  36.7 8.7 %collective-permute-start.9 = (f32[128,512]{1,0:T(8,128)S(1)}, f32[128,512]{1,0:T(8,128)S(1)}, u32[]{:S(2)}, u32[]{:S(2)}) collective-permute-start(f32[128,512]{1,0:T(8,128)S(1)} %get-tuple-element.37.refs_0_.refs_16_), channel_id=1, source_target_pairs={{0,1},{1,2},{2,3},{3,0},{4,5},{5,6},{6,7},{7,4},{8,9},{9,10},{10,1... | collective-permute-start | bytes 786440 | tf_op jit(solution)/shard_map/ppermute | solution.py:55
  36.7 11.5 %collective-permute-start.18 = (f32[128,512]{1,0:T(8,128)S(1)}, f32[128,512]{1,0:T(8,128)S(1)}, u32[]{:S(2)}, u32[]{:S(2)}) collective-permute-start(f32[128,512]{1,0:T(8,128)S(1)} %get-tuple-element.37.refs_0_.refs_16_), channel_id=1, source_target_pairs={{0,3},{1,0},{2,1},{3,2},{4,7},{5,4},{6,5},{7,6},{8,11},{9,8},{10,9... | collective-permute-start | bytes 786440 | tf_op jit(solution)/shard_map/ppermute | solution.py:55
  39.4 9.6 %collective-permute-start.7 = (f32[128,512]{1,0:T(8,128)S(1)}, f32[128,512]{1,0:T(8,128)S(1)}, u32[]{:S(2)}, u32[]{:S(2)}) collective-permute-start(f32[128,512]{1,0:T(8,128)S(1)} %get-tuple-element.37.refs_0_.refs_16_), channel_id=1, source_target_pairs={{0,4},{1,5},{2,6},{3,7},{4,0},{5,1},{6,2},{7,3},{8,12},{9,13},{10,... | collective-permute-start | bytes 786440 | tf_op jit(solution)/shard_map/ppermute | solution.py:55
  40.4 10.9 %collective-permute-start.10 = (f32[136,512]{1,0:T(8,128)S(1)}, f32[136,512]{1,0:T(8,128)S(1)}, u32[]{:S(2)}, u32[]{:S(2)}) collective-permute-start(f32[136,512]{1,0:T(8,128)S(1)} %get-tuple-element.38.refs_1_.refs_17_), channel_id=1, source_target_pairs={{0,1},{1,2},{2,3},{3,0},{4,5},{5,6},{6,7},{7,4},{8,9},{9,10},{10,1... | collective-permute-start | bytes 835592 | tf_op jit(solution)/shard_map/ppermute | solution.py:55
  45.4 7.2 %collective-permute-start.8 = (f32[136,512]{1,0:T(8,128)S(1)}, f32[136,512]{1,0:T(8,128)S(1)}, u32[]{:S(2)}, u32[]{:S(2)}) collective-permute-start(f32[136,512]{1,0:T(8,128)S(1)} %get-tuple-element.38.refs_1_.refs_17_), channel_id=1, source_target_pairs={{0,4},{1,5},{2,6},{3,7},{4,0},{5,1},{6,2},{7,3},{8,12},{9,13},{10,... | collective-permute-start | bytes 835592 | tf_op jit(solution)/shard_map/ppermute | solution.py:55
  47.6 8.3 %collective-permute-start.15 = (f32[136,512]{1,0:T(8,128)S(1)}, f32[136,512]{1,0:T(8,128)S(1)}, u32[]{:S(2)}, u32[]{:S(2)}) collective-permute-start(f32[136,512]{1,0:T(8,128)S(1)} %collective-permute-done.14.refs_13_.refs_29_), channel_id=1, source_target_pairs={{0,3},{1,0},{2,1},{3,2},{4,7},{5,4},{6,5},{7,6},{8,11},{9,8},{10,9... | collective-permute-start | bytes 835592 | tf_op jit(solution)/shard_map/ppermute | solution.py:55
  48.3 8.5 %collective-permute-start.13 = (f32[128,512]{1,0:T(8,128)S(1)}, f32[128,512]{1,0:T(8,128)S(1)}, u32[]{:S(2)}, u32[]{:S(2)}) collective-permute-start(f32[128,512]{1,0:T(8,128)S(1)} %collective-permute-done.9.refs_4_.refs_20_), channel_id=1, source_target_pairs={{0,1},{1,2},{2,3},{3,0},{4,5},{5,6},{6,7},{7,4},{8,9},{9,10},{10,1... | collective-permute-start | bytes 786440 | tf_op jit(solution)/shard_map/ppermute | solution.py:55
  49.0 9.9 %collective-permute-start.11 = (f32[128,512]{1,0:T(8,128)S(1)}, f32[128,512]{1,0:T(8,128)S(1)}, u32[]{:S(2)}, u32[]{:S(2)}) collective-permute-start(f32[128,512]{1,0:T(8,128)S(1)} %collective-permute-done.9.refs_4_.refs_20_), channel_id=1, source_target_pairs={{0,4},{1,5},{2,6},{3,7},{4,0},{5,1},{6,2},{7,3},{8,12},{9,13},{10,... | collective-permute-start | bytes 786440 | tf_op jit(solution)/shard_map/ppermute | solution.py:55
  51.4 8.7 %collective-permute-start.20 = (f32[136,512]{1,0:T(8,128)S(1)}, f32[136,512]{1,0:T(8,128)S(1)}, u32[]{:S(2)}, u32[]{:S(2)}) collective-permute-start(f32[136,512]{1,0:T(8,128)S(1)} %collective-permute-done.14.refs_13_.refs_29_), channel_id=1, source_target_pairs={{0,4},{1,5},{2,6},{3,7},{4,0},{5,1},{6,2},{7,3},{8,12},{9,13},{10,... | collective-permute-start | bytes 835592 | tf_op jit(solution)/shard_map/ppermute | solution.py:55
  52.6 7.5 %collective-permute-start.12 = (f32[136,512]{1,0:T(8,128)S(1)}, f32[136,512]{1,0:T(8,128)S(1)}, u32[]{:S(2)}, u32[]{:S(2)}) collective-permute-start(f32[136,512]{1,0:T(8,128)S(1)} %collective-permute-done.10.refs_5_.refs_21_), channel_id=1, source_target_pairs={{0,4},{1,5},{2,6},{3,7},{4,0},{5,1},{6,2},{7,3},{8,12},{9,13},{10,... | collective-permute-start | bytes 835592 | tf_op jit(solution)/shard_map/ppermute | solution.py:55
  55.8 4.6 %collective-permute-start.17 = (f32[136,512]{1,0:T(8,128)S(1)}, f32[136,512]{1,0:T(8,128)S(1)}, u32[]{:S(2)}, u32[]{:S(2)}) collective-permute-start(f32[136,512]{1,0:T(8,128)S(1)} %collective-permute-done.15.refs_9_.refs_25_), channel_id=1, source_target_pairs={{0,4},{1,5},{2,6},{3,7},{4,0},{5,1},{6,2},{7,3},{8,12},{9,13},{10,... | collective-permute-start | bytes 835592 | tf_op jit(solution)/shard_map/ppermute | solution.py:55
  56.8 3.3 %collective-permute-start.19 = (f32[128,512]{1,0:T(8,128)S(1)}, f32[128,512]{1,0:T(8,128)S(1)}, u32[]{:S(2)}, u32[]{:S(2)}) collective-permute-start(f32[128,512]{1,0:T(8,128)S(1)} %collective-permute-done.18.refs_12_.refs_28_), channel_id=1, source_target_pairs={{0,4},{1,5},{2,6},{3,7},{4,0},{5,1},{6,2},{7,3},{8,12},{9,13},{10,... | collective-permute-start | bytes 786440 | tf_op jit(solution)/shard_map/ppermute | solution.py:55
  58.9 1.5 %collective-permute-start.16 = (f32[128,512]{1,0:T(8,128)S(1)}, f32[128,512]{1,0:T(8,128)S(1)}, u32[]{:S(2)}, u32[]{:S(2)}) collective-permute-start(f32[128,512]{1,0:T(8,128)S(1)} %collective-permute-done.13.refs_8_.refs_24_), channel_id=1, source_target_pairs={{0,4},{1,5},{2,6},{3,7},{4,0},{5,1},{6,2},{7,3},{8,12},{9,13},{10,... | collective-permute-start | bytes 786440 | tf_op jit(solution)/shard_map/ppermute | solution.py:55
  62.8 13.9 %collective-permute-start.28 = (f32[136,512]{1,0:T(8,128)S(1)}, f32[136,512]{1,0:T(8,128)S(1)}, u32[]{:S(2)}, u32[]{:S(2)}) collective-permute-start(f32[136,512]{1,0:T(8,128)S(1)} %get-tuple-element.40.refs_1_), channel_id=1, source_target_pairs={{0,24},{1,25},{2,26},{3,27},{4,28},{5,29},{6,30},{7,31},{8,0},{9,1... | collective-permute-start | bytes 835592 | tf_op jit(solution)/shard_map/ppermute | solution.py:55
  65.6 8.4 %collective-permute-start.23 = (f32[128,512]{1,0:T(8,128)S(1)}, f32[128,512]{1,0:T(8,128)S(1)}, u32[]{:S(2)}, u32[]{:S(2)}) collective-permute-start(f32[128,512]{1,0:T(8,128)S(1)} %get-tuple-element.39.refs_0_), channel_id=1, source_target_pairs={{0,8},{1,9},{2,10},{3,11},{4,12},{5,13},{6,14},{7,15},{8,16},{9,17... | collective-permute-start | bytes 786440 | tf_op jit(solution)/shard_map/ppermute | solution.py:55
  65.6 11.3 %collective-permute-start.32 = (f32[128,512]{1,0:T(8,128)S(1)}, f32[128,512]{1,0:T(8,128)S(1)}, u32[]{:S(2)}, u32[]{:S(2)}) collective-permute-start(f32[128,512]{1,0:T(8,128)S(1)} %get-tuple-element.39.refs_0_), channel_id=1, source_target_pairs={{0,24},{1,25},{2,26},{3,27},{4,28},{5,29},{6,30},{7,31},{8,0},{9,1... | collective-permute-start | bytes 786440 | tf_op jit(solution)/shard_map/ppermute | solution.py:55
  68.3 9.9 %collective-permute-start.21 = (f32[128,512]{1,0:T(8,128)S(1)}, f32[128,512]{1,0:T(8,128)S(1)}, u32[]{:S(2)}, u32[]{:S(2)}) collective-permute-start(f32[128,512]{1,0:T(8,128)S(1)} %get-tuple-element.39.refs_0_), channel_id=1, source_target_pairs={{0,4},{1,5},{2,6},{3,7},{4,0},{5,1},{6,2},{7,3},{8,12},{9,13},{10,... | collective-permute-start | bytes 786440 | tf_op jit(solution)/shard_map/ppermute | solution.py:55
  69.5 10.5 %collective-permute-start.24 = (f32[136,512]{1,0:T(8,128)S(1)}, f32[136,512]{1,0:T(8,128)S(1)}, u32[]{:S(2)}, u32[]{:S(2)}) collective-permute-start(f32[136,512]{1,0:T(8,128)S(1)} %get-tuple-element.40.refs_1_), channel_id=1, source_target_pairs={{0,8},{1,9},{2,10},{3,11},{4,12},{5,13},{6,14},{7,15},{8,16},{9,17... | collective-permute-start | bytes 835592 | tf_op jit(solution)/shard_map/ppermute | solution.py:55
  74.0 7.5 %collective-permute-start.22 = (f32[136,512]{1,0:T(8,128)S(1)}, f32[136,512]{1,0:T(8,128)S(1)}, u32[]{:S(2)}, u32[]{:S(2)}) collective-permute-start(f32[136,512]{1,0:T(8,128)S(1)} %get-tuple-element.40.refs_1_), channel_id=1, source_target_pairs={{0,4},{1,5},{2,6},{3,7},{4,0},{5,1},{6,2},{7,3},{8,12},{9,13},{10,... | collective-permute-start | bytes 835592 | tf_op jit(solution)/shard_map/ppermute | solution.py:55
  76.7 8.3 %collective-permute-start.29 = (f32[136,512]{1,0:T(8,128)S(1)}, f32[136,512]{1,0:T(8,128)S(1)}, u32[]{:S(2)}, u32[]{:S(2)}) collective-permute-start(f32[136,512]{1,0:T(8,128)S(1)} %collective-permute-done.28.refs_13_), channel_id=1, source_target_pairs={{0,24},{1,25},{2,26},{3,27},{4,28},{5,29},{6,30},{7,31},{8,0},{9,1... | collective-permute-start | bytes 835592 | tf_op jit(solution)/shard_map/ppermute | solution.py:55
  76.9 8.8 %collective-permute-start.27 = (f32[128,512]{1,0:T(8,128)S(1)}, f32[128,512]{1,0:T(8,128)S(1)}, u32[]{:S(2)}, u32[]{:S(2)}) collective-permute-start(f32[128,512]{1,0:T(8,128)S(1)} %collective-permute-done.23.refs_4_), channel_id=1, source_target_pairs={{0,8},{1,9},{2,10},{3,11},{4,12},{5,13},{6,14},{7,15},{8,16},{9,17... | collective-permute-start | bytes 786440 | tf_op jit(solution)/shard_map/ppermute | solution.py:55
  78.2 9.4 %collective-permute-start.25 = (f32[128,512]{1,0:T(8,128)S(1)}, f32[128,512]{1,0:T(8,128)S(1)}, u32[]{:S(2)}, u32[]{:S(2)}) collective-permute-start(f32[128,512]{1,0:T(8,128)S(1)} %collective-permute-done.23.refs_4_), channel_id=1, source_target_pairs={{0,4},{1,5},{2,6},{3,7},{4,0},{5,1},{6,2},{7,3},{8,12},{9,13},{10,... | collective-permute-start | bytes 786440 | tf_op jit(solution)/shard_map/ppermute | solution.py:55
  80.0 8.7 %collective-permute-start.26 = (f32[136,512]{1,0:T(8,128)S(1)}, f32[136,512]{1,0:T(8,128)S(1)}, u32[]{:S(2)}, u32[]{:S(2)}) collective-permute-start(f32[136,512]{1,0:T(8,128)S(1)} %collective-permute-done.24.refs_5_), channel_id=1, source_target_pairs={{0,4},{1,5},{2,6},{3,7},{4,0},{5,1},{6,2},{7,3},{8,12},{9,13},{10,... | collective-permute-start | bytes 835592 | tf_op jit(solution)/shard_map/ppermute | solution.py:55
  81.5 7.2 %collective-permute-start.34 = (f32[136,512]{1,0:T(8,128)S(1)}, f32[136,512]{1,0:T(8,128)S(1)}, u32[]{:S(2)}, u32[]{:S(2)}) collective-permute-start(f32[136,512]{1,0:T(8,128)S(1)} %collective-permute-done.28.refs_13_), channel_id=1, source_target_pairs={{0,4},{1,5},{2,6},{3,7},{4,0},{5,1},{6,2},{7,3},{8,12},{9,13},{10,... | collective-permute-start | bytes 835592 | tf_op jit(solution)/shard_map/ppermute | solution.py:55
  85.0 4.2 %collective-permute-start.31 = (f32[136,512]{1,0:T(8,128)S(1)}, f32[136,512]{1,0:T(8,128)S(1)}, u32[]{:S(2)}, u32[]{:S(2)}) collective-permute-start(f32[136,512]{1,0:T(8,128)S(1)} %collective-permute-done.29.refs_9_), channel_id=1, source_target_pairs={{0,4},{1,5},{2,6},{3,7},{4,0},{5,1},{6,2},{7,3},{8,12},{9,13},{10,... | collective-permute-start | bytes 835592 | tf_op jit(solution)/shard_map/ppermute | solution.py:55
  85.8 3.0 %collective-permute-start.33 = (f32[128,512]{1,0:T(8,128)S(1)}, f32[128,512]{1,0:T(8,128)S(1)}, u32[]{:S(2)}, u32[]{:S(2)}) collective-permute-start(f32[128,512]{1,0:T(8,128)S(1)} %collective-permute-done.32.refs_12_), channel_id=1, source_target_pairs={{0,4},{1,5},{2,6},{3,7},{4,0},{5,1},{6,2},{7,3},{8,12},{9,13},{10,... | collective-permute-start | bytes 786440 | tf_op jit(solution)/shard_map/ppermute | solution.py:55
  87.6 1.5 %collective-permute-start.30 = (f32[128,512]{1,0:T(8,128)S(1)}, f32[128,512]{1,0:T(8,128)S(1)}, u32[]{:S(2)}, u32[]{:S(2)}) collective-permute-start(f32[128,512]{1,0:T(8,128)S(1)} %collective-permute-done.27.refs_8_), channel_id=1, source_target_pairs={{0,4},{1,5},{2,6},{3,7},{4,0},{5,1},{6,2},{7,3},{8,12},{9,13},{10,... | collective-permute-start | bytes 786440 | tf_op jit(solution)/shard_map/ppermute | solution.py:55
  92.8 0.7 collective-permute-start.35
  93.7 0.7 collective-permute-start.36
  94.7 0.7 collective-permute-start.37
  95.6 0.7 collective-permute-start.38
  96.6 0.7 collective-permute-start.39
  97.5 0.7 collective-permute-start.40
  98.5 24.1 %collective-permute-start.41 = (f32[8,512]{1,0:T(8,128)S(1)}, f32[8,512]{1,0:T(8,128)S(1)}, u32[]{:S(2)}, u32[]{:S(2)}) collective-permute-start(f32[8,512]{1,0:T(8,128)S(1)} %get-tuple-element.54), channel_id=1, source_target_pairs={{32,0},{36,4},{40,8},{44,12},{48,16},{52,20},{56,24},{60,28},{33,1... | collective-permute-start | bytes 49160 | tf_op jit(solution)/shard_map/ppermute | solution.py:355
  126.2 10.1 %collective-permute-start.42 = (f32[8,128]{1,0:T(8,128)S(1)}, f32[8,128]{1,0:T(8,128)S(1)}, u32[]{:S(2)}, u32[]{:S(2)}) collective-permute-start(f32[8,128]{1,0:T(8,128)S(1)} %get-tuple-element.55), channel_id=1, source_target_pairs={{0,1},{1,0},{2,5},{3,4},{4,3},{5,2},{6,7},{7,6},{8,9},{9,8},{10,13... | collective-permute-start | bytes 12296 | tf_op jit(solution)/shard_map/ppermute | solution.py:55
  134.4 6.4 %collective-permute-start.43 = (f32[8,128]{1,0:T(8,128)S(1)}, f32[8,128]{1,0:T(8,128)S(1)}, u32[]{:S(2)}, u32[]{:S(2)}) collective-permute-start(f32[8,128]{1,0:T(8,128)S(1)} %get-tuple-element.56), channel_id=1, source_target_pairs={{0,0},{1,1},{2,4},{3,5},{4,2},{5,3},{6,6},{7,7},{8,8},{9,9},{10,12... | collective-permute-start | bytes 12296 | tf_op jit(solution)/shard_map/ppermute | solution.py:55

commit v3 on v2

v3 whole, which is shorter than its diff:
```python
import jax
import jax.numpy as jnp
from jax import lax
from jax.experimental import pallas as pl
from jax.experimental.pallas import tpu as pltpu
from jax.sharding import PartitionSpec as P

NZ, NY, NC, NX = 8, 4, 2, 4
W = 512
B = 128
HALF = 256
PAN = HALF + 8
FULL = W + 8
AXES = ("tm", "state")
F32 = jnp.float32
VMEM_LIMIT = 24 * 1024 * 1024


def turn(x):
    return 2 * (x % 2) + x // 2


def joint(move):
    pairs = []
    for z in range(NZ):
        for y in range(NY):
            for c in range(NC):
                for x in range(NX):
                    y2, c2, x2 = move(y, c, x)
                    source = ((z * NY + y) * NC + c) * NX + x
                    pairs.append((source, ((z * NY + y2) * NC + c2) * NX + x2))
    return pairs


def spread_move(p):
    def move(y, c, x):
        q = (x + p) % 4
        return y, q % 2, turn(2 * c + q // 2)

    return move


def collect_move(r):
    def move(y, c, x):
        return y, x % 2, 2 * c + (x // 2 + r) % 2

    return move


SWAP = joint(lambda y, c, x: (y, 1 - c, x))
SPREAD = [joint(spread_move(p)) for p in range(4)]
COLLECT = [joint(collect_move(r)) for r in range(2)]
RING_X = joint(lambda y, c, x: (y, c, (x + 1 + 2 * c) % 4))
RING_Y = joint(lambda y, c, x: ((y + 1 + 2 * c) % 4, c, x))


def move(value, pairs):
    return lax.ppermute(value, AXES, pairs)


def split(a):
    high = a.astype(jnp.bfloat16)
    return high, (a - high.astype(F32)).astype(jnp.bfloat16)


def dot(a, b):
    return jnp.dot(a, b, preferred_element_type=F32)


def mm3(a, b):
    return dot(a[0], b[0]) + (dot(a[0], b[1]) + dot(a[1], b[0]))


def rows_times(row8, matrix):
    column = jnp.transpose(row8)[:, 0:1]
    product = (matrix * column).reshape(matrix.shape[0] // 8, 8, matrix.shape[1])
    total = jnp.sum(jnp.sum(product, axis=0), axis=0, keepdims=True)
    return jnp.broadcast_to(total, (8, matrix.shape[1]))


def block(i):
    return pl.ds(pl.multiple_of(i * B, B), B)


def place():
    tm = lax.axis_index("tm")
    return lax.axis_index("state"), lax.rem(tm // 2, 4), tm // 8, lax.rem(tm, 2)


def next_block(x, skip):
    one = lax.rem(x + 1, 4)
    return jnp.where(one == skip, lax.rem(x + 2, 4), one)


def pack_kernel(
    p_ref, r_ref, t_ref, m_ref, q_ref, i_ref, pay0, pay1, pay2, pay3, local_ref, other_ref, means, ids, sems
):
    x, _, _, c = place()
    copies = []

    def start(source, target):
        copy = pltpu.make_async_copy(source, target, sems.at[len(copies)])
        copy.start()
        copies.append(copy)

    start(m_ref, means.at[0])
    start(q_ref, means.at[1])
    start(i_ref, ids)
    for p, pay in enumerate((pay0, pay1, pay2, pay3)):
        j = lax.rem(x + p, 4)
        after = next_block(x, 2 * lax.rem(j // 2, 2) + c)
        for row, ref in ((0, p_ref), (B, r_ref)):
            start(ref.at[j, :, block(x)], pay.at[row : row + B, 0:B])
            start(ref.at[j, :, block(after)], pay.at[row : row + B, B : 2 * B])
        start(t_ref.at[j, 0], pay.at[256:320, 0:B])
        start(t_ref.at[j, 1], pay.at[256:320, B : 2 * B])
    mine = 2 * (x // 2) + c
    theirs = 2 * (x // 2) + 1 - c
    for row, ref in ((0, p_ref), (B, r_ref)):
        start(ref.at[mine], local_ref.at[row : row + B])
        start(ref.at[theirs], other_ref.at[row : row + B])
    for copy in copies[:3]:
        copy.wait()
    lane = lax.broadcasted_iota(jnp.int32, (2, 8), 1)
    low = lax.broadcasted_iota(jnp.int32, (1, B), 1) < 64
    for p, pay in enumerate((pay0, pay1, pay2, pay3)):
        j = lax.rem(x + p, 4)
        pay[320:321, 0:B] = means[0, pl.ds(j, 1), :]
        pay[320:321, B : 2 * B] = means[1, pl.ds(j, 1), :]
        for half in range(2):
            pair = jnp.sum(
                jnp.where(lane == 2 * x + half, ids[j].astype(F32), 0.0), axis=1, keepdims=True
            )
            first = jnp.broadcast_to(pair[0:1], (1, B))
            second = jnp.broadcast_to(pair[1:2], (1, B))
            pay[321:322, half * B : (half + 1) * B] = jnp.where(low, first, second)
            pay[322:323, half * B : (half + 1) * B] = jnp.where(low, second, first)
    for copy in copies[3:]:
        copy.wait()


def step_kernel(pay0, pay1, pay2, pay3, local_ref, other_ref, out_ref, pf, rf, inc, vec):
    x, y, z, c = place()
    j = 2 * (x // 2) + c
    same = lax.rem(x, 2) == c
    low = lax.broadcasted_iota(jnp.int32, (64, B), 1) < 64
    for p, pay in enumerate((pay0, pay1, pay2, pay3)):
        source = lax.rem(j - p + 4, 4)
        after = next_block(source, x)
        for row, full in ((0, pf), (B, rf)):
            full[block(source), block(source)] = pay[row : row + B, 0:B]
            beside = pay[row : row + B, B : 2 * B]
            full[block(source), block(after)] = beside
            full[block(after), block(source)] = jnp.transpose(beside)
        for half in range(2):
            r = 2 * source + half
            lanes = slice(half * B, (half + 1) * B)
            tiles = pay[256:320, lanes]
            turned = jnp.concatenate([tiles[:, 64:], tiles[:, :64]], axis=1)
            straight_to = jnp.broadcast_to(pay[321:322, lanes], (64, B))
            turned_to = jnp.broadcast_to(pay[322:323, lanes], (64, B))
            for g in range(4):
                here = jnp.where(low, 2.0 * g, 2.0 * g + 1.0)
                value = jnp.where(
                    straight_to == here, tiles, jnp.where(turned_to == here, turned, 0.0)
                )
                inc[pl.ds(pl.multiple_of(r * 64, 64), 64), g * B : (g + 1) * B] = value
        vec[0:8, block(source)] = jnp.broadcast_to(pay[320:321, 0:B], (8, B))
        vec[8:16, block(source)] = jnp.broadcast_to(pay[320:321, B : 2 * B], (8, B))
    for row, full in ((0, pf), (B, rf)):
        full[block(x), :] = jnp.where(
            same, local_ref[row : row + B, :], other_ref[row : row + B, :]
        )
        for d in (1, 2, 3):
            v = lax.rem(x + d, 4)
            full[block(v), block(x)] = jnp.transpose(full[block(x), block(v)])
    mixed = pf[...] + mm3(split(inc[...]), split(pf[...]))
    mixed = split(mixed)
    precision = split(rf[...])
    lead = split(mm3(split(vec[8:16, :]), precision))
    last = (z == NZ - 1) & (y == NY - 1) & (x == NX - 1) & (c == NC - 1)
    gain = mm3(precision, mixed)
    out_ref[0:W, :] = jnp.where(last, 0.0, gain)
    out_ref[W:FULL, :] = vec[0:8, :] - jnp.where(last, 0.0, mm3(lead, mixed))


def halves(ref, c):
    n = pl.multiple_of(c * HALF, HALF)
    m = pl.multiple_of((1 - c) * HALF, HALF)
    return ref[pl.ds(n, HALF), :], ref[pl.ds(m, HALF), :]


def pair_kernel(own_ref, other_ref, first_ref, second_ref):
    _, _, _, c = place()

    def compose(early, late):
        rows = jnp.concatenate([*halves(early, c), early[W:FULL, :]], axis=0)
        value = mm3(split(rows), split(late[0:W, :]))
        tail = value[W:] + late[W:FULL, :]
        for n, ref in enumerate((first_ref, second_ref)):
            ref[0:HALF, :] = value[n * HALF : (n + 1) * HALF]
            ref[HALF:PAN, :] = tail

    @pl.when(c == 0)
    def _():
        compose(other_ref, own_ref)

    @pl.when(c == 1)
    def _():
        compose(own_ref, other_ref)


def fetch(panels, held, sems, index, c, turned):
    forth, back, far = index + 3 - 2 * c, index + 1 + 2 * c, index + 2
    homes = ((index, c), (index, 1 - c), (forth, c), (forth, 1 - c), (back, 1 - c), (back, c), (far, c), (far, 1 - c))
    copies = []
    for n, (ref, (source, half)) in enumerate(zip(panels, homes)):
        slot = lax.rem(source, 4)
        if turned:
            slot = 2 * lax.rem(slot, 2) + slot // 2
        copy = pltpu.make_async_copy(ref, held.at[slot, half], sems.at[n])
        copy.start()
        copies.append(copy)
    return copies


def chain_kernel(along, whole, *refs):
    panels, held, outs, sems = refs[:8], refs[8], refs[9:-1], refs[-1]
    x, y, _, c = place()
    for copy in fetch(panels, held, sems, x if along == "x" else y, c, along == "x"):
        copy.wait()
    tail = held[3, 0, HALF:PAN, :]
    begin = 0 if whole else c
    rows = jnp.concatenate([held[3, begin, 0:HALF, :], held[3, 1 - begin, 0:HALF, :], tail], axis=0)
    for t in (2, 1, 0):
        left = split(rows)
        top = split(held[t, 0, 0:HALF, :])
        bottom = split(held[t, 1, 0:HALF, :])
        value = mm3((left[0][:, :HALF], left[1][:, :HALF]), top) + mm3(
            (left[0][:, HALF:], left[1][:, HALF:]), bottom
        )
        rows = jnp.concatenate([value[0:W], value[W:] + held[t, 0, HALF:PAN, :]], axis=0)
    if whole:
        outs[0][...] = rows
    else:
        for n in range(2):
            outs[n][0:HALF, :] = rows[n * HALF : (n + 1) * HALF]
            outs[n][HALF:PAN, :] = rows[W:FULL]


def plane_kernel(map_ref, carried_ref, came_ref, carried_out, out_ref):
    carried = carried_ref[...] + came_ref[...]
    carried_out[...] = carried
    out_ref[...] = rows_times(carried, map_ref[0:W, :]) + map_ref[W:FULL, :]


def down_kernel(carried_ref, came_ref, own_ref, other_ref, held_y, held_x, send0, send1, values):
    x, y, _, c = place()
    carried = carried_ref[...] + came_ref[...]
    for held, index in ((held_y, y), (held_x, 2 * lax.rem(x, 2) + x // 2)):
        for t in (3, 2, 1):
            matrix = jnp.concatenate([held[t, 0, 0:HALF, :], held[t, 1, 0:HALF, :]], axis=0)
            value = rows_times(carried, matrix) + held[t, 0, HALF:PAN, :]
            carried = jnp.where(t > index, value, carried)
    own_last = c == 1
    late = jnp.where(own_last, own_ref[...], other_ref[...])
    early = jnp.where(own_last, other_ref[...], own_ref[...])
    after = rows_times(carried, late[0:W]) + late[W:FULL]
    before = rows_times(after, early[0:W]) + early[W:FULL]
    top = lax.broadcasted_iota(jnp.int32, (8, W), 0) == 0
    values[...] = jnp.where(top, before, after)
    for r, send in enumerate((send0, send1)):
        send[...] = values[:, block(2 * c + lax.rem(x // 2 + r, 2))]


def shape(*dims):
    return jax.ShapeDtypeStruct(dims, F32)


PARAMS = pltpu.CompilerParams(vmem_limit_bytes=VMEM_LIMIT)
IN_VMEM = pl.BlockSpec(memory_space=pltpu.VMEM)
IN_HBM = pl.BlockSpec(memory_space=pltpu.HBM)
ANYWHERE = pl.BlockSpec(memory_space=pl.ANY)


def gather_panels(first, second, ring):
    one, two = move(first, ring), move(second, ring)
    far = move(one, ring)
    return first, second, one, two, move(one, SWAP), move(two, SWAP), far, move(far, SWAP)


def chain(along, whole, panels):
    def kernel(*refs):
        chain_kernel(along, whole, *refs)

    return pl.pallas_call(
        kernel,
        out_shape=[shape(4, 2, PAN, W)]
        + ([shape(FULL, W)] if whole else [shape(PAN, W)] * 2),
        in_specs=[ANYWHERE] * 8,
        out_specs=[IN_VMEM] * (2 if whole else 3),
        scratch_shapes=[pltpu.SemaphoreType.DMA((8,))],
        compiler_params=PARAMS,
        name="chain_" + along,
    )(*panels)


def in_hbm(value):
    return pltpu.with_memory_space_constraint(value, pltpu.HBM)


def on_device(spread, inverse, tiles, ids, mean, prior):
    *pays, local, other = pl.pallas_call(
        pack_kernel,
        out_shape=[shape(328, HALF)] * 4 + [shape(2 * B, W)] * 2,
        in_specs=[IN_HBM] * 6,
        out_specs=[IN_VMEM] * 6,
        scratch_shapes=[
            pltpu.VMEM((2, 4, B), F32),
            pltpu.VMEM((4, 2, 8), jnp.int32),
            pltpu.SemaphoreType.DMA((31,)),
        ],
        compiler_params=PARAMS,
        name="pack",
    )(*(in_hbm(a) for a in (spread, inverse, tiles, mean, prior, jnp.swapaxes(ids, 1, 2))))
    got = [move(pay, SPREAD[p]) for p, pay in enumerate(pays)]
    other = move(other, SWAP)
    step = pl.pallas_call(
        step_kernel,
        out_shape=shape(FULL, W),
        in_specs=[IN_VMEM] * 6,
        out_specs=IN_VMEM,
        scratch_shapes=[pltpu.VMEM((W, W), F32)] * 3 + [pltpu.VMEM((16, W), F32)],
        compiler_params=PARAMS,
        name="step",
    )(*got, local, other)
    twin = move(step, SWAP)
    pair = pl.pallas_call(
        pair_kernel,
        out_shape=[shape(PAN, W)] * 2,
        in_specs=[IN_VMEM] * 2,
        out_specs=[IN_VMEM] * 2,
        compiler_params=PARAMS,
        name="pair",
    )(step, twin)
    held_x, *row_map = chain("x", False, gather_panels(*pair, RING_X))
    held_y, plane_map = chain("y", True, gather_panels(*row_map, RING_Y))
    carried = jnp.zeros((8, W), F32)
    came = jnp.zeros((8, W), F32)
    for i in range(NZ - 1):
        carried, out = pl.pallas_call(
            plane_kernel,
            out_shape=[shape(8, W)] * 2,
            in_specs=[IN_VMEM] * 3,
            out_specs=[IN_VMEM] * 2,
            compiler_params=PARAMS,
            name="plane",
        )(plane_map, carried, came)
        came = lax.ppermute(out, "tm", [(t, t - 8) for t in range(64) if t // 8 == 7 - i and t % 2])
    carried = carried + came
    came = lax.ppermute(carried, "tm", [(t, t - 1) for t in range(64) if t % 2])
    sends = pl.pallas_call(
        down_kernel,
        out_shape=[shape(8, B)] * 2,
        in_specs=[IN_VMEM] * 6,
        out_specs=[IN_VMEM] * 2,
        scratch_shapes=[pltpu.VMEM((8, W), F32)],
        compiler_params=PARAMS,
        name="down",
    )(carried, came, step, twin, held_y, held_x)
    even, odd = (move(send, COLLECT[r])[0:2] for r, send in enumerate(sends))
    flip = lax.rem(lax.axis_index("state"), 2) == 1
    return jnp.concatenate([jnp.where(flip, odd, even), jnp.where(flip, even, odd)], axis=0)


def solution(mesh):
    return jax.shard_map(
        on_device,
        mesh=mesh,
        in_specs=(
            P("tm", "state", None),
            P("tm", "state", None),
            P("tm", "state", None, None),
            P("tm", None, None),
            P("tm", "state"),
            P("tm", "state"),
        ),
        out_specs=P("tm", "state"),
        check_vma=False,
    )
```

time: 142 us -> 128 us (0.901)
  starting transfers between devices: 57.7 us -> 43.1 us
  waiting for transfers between devices: 65.3 us -> 66.8 us
    ppermute x37 -> x20, starting transfers between devices: 52.4 us -> 36.6 us  [move(): return lax.ppermute(value, AXES, pairs)]
    ppermute x7 -> x8, starting transfers between devices: 5.26 us -> 6.54 us  [the longest x7 5.26 us: on_device(): lax.ppermute(out, 'tm', [(t, t - 8) for t in range(64) if t // 8 == 7 - i...]
    ppermute x37 -> x20, waiting for transfers between devices: 42.5 us -> 43.6 us  [move(): return lax.ppermute(value, AXES, pairs)]
    ppermute x7 -> x8, waiting for transfers between devices: 22.8 us -> 23.2 us  [the longest x7 22.4 us: on_device(): lax.ppermute(out, 'tm', [(t, t - 8) for t in range(64) if t // 8 == 7 - i...]
  transfers between devices with their start and end apart: 44 -> 28, of which waited for: 19 -> 15; matrix products, arithmetic and copies ran while one was open for 0% -> 0% of each run, Pallas kernels for 0% -> 0%
where the time goes in v3:
time: 128 us
  waiting for transfers between devices  66.8 us (52%)
  starting transfers between devices  43.1 us (34%)
  Pallas kernels  16.7 us (13%)
    ppermute x20, waiting for transfers between devices, move(): return lax.ppermute(value, AXES, pairs)  43.6 us
    ppermute x20, starting transfers between devices, move(): return lax.ppermute(value, AXES, pairs)  36.6 us
    ppermute x7, waiting for transfers between devices, on_device(): lax.ppermute(out, 'tm', [(t, t - 8) for t in range(64) if t // 8 == 7 - i...  22.4 us
    pallas_call x2, Pallas kernels, chain(): pl.pallas_call(kernel, out_shape=[shape(4, 2, PAN, W)] + ([shape(FULL, W)...  6.59 us
    ppermute x7, starting transfers between devices, on_device(): lax.ppermute(out, 'tm', [(t, t - 8) for t in range(64) if t // 8 == 7 - i...  5.26 us
    pallas_call x1, Pallas kernels, on_device(): pl.pallas_call(step_kernel, out_shape=shape(FULL, W), in_specs=[IN_VMEM]...  2.9 us
  transfers between devices with their start and end apart: 28, of which 15 were waited for; matrix products, arithmetic and copies ran while one was open for 0% of the time, Pallas kernels for 0%

profile of v3, /device:TPU:1, one launch (start us, length us, event | category | flops | bytes accessed | tf_op | source)
XLA Modules:
  0.0 127.5 jit_solution(15381541264700375658)
XLA Ops:
  0.0 2.0 %pack.1 = (f32[328,256]{1,0:T(8,128)S(1)}, f32[328,256]{1,0:T(8,128)S(1)}, f32[328,256]{1,0:T(8,128)S(1)}, f32[328,256]{1,0:T(8,128)S(1)}, f32[256,512]{1,0:T(8,128)S(1)}, /*index=5*/f32[256,512]{1,0:T(8,128)S(1)}) custom-call(f32[4,128,512]{2,1,0:T(8,128)} %p_ref.1, f32[4,128,512]{2,1,0:T(8,128)} %r_ref.1, f32[4,2,64,128]{3,2,1,0:T(8,128)} %t_ref.1, ...), custom_call_target="tpu_custom_call" | custom-call | tf_op jit(solution)/shard_map/pack/pallas_call | solution.py:313
  2.0 3.3 %collective-permute-start.4 = (f32[256,512]{1,0:T(8,128)S(1)}, f32[256,512]{1,0:T(8,128)S(1)}, u32[]{:S(2)}, u32[]{:S(2)}) collective-permute-start(f32[256,512]{1,0:T(8,128)S(1)} %get-tuple-element.39), channel_id=1, source_target_pairs={{0,4},{1,5},{2,6},{3,7},{4,0},{5,1},{6,2},{7,3},{8,12},{9,13},{10,... | collective-permute-start | bytes 1572872 | tf_op jit(solution)/shard_map/ppermute | solution.py:58
  5.4 1.9 %collective-permute-start = (f32[328,256]{1,0:T(8,128)S(1)}, f32[328,256]{1,0:T(8,128)S(1)}, u32[]{:S(2)}, u32[]{:S(2)}) collective-permute-start(f32[328,256]{1,0:T(8,128)S(1)} %get-tuple-element.34), channel_id=1, source_target_pairs={{0,0},{1,4},{2,2},{3,6},{4,1},{5,5},{6,3},{7,7},{8,8},{9,12},{10,1... | collective-permute-start | bytes 1007624 | tf_op jit(solution)/shard_map/ppermute | solution.py:58
  7.3 0.1 collective-permute-start.1
  7.4 1.7 %collective-permute-start.2 = (f32[328,256]{1,0:T(8,128)S(1)}, f32[328,256]{1,0:T(8,128)S(1)}, u32[]{:S(2)}, u32[]{:S(2)}) collective-permute-start(f32[328,256]{1,0:T(8,128)S(1)} %get-tuple-element.36), channel_id=1, source_target_pairs={{0,2},{1,6},{2,0},{3,4},{4,3},{5,7},{6,1},{7,5},{8,10},{9,14},{10,... | collective-permute-start | bytes 1007624 | tf_op jit(solution)/shard_map/ppermute | solution.py:58
  9.0 2.9 %collective-permute-start.3 = (f32[328,256]{1,0:T(8,128)S(1)}, f32[328,256]{1,0:T(8,128)S(1)}, u32[]{:S(2)}, u32[]{:S(2)}) collective-permute-start(f32[328,256]{1,0:T(8,128)S(1)} %get-tuple-element.37), channel_id=1, source_target_pairs={{0,6},{1,0},{2,4},{3,2},{4,7},{5,1},{6,5},{7,3},{8,14},{9,8},{10,1... | collective-permute-start | bytes 1007624 | tf_op jit(solution)/shard_map/ppermute | solution.py:58
  11.9 5.6 %collective-permute-done.pay0 = f32[328,256]{1,0:T(8,128)S(1)} collective-permute-done((f32[328,256]{1,0:T(8,128)S(1)}, f32[328,256]{1,0:T(8,128)S(1)}, u32[]{:S(2)}, u32[]{:S(2)}) %collective-permute-start) | collective-permute-done | bytes 335904 | tf_op jit(solution)/shard_map/ppermute | solution.py:58
  17.5 1.7 %collective-permute-done.1.pay1 = f32[328,256]{1,0:T(8,128)S(1)} collective-permute-done((f32[328,256]{1,0:T(8,128)S(1)}, f32[328,256]{1,0:T(8,128)S(1)}, u32[]{:S(2)}, u32[]{:S(2)}) %collective-permute-start.1) | collective-permute-done | bytes 335904 | tf_op jit(solution)/shard_map/ppermute | solution.py:58
  19.2 5.5 %collective-permute-done.2.pay2 = f32[328,256]{1,0:T(8,128)S(1)} collective-permute-done((f32[328,256]{1,0:T(8,128)S(1)}, f32[328,256]{1,0:T(8,128)S(1)}, u32[]{:S(2)}, u32[]{:S(2)}) %collective-permute-start.2) | collective-permute-done | bytes 335904 | tf_op jit(solution)/shard_map/ppermute | solution.py:58
  24.6 0.0 collective-permute-done.4.other_ref
  24.6 2.9 %step.1.own_ref = f32[520,512]{1,0:T(8,128)S(1)} custom-call(f32[328,256]{1,0:T(8,128)S(1)} %collective-permute-done.pay0, f32[328,256]{1,0:T(8,128)S(1)} %collective-permute-done.1.pay1, f32[328,256]{1,0:T(8,128)S(1)} %collective-permute-done.2.pay2, f32[328,256]{1,0:T(8,128)S(1)} %collective-permute-done.3.pay3, ...), custom_call_target="tpu_custom_call" | custom-call | tf_op jit(solution)/shard_map/step/pallas_call | solution.py:328
  27.5 0.5 collective-permute-start.5
  28.0 2.3 %collective-permute-done.5.other_ref = f32[520,512]{1,0:T(8,128)S(1)} collective-permute-done((f32[520,512]{1,0:T(8,128)S(1)}, f32[520,512]{1,0:T(8,128)S(1)}, u32[]{:S(2)}, u32[]{:S(2)}) %collective-permute-start.5) | collective-permute-done | bytes 1064992 | tf_op jit(solution)/shard_map/ppermute | solution.py:58
  30.3 1.0 pair.1
  31.3 2.4 %collective-permute-start.6 = (f32[264,512]{1,0:T(8,128)S(1)}, f32[264,512]{1,0:T(8,128)S(1)}, u32[]{:S(2)}, u32[]{:S(2)}) collective-permute-start(f32[264,512]{1,0:T(8,128)S(1)} %get-tuple-element.40.refs_0_), channel_id=1, source_target_pairs={{0,1},{1,2},{2,3},{3,0},{4,7},{5,4},{6,5},{7,6},{8,9},{9,10},{10,1... | collective-permute-start | bytes 1622024 | tf_op jit(solution)/shard_map/ppermute | solution.py:58
  33.8 0.1 collective-permute-start.7
  33.8 6.2 %collective-permute-done.6.refs_2_ = f32[264,512]{1,0:T(8,128)S(1)} collective-permute-done((f32[264,512]{1,0:T(8,128)S(1)}, f32[264,512]{1,0:T(8,128)S(1)}, u32[]{:S(2)}, u32[]{:S(2)}) %collective-permute-start.6) | collective-permute-done | bytes 540704 | tf_op jit(solution)/shard_map/ppermute | solution.py:58
  40.1 3.1 %collective-permute-start.10 = (f32[264,512]{1,0:T(8,128)S(1)}, f32[264,512]{1,0:T(8,128)S(1)}, u32[]{:S(2)}, u32[]{:S(2)}) collective-permute-start(f32[264,512]{1,0:T(8,128)S(1)} %collective-permute-done.6.refs_2_), channel_id=1, source_target_pairs={{0,1},{1,2},{2,3},{3,0},{4,7},{5,4},{6,5},{7,6},{8,9},{9,10},{10,1... | collective-permute-start | bytes 1622024 | tf_op jit(solution)/shard_map/ppermute | solution.py:58
  43.2 0.0 collective-permute-start.8
  43.2 2.7 %collective-permute-done.7.refs_3_ = f32[264,512]{1,0:T(8,128)S(1)} collective-permute-done((f32[264,512]{1,0:T(8,128)S(1)}, f32[264,512]{1,0:T(8,128)S(1)}, u32[]{:S(2)}, u32[]{:S(2)}) %collective-permute-start.7) | collective-permute-done | bytes 540704 | tf_op jit(solution)/shard_map/ppermute | solution.py:58
  45.8 2.3 %collective-permute-start.9 = (f32[264,512]{1,0:T(8,128)S(1)}, f32[264,512]{1,0:T(8,128)S(1)}, u32[]{:S(2)}, u32[]{:S(2)}) collective-permute-start(f32[264,512]{1,0:T(8,128)S(1)} %collective-permute-done.7.refs_3_), channel_id=1, source_target_pairs={{0,4},{1,5},{2,6},{3,7},{4,0},{5,1},{6,2},{7,3},{8,12},{9,13},{10,... | collective-permute-start | bytes 1622024 | tf_op jit(solution)/shard_map/ppermute | solution.py:58
  48.2 3.5 %collective-permute-done.10.refs_6_ = f32[264,512]{1,0:T(8,128)S(1)} collective-permute-done((f32[264,512]{1,0:T(8,128)S(1)}, f32[264,512]{1,0:T(8,128)S(1)}, u32[]{:S(2)}, u32[]{:S(2)}) %collective-permute-start.10) | collective-permute-done | bytes 540704 | tf_op jit(solution)/shard_map/ppermute | solution.py:58
  51.6 2.3 %collective-permute-start.11 = (f32[264,512]{1,0:T(8,128)S(1)}, f32[264,512]{1,0:T(8,128)S(1)}, u32[]{:S(2)}, u32[]{:S(2)}) collective-permute-start(f32[264,512]{1,0:T(8,128)S(1)} %collective-permute-done.10.refs_6_), channel_id=1, source_target_pairs={{0,4},{1,5},{2,6},{3,7},{4,0},{5,1},{6,2},{7,3},{8,12},{9,13},{10,... | collective-permute-start | bytes 1622024 | tf_op jit(solution)/shard_map/ppermute | solution.py:58
  54.0 1.6 %collective-permute-done.11.refs_7_ = f32[264,512]{1,0:T(8,128)S(1)} collective-permute-done((f32[264,512]{1,0:T(8,128)S(1)}, f32[264,512]{1,0:T(8,128)S(1)}, u32[]{:S(2)}, u32[]{:S(2)}) %collective-permute-start.11) | collective-permute-done | bytes 540704 | tf_op jit(solution)/shard_map/ppermute | solution.py:58
  55.5 3.3 %chain_x.1 = (f32[4,2,264,512]{3,2,1,0:T(8,128)S(1)}, f32[264,512]{1,0:T(8,128)S(1)}, f32[264,512]{1,0:T(8,128)S(1)}) custom-call(f32[264,512]{1,0:T(8,128)S(1)} %get-tuple-element.40.refs_0_, f32[264,512]{1,0:T(8,128)S(1)} %get-tuple-element.41.refs_1_, f32[264,512]{1,0:T(8,128)S(1)} %collective-permute-done.6.refs_2_, ...), custom_call_target="tpu_custom_call" | custom-call | tf_op jit(solution)/shard_map/chain_x/pallas_call | solution.py:296
  58.8 2.4 %collective-permute-start.12 = (f32[264,512]{1,0:T(8,128)S(1)}, f32[264,512]{1,0:T(8,128)S(1)}, u32[]{:S(2)}, u32[]{:S(2)}) collective-permute-start(f32[264,512]{1,0:T(8,128)S(1)} %get-tuple-element.42.refs_0_), channel_id=1, source_target_pairs={{0,8},{1,9},{2,10},{3,11},{4,28},{5,29},{6,30},{7,31},{8,16},{9,17... | collective-permute-start | bytes 1622024 | tf_op jit(solution)/shard_map/ppermute | solution.py:58
  61.3 0.5 collective-permute-start.13
  61.7 5.8 %collective-permute-done.12.refs_2_ = f32[264,512]{1,0:T(8,128)S(1)} collective-permute-done((f32[264,512]{1,0:T(8,128)S(1)}, f32[264,512]{1,0:T(8,128)S(1)}, u32[]{:S(2)}, u32[]{:S(2)}) %collective-permute-start.12) | collective-permute-done | bytes 540704 | tf_op jit(solution)/shard_map/ppermute | solution.py:58
  67.6 3.1 %collective-permute-start.16 = (f32[264,512]{1,0:T(8,128)S(1)}, f32[264,512]{1,0:T(8,128)S(1)}, u32[]{:S(2)}, u32[]{:S(2)}) collective-permute-start(f32[264,512]{1,0:T(8,128)S(1)} %collective-permute-done.12.refs_2_), channel_id=1, source_target_pairs={{0,8},{1,9},{2,10},{3,11},{4,28},{5,29},{6,30},{7,31},{8,16},{9,17... | collective-permute-start | bytes 1622024 | tf_op jit(solution)/shard_map/ppermute | solution.py:58
  70.7 0.0 collective-permute-start.14
  70.7 2.7 %collective-permute-done.13.refs_3_ = f32[264,512]{1,0:T(8,128)S(1)} collective-permute-done((f32[264,512]{1,0:T(8,128)S(1)}, f32[264,512]{1,0:T(8,128)S(1)}, u32[]{:S(2)}, u32[]{:S(2)}) %collective-permute-start.13) | collective-permute-done | bytes 540704 | tf_op jit(solution)/shard_map/ppermute | solution.py:58
  73.4 2.3 %collective-permute-start.15 = (f32[264,512]{1,0:T(8,128)S(1)}, f32[264,512]{1,0:T(8,128)S(1)}, u32[]{:S(2)}, u32[]{:S(2)}) collective-permute-start(f32[264,512]{1,0:T(8,128)S(1)} %collective-permute-done.13.refs_3_), channel_id=1, source_target_pairs={{0,4},{1,5},{2,6},{3,7},{4,0},{5,1},{6,2},{7,3},{8,12},{9,13},{10,... | collective-permute-start | bytes 1622024 | tf_op jit(solution)/shard_map/ppermute | solution.py:58
  75.6 3.5 %collective-permute-done.16.refs_6_ = f32[264,512]{1,0:T(8,128)S(1)} collective-permute-done((f32[264,512]{1,0:T(8,128)S(1)}, f32[264,512]{1,0:T(8,128)S(1)}, u32[]{:S(2)}, u32[]{:S(2)}) %collective-permute-start.16) | collective-permute-done | bytes 540704 | tf_op jit(solution)/shard_map/ppermute | solution.py:58
  79.2 2.3 %collective-permute-start.17 = (f32[264,512]{1,0:T(8,128)S(1)}, f32[264,512]{1,0:T(8,128)S(1)}, u32[]{:S(2)}, u32[]{:S(2)}) collective-permute-start(f32[264,512]{1,0:T(8,128)S(1)} %collective-permute-done.16.refs_6_), channel_id=1, source_target_pairs={{0,4},{1,5},{2,6},{3,7},{4,0},{5,1},{6,2},{7,3},{8,12},{9,13},{10,... | collective-permute-start | bytes 1622024 | tf_op jit(solution)/shard_map/ppermute | solution.py:58
  81.4 0.0 collective-permute-done.15.refs_5_
  81.4 1.6 %collective-permute-done.17.refs_7_ = f32[264,512]{1,0:T(8,128)S(1)} collective-permute-done((f32[264,512]{1,0:T(8,128)S(1)}, f32[264,512]{1,0:T(8,128)S(1)}, u32[]{:S(2)}, u32[]{:S(2)}) %collective-permute-start.17) | collective-permute-done | bytes 540704 | tf_op jit(solution)/shard_map/ppermute | solution.py:58
  83.0 3.3 %chain_y.1 = (f32[4,2,264,512]{3,2,1,0:T(8,128)S(1)}, f32[520,512]{1,0:T(8,128)S(1)}) custom-call(f32[264,512]{1,0:T(8,128)S(1)} %get-tuple-element.42.refs_0_, f32[264,512]{1,0:T(8,128)S(1)} %get-tuple-element.43.refs_1_, f32[264,512]{1,0:T(8,128)S(1)} %collective-permute-done.12.refs_2_, f32[264,512]{1,0:T(8,128)S(1)} %collective-permute-done.13.refs_3_, ...), custom_call_target="tpu_custom_call" | custom-call | tf_op jit(solution)/shard_map/chain_y/pallas_call | solution.py:296
  86.3 0.3 plane.7
  86.6 0.7 collective-permute-start.18
  87.2 0.0 collective-permute-done.18.came_ref
  87.2 0.3 plane.8
  87.5 0.7 collective-permute-start.19
  88.2 0.0 collective-permute-done.19.came_ref
  88.2 0.3 plane.9
  88.5 0.7 collective-permute-start.20
  89.1 0.3 plane.10
  89.4 0.7 collective-permute-start.21
  90.1 0.0 collective-permute-done.21.came_ref
  90.1 0.3 plane.11
  90.4 0.7 collective-permute-start.22
  91.0 0.0 collective-permute-done.22.came_ref
  91.0 0.3 plane.12
  91.3 0.7 collective-permute-start.23
  92.0 0.3 plane.13
  92.3 1.3 %collective-permute-start.24 = (f32[8,512]{1,0:T(8,128)S(1)}, f32[8,512]{1,0:T(8,128)S(1)}, u32[]{:S(2)}, u32[]{:S(2)}) collective-permute-start(f32[8,512]{1,0:T(8,128)S(1)} %get-tuple-element.58), channel_id=1, source_target_pairs={{36,4},{44,12},{52,20},{60,28},{37,5},{45,13},{53,21},{61,29},{38,... | collective-permute-start | bytes 49160 | tf_op jit(solution)/shard_map/ppermute | solution.py:359
  93.6 22.4 %collective-permute-done.24 = f32[8,512]{1,0:T(8,128)S(1)} collective-permute-done((f32[8,512]{1,0:T(8,128)S(1)}, f32[8,512]{1,0:T(8,128)S(1)}, u32[]{:S(2)}, u32[]{:S(2)}) %collective-permute-start.24) | collective-permute-done | bytes 16416 | tf_op jit(solution)/shard_map/ppermute | solution.py:359
  115.9 1.3 %collective-permute-start.25 = (f32[8,512]{1,0:T(8,128)S(1)}, f32[8,512]{1,0:T(8,128)S(1)}, u32[]{:S(2)}, u32[]{:S(2)}) collective-permute-start(f32[8,512]{1,0:T(8,128)S(1)} %add.3.carried_ref), channel_id=1, source_target_pairs={{4,0},{12,8},{20,16},{28,24},{36,32},{44,40},{52,48},{60,56},{68,6... | collective-permute-start | bytes 49160 | tf_op jit(solution)/shard_map/ppermute | solution.py:361
  117.2 0.8 collective-permute-done.25.came_ref
  118.1 2.3 %down.1 = (f32[8,128]{1,0:T(8,128)S(1)}, f32[8,128]{1,0:T(8,128)S(1)}) custom-call(f32[8,512]{1,0:T(8,128)S(1)} %add.3.carried_ref, f32[8,512]{1,0:T(8,128)S(1)} %collective-permute-done.25.came_ref, f32[520,512]{1,0:T(8,128)S(1)} %step.1.own_ref, f32[520,512]{1,0:T(8,128)S(1)} %collective-permute-done.5.other_ref, ...), custom_call_target="tpu_custom_call" | custom-call | tf_op jit(solution)/shard_map/down/pallas_call | solution.py:362
  120.4 1.6 %collective-permute-start.26 = (f32[8,128]{1,0:T(8,128)S(1)}, f32[8,128]{1,0:T(8,128)S(1)}, u32[]{:S(2)}, u32[]{:S(2)}) collective-permute-start(f32[8,128]{1,0:T(8,128)S(1)} %get-tuple-element.61), channel_id=1, source_target_pairs={{0,1},{1,5},{2,0},{3,4},{4,3},{5,7},{6,2},{7,6},{8,9},{9,13},{10,8... | collective-permute-start | bytes 12296 | tf_op jit(solution)/shard_map/ppermute | solution.py:58
  122.0 3.8 %collective-permute-start.27 = (f32[8,128]{1,0:T(8,128)S(1)}, f32[8,128]{1,0:T(8,128)S(1)}, u32[]{:S(2)}, u32[]{:S(2)}) collective-permute-start(f32[8,128]{1,0:T(8,128)S(1)} %get-tuple-element.62), channel_id=1, source_target_pairs={{0,0},{1,4},{2,1},{3,5},{4,2},{5,6},{6,3},{7,7},{8,8},{9,12},{10,9... | collective-permute-start | bytes 12296 | tf_op jit(solution)/shard_map/ppermute | solution.py:58
  125.9 0.0 collective-permute-done.26
  125.9 1.1 collective-permute-done.27
  126.9 0.6 pad_maximum_fusion
  (9 shorter events, 0.0 us)
Async XLA Ops:
  2.0 22.6 %collective-permute-start.4 = (f32[256,512]{1,0:T(8,128)S(1)}, f32[256,512]{1,0:T(8,128)S(1)}, u32[]{:S(2)}, u32[]{:S(2)}) collective-permute-start(f32[256,512]{1,0:T(8,128)S(1)} %get-tuple-element.39), channel_id=1, source_target_pairs={{0,4},{1,5},{2,6},{3,7},{4,0},{5,1},{6,2},{7,3},{8,12},{9,13},{10,... | collective-permute-start | bytes 1572872 | tf_op jit(solution)/shard_map/ppermute | solution.py:58
  5.4 12.1 %collective-permute-start = (f32[328,256]{1,0:T(8,128)S(1)}, f32[328,256]{1,0:T(8,128)S(1)}, u32[]{:S(2)}, u32[]{:S(2)}) collective-permute-start(f32[328,256]{1,0:T(8,128)S(1)} %get-tuple-element.34), channel_id=1, source_target_pairs={{0,0},{1,4},{2,2},{3,6},{4,1},{5,5},{6,3},{7,7},{8,8},{9,12},{10,1... | collective-permute-start | bytes 1007624 | tf_op jit(solution)/shard_map/ppermute | solution.py:58
  7.3 11.9 %collective-permute-start.1 = (f32[328,256]{1,0:T(8,128)S(1)}, f32[328,256]{1,0:T(8,128)S(1)}, u32[]{:S(2)}, u32[]{:S(2)}) collective-permute-start(f32[328,256]{1,0:T(8,128)S(1)} %get-tuple-element.35), channel_id=1, source_target_pairs={{0,4},{1,2},{2,6},{3,0},{4,5},{5,3},{6,7},{7,1},{8,12},{9,10},{10,... | collective-permute-start | bytes 1007624 | tf_op jit(solution)/shard_map/ppermute | solution.py:58
  7.4 17.3 %collective-permute-start.2 = (f32[328,256]{1,0:T(8,128)S(1)}, f32[328,256]{1,0:T(8,128)S(1)}, u32[]{:S(2)}, u32[]{:S(2)}) collective-permute-start(f32[328,256]{1,0:T(8,128)S(1)} %get-tuple-element.36), channel_id=1, source_target_pairs={{0,2},{1,6},{2,0},{3,4},{4,3},{5,7},{6,1},{7,5},{8,10},{9,14},{10,... | collective-permute-start | bytes 1007624 | tf_op jit(solution)/shard_map/ppermute | solution.py:58
  9.0 15.6 %collective-permute-start.3 = (f32[328,256]{1,0:T(8,128)S(1)}, f32[328,256]{1,0:T(8,128)S(1)}, u32[]{:S(2)}, u32[]{:S(2)}) collective-permute-start(f32[328,256]{1,0:T(8,128)S(1)} %get-tuple-element.37), channel_id=1, source_target_pairs={{0,6},{1,0},{2,4},{3,2},{4,7},{5,1},{6,5},{7,3},{8,14},{9,8},{10,1... | collective-permute-start | bytes 1007624 | tf_op jit(solution)/shard_map/ppermute | solution.py:58
  27.5 2.8 %collective-permute-start.5 = (f32[520,512]{1,0:T(8,128)S(1)}, f32[520,512]{1,0:T(8,128)S(1)}, u32[]{:S(2)}, u32[]{:S(2)}) collective-permute-start(f32[520,512]{1,0:T(8,128)S(1)} %step.1.own_ref), channel_id=1, source_target_pairs={{0,4},{1,5},{2,6},{3,7},{4,0},{5,1},{6,2},{7,3},{8,12},{9,13},{10,... | collective-permute-start | bytes 3194888 | tf_op jit(solution)/shard_map/ppermute | solution.py:58
  31.3 8.7 %collective-permute-start.6 = (f32[264,512]{1,0:T(8,128)S(1)}, f32[264,512]{1,0:T(8,128)S(1)}, u32[]{:S(2)}, u32[]{:S(2)}) collective-permute-start(f32[264,512]{1,0:T(8,128)S(1)} %get-tuple-element.40.refs_0_), channel_id=1, source_target_pairs={{0,1},{1,2},{2,3},{3,0},{4,7},{5,4},{6,5},{7,6},{8,9},{9,10},{10,1... | collective-permute-start | bytes 1622024 | tf_op jit(solution)/shard_map/ppermute | solution.py:58
  33.8 12.1 %collective-permute-start.7 = (f32[264,512]{1,0:T(8,128)S(1)}, f32[264,512]{1,0:T(8,128)S(1)}, u32[]{:S(2)}, u32[]{:S(2)}) collective-permute-start(f32[264,512]{1,0:T(8,128)S(1)} %get-tuple-element.41.refs_1_), channel_id=1, source_target_pairs={{0,1},{1,2},{2,3},{3,0},{4,7},{5,4},{6,5},{7,6},{8,9},{9,10},{10,1... | collective-permute-start | bytes 1622024 | tf_op jit(solution)/shard_map/ppermute | solution.py:58
  40.1 11.6 %collective-permute-start.10 = (f32[264,512]{1,0:T(8,128)S(1)}, f32[264,512]{1,0:T(8,128)S(1)}, u32[]{:S(2)}, u32[]{:S(2)}) collective-permute-start(f32[264,512]{1,0:T(8,128)S(1)} %collective-permute-done.6.refs_2_), channel_id=1, source_target_pairs={{0,1},{1,2},{2,3},{3,0},{4,7},{5,4},{6,5},{7,6},{8,9},{9,10},{10,1... | collective-permute-start | bytes 1622024 | tf_op jit(solution)/shard_map/ppermute | solution.py:58
  43.2 10.8 %collective-permute-start.8 = (f32[264,512]{1,0:T(8,128)S(1)}, f32[264,512]{1,0:T(8,128)S(1)}, u32[]{:S(2)}, u32[]{:S(2)}) collective-permute-start(f32[264,512]{1,0:T(8,128)S(1)} %collective-permute-done.6.refs_2_), channel_id=1, source_target_pairs={{0,4},{1,5},{2,6},{3,7},{4,0},{5,1},{6,2},{7,3},{8,12},{9,13},{10,... | collective-permute-start | bytes 1622024 | tf_op jit(solution)/shard_map/ppermute | solution.py:58
  45.8 8.1 %collective-permute-start.9 = (f32[264,512]{1,0:T(8,128)S(1)}, f32[264,512]{1,0:T(8,128)S(1)}, u32[]{:S(2)}, u32[]{:S(2)}) collective-permute-start(f32[264,512]{1,0:T(8,128)S(1)} %collective-permute-done.7.refs_3_), channel_id=1, source_target_pairs={{0,4},{1,5},{2,6},{3,7},{4,0},{5,1},{6,2},{7,3},{8,12},{9,13},{10,... | collective-permute-start | bytes 1622024 | tf_op jit(solution)/shard_map/ppermute | solution.py:58
  51.6 3.9 %collective-permute-start.11 = (f32[264,512]{1,0:T(8,128)S(1)}, f32[264,512]{1,0:T(8,128)S(1)}, u32[]{:S(2)}, u32[]{:S(2)}) collective-permute-start(f32[264,512]{1,0:T(8,128)S(1)} %collective-permute-done.10.refs_6_), channel_id=1, source_target_pairs={{0,4},{1,5},{2,6},{3,7},{4,0},{5,1},{6,2},{7,3},{8,12},{9,13},{10,... | collective-permute-start | bytes 1622024 | tf_op jit(solution)/shard_map/ppermute | solution.py:58
  58.8 8.7 %collective-permute-start.12 = (f32[264,512]{1,0:T(8,128)S(1)}, f32[264,512]{1,0:T(8,128)S(1)}, u32[]{:S(2)}, u32[]{:S(2)}) collective-permute-start(f32[264,512]{1,0:T(8,128)S(1)} %get-tuple-element.42.refs_0_), channel_id=1, source_target_pairs={{0,8},{1,9},{2,10},{3,11},{4,28},{5,29},{6,30},{7,31},{8,16},{9,17... | collective-permute-start | bytes 1622024 | tf_op jit(solution)/shard_map/ppermute | solution.py:58
  61.3 12.1 %collective-permute-start.13 = (f32[264,512]{1,0:T(8,128)S(1)}, f32[264,512]{1,0:T(8,128)S(1)}, u32[]{:S(2)}, u32[]{:S(2)}) collective-permute-start(f32[264,512]{1,0:T(8,128)S(1)} %get-tuple-element.43.refs_1_), channel_id=1, source_target_pairs={{0,8},{1,9},{2,10},{3,11},{4,28},{5,29},{6,30},{7,31},{8,16},{9,17... | collective-permute-start | bytes 1622024 | tf_op jit(solution)/shard_map/ppermute | solution.py:58
  67.6 11.6 %collective-permute-start.16 = (f32[264,512]{1,0:T(8,128)S(1)}, f32[264,512]{1,0:T(8,128)S(1)}, u32[]{:S(2)}, u32[]{:S(2)}) collective-permute-start(f32[264,512]{1,0:T(8,128)S(1)} %collective-permute-done.12.refs_2_), channel_id=1, source_target_pairs={{0,8},{1,9},{2,10},{3,11},{4,28},{5,29},{6,30},{7,31},{8,16},{9,17... | collective-permute-start | bytes 1622024 | tf_op jit(solution)/shard_map/ppermute | solution.py:58
  70.7 10.8 %collective-permute-start.14 = (f32[264,512]{1,0:T(8,128)S(1)}, f32[264,512]{1,0:T(8,128)S(1)}, u32[]{:S(2)}, u32[]{:S(2)}) collective-permute-start(f32[264,512]{1,0:T(8,128)S(1)} %collective-permute-done.12.refs_2_), channel_id=1, source_target_pairs={{0,4},{1,5},{2,6},{3,7},{4,0},{5,1},{6,2},{7,3},{8,12},{9,13},{10,... | collective-permute-start | bytes 1622024 | tf_op jit(solution)/shard_map/ppermute | solution.py:58
  73.4 8.1 %collective-permute-start.15 = (f32[264,512]{1,0:T(8,128)S(1)}, f32[264,512]{1,0:T(8,128)S(1)}, u32[]{:S(2)}, u32[]{:S(2)}) collective-permute-start(f32[264,512]{1,0:T(8,128)S(1)} %collective-permute-done.13.refs_3_), channel_id=1, source_target_pairs={{0,4},{1,5},{2,6},{3,7},{4,0},{5,1},{6,2},{7,3},{8,12},{9,13},{10,... | collective-permute-start | bytes 1622024 | tf_op jit(solution)/shard_map/ppermute | solution.py:58
  79.2 3.8 %collective-permute-start.17 = (f32[264,512]{1,0:T(8,128)S(1)}, f32[264,512]{1,0:T(8,128)S(1)}, u32[]{:S(2)}, u32[]{:S(2)}) collective-permute-start(f32[264,512]{1,0:T(8,128)S(1)} %collective-permute-done.16.refs_6_), channel_id=1, source_target_pairs={{0,4},{1,5},{2,6},{3,7},{4,0},{5,1},{6,2},{7,3},{8,12},{9,13},{10,... | collective-permute-start | bytes 1622024 | tf_op jit(solution)/shard_map/ppermute | solution.py:58
  86.6 0.7 collective-permute-start.18
  87.5 0.7 collective-permute-start.19
  88.5 0.7 collective-permute-start.20
  89.4 0.7 collective-permute-start.21
  90.4 0.7 collective-permute-start.22
  91.3 0.7 collective-permute-start.23
  92.3 23.7 %collective-permute-start.24 = (f32[8,512]{1,0:T(8,128)S(1)}, f32[8,512]{1,0:T(8,128)S(1)}, u32[]{:S(2)}, u32[]{:S(2)}) collective-permute-start(f32[8,512]{1,0:T(8,128)S(1)} %get-tuple-element.58), channel_id=1, source_target_pairs={{36,4},{44,12},{52,20},{60,28},{37,5},{45,13},{53,21},{61,29},{38,... | collective-permute-start | bytes 49160 | tf_op jit(solution)/shard_map/ppermute | solution.py:359
  115.9 2.1 %collective-permute-start.25 = (f32[8,512]{1,0:T(8,128)S(1)}, f32[8,512]{1,0:T(8,128)S(1)}, u32[]{:S(2)}, u32[]{:S(2)}) collective-permute-start(f32[8,512]{1,0:T(8,128)S(1)} %add.3.carried_ref), channel_id=1, source_target_pairs={{4,0},{12,8},{20,16},{28,24},{36,32},{44,40},{52,48},{60,56},{68,6... | collective-permute-start | bytes 49160 | tf_op jit(solution)/shard_map/ppermute | solution.py:361
  120.4 5.5 %collective-permute-start.26 = (f32[8,128]{1,0:T(8,128)S(1)}, f32[8,128]{1,0:T(8,128)S(1)}, u32[]{:S(2)}, u32[]{:S(2)}) collective-permute-start(f32[8,128]{1,0:T(8,128)S(1)} %get-tuple-element.61), channel_id=1, source_target_pairs={{0,1},{1,5},{2,0},{3,4},{4,3},{5,7},{6,2},{7,6},{8,9},{9,13},{10,8... | collective-permute-start | bytes 12296 | tf_op jit(solution)/shard_map/ppermute | solution.py:58
  122.0 4.9 %collective-permute-start.27 = (f32[8,128]{1,0:T(8,128)S(1)}, f32[8,128]{1,0:T(8,128)S(1)}, u32[]{:S(2)}, u32[]{:S(2)}) collective-permute-start(f32[8,128]{1,0:T(8,128)S(1)} %get-tuple-element.62), channel_id=1, source_target_pairs={{0,0},{1,4},{2,1},{3,5},{4,2},{5,6},{6,3},{7,7},{8,8},{9,12},{10,9... | collective-permute-start | bytes 12296 | tf_op jit(solution)/shard_map/ppermute | solution.py:58

commit v4 on v3

--- a/solution.py
+++ b/solution.py
@@ -225,13 +225,16 @@
 
 
 def chain_kernel(along, whole, *refs):
-    panels, held, outs, sems = refs[:8], refs[8], refs[9:-1], refs[-1]
+    panels, held, prefix, outs, sems = refs[:8], refs[8], refs[9], refs[10:-1], refs[-1]
     x, y, _, c = place()
     for copy in fetch(panels, held, sems, x if along == "x" else y, c, along == "x"):
         copy.wait()
     tail = held[3, 0, HALF:PAN, :]
     begin = 0 if whole else c
     rows = jnp.concatenate([held[3, begin, 0:HALF, :], held[3, 1 - begin, 0:HALF, :], tail], axis=0)
+
+    if whole:
+        prefix[2] = rows
     for t in (2, 1, 0):
         left = split(rows)
         top = split(held[t, 0, 0:HALF, :])
@@ -240,6 +243,12 @@
             (left[0][:, HALF:], left[1][:, HALF:]), bottom
         )
         rows = jnp.concatenate([value[0:W], value[W:] + held[t, 0, HALF:PAN, :]], axis=0)
+        if whole and t > 0:
+            prefix[t - 1] = rows
+        if not whole and t == 2:
+            prefix[pl.ds(pl.multiple_of(c * HALF, HALF), HALF), :] = rows[0:HALF]
+            prefix[pl.ds(pl.multiple_of((1 - c) * HALF, HALF), HALF), :] = rows[HALF:W]
+            prefix[W:FULL, :] = rows[W:FULL]
     if whole:
         outs[0][...] = rows
     else:
@@ -254,23 +263,44 @@
     out_ref[...] = rows_times(carried, map_ref[0:W, :]) + map_ref[W:FULL, :]
 
 
-def down_kernel(carried_ref, came_ref, own_ref, other_ref, held_y, held_x, send0, send1, values):
+def columns_kernel(own_ref, other_ref, after_ref, send0, send1):
+    x, _, _, c = place()
+
+    def cut(odd):
+        for r, send in enumerate((send0, send1)):
+            send[...] = odd[:, block(2 * c + lax.rem(x // 2 + r, 2))]
+
+    @pl.when(c == 0)
+    def _():
+        cut(other_ref)
+
+    @pl.when(c == 1)
+    def _():
+        cut(own_ref)
+
+
+def down_kernel(carried_ref, came_ref, cut0_ref, cut1_ref, rows_ref, pairs_ref, held_x, out_ref):
     x, y, _, c = place()
-    carried = carried_ref[...] + came_ref[...]
-    for held, index in ((held_y, y), (held_x, 2 * lax.rem(x, 2) + x // 2)):
-        for t in (3, 2, 1):
-            matrix = jnp.concatenate([held[t, 0, 0:HALF, :], held[t, 1, 0:HALF, :]], axis=0)
-            value = rows_times(carried, matrix) + held[t, 0, HALF:PAN, :]
-            carried = jnp.where(t > index, value, carried)
-    own_last = c == 1
-    late = jnp.where(own_last, own_ref[...], other_ref[...])
-    early = jnp.where(own_last, other_ref[...], own_ref[...])
-    after = rows_times(carried, late[0:W]) + late[W:FULL]
-    before = rows_times(after, early[0:W]) + early[W:FULL]
-    top = lax.broadcasted_iota(jnp.int32, (8, W), 0) == 0
-    values[...] = jnp.where(top, before, after)
-    for r, send in enumerate((send0, send1)):
-        send[...] = values[:, block(2 * c + lax.rem(x // 2 + r, 2))]
+
+    def apply(row8, ref):
+        return rows_times(row8, ref[0:W, :]) + ref[W:FULL, :]
+
+    def pair(row8, t, lanes):
+        matrix = jnp.concatenate([held_x[t, 0, 0:HALF, lanes], held_x[t, 1, 0:HALF, lanes]], axis=0)
+        return rows_times(row8, matrix) + held_x[t, 0, HALF:PAN, lanes]
+
+    def odd(row8, parity):
+        cut = jnp.where(lax.rem(x, 2) == parity, cut0_ref[...], cut1_ref[...])
+        return (rows_times(row8, cut[0:W]) + cut[W:FULL])[0:1]
+
+    late = carried_ref[...] + came_ref[...]
+    late = jnp.where(y == 3, late, apply(late, rows_ref.at[jnp.minimum(y, 2)]))
+    late = jnp.where(c == 1, late, apply(late, pairs_ref))
+    early = pair(late, 2 * c + 1, slice(None))
+    out_ref[3:4, :] = odd(late, 1)
+    out_ref[2:3, :] = pair(late, 2 * c + 1, block(x))[0:1]
+    out_ref[1:2, :] = odd(early, 0)
+    out_ref[0:1, :] = pair(early, 2 * c, block(x))[0:1]
 
 
 def shape(*dims):
@@ -283,10 +313,13 @@
 ANYWHERE = pl.BlockSpec(memory_space=pl.ANY)
 
 
-def gather_panels(first, second, ring):
+def gather_panels(first, second, ring, beside=None):
     one, two = move(first, ring), move(second, ring)
     far = move(one, ring)
-    return first, second, one, two, move(one, SWAP), move(two, SWAP), far, move(far, SWAP)
+    if beside is not None:
+        two, *beside = lax.optimization_barrier((two, *beside))
+    panels = first, second, one, two, move(one, SWAP), move(two, SWAP), far, move(far, SWAP)
+    return panels, beside
 
 
 def chain(along, whole, panels):
@@ -295,10 +328,10 @@
 
     return pl.pallas_call(
         kernel,
-        out_shape=[shape(4, 2, PAN, W)]
+        out_shape=[shape(4, 2, PAN, W), shape(3, FULL, W) if whole else shape(FULL, W)]
         + ([shape(FULL, W)] if whole else [shape(PAN, W)] * 2),
         in_specs=[ANYWHERE] * 8,
-        out_specs=[IN_VMEM] * (2 if whole else 3),
+        out_specs=[IN_VMEM] * (3 if whole else 4),
         scratch_shapes=[pltpu.SemaphoreType.DMA((8,))],
         compiler_params=PARAMS,
         name="chain_" + along,
@@ -343,8 +376,18 @@
         compiler_params=PARAMS,
         name="pair",
     )(step, twin)
-    held_x, *row_map = chain("x", False, gather_panels(*pair, RING_X))
-    held_y, plane_map = chain("y", True, gather_panels(*row_map, RING_Y))
+    held_x, pairs_map, *row_map = chain("x", False, gather_panels(*pair, RING_X)[0])
+    cuts = pl.pallas_call(
+        columns_kernel,
+        out_shape=[shape(FULL, B)] * 2,
+        in_specs=[IN_VMEM] * 2 + [ANYWHERE],
+        out_specs=[IN_VMEM] * 2,
+        compiler_params=PARAMS,
+        name="columns",
+    )(step, twin, row_map[0])
+    cuts = [move(cut, COLLECT[r]) for r, cut in enumerate(cuts)]
+    panels_y, cuts = gather_panels(*row_map, RING_Y, cuts)
+    _, rows_map, plane_map = chain("y", True, panels_y)
     carried = jnp.zeros((8, W), F32)
     came = jnp.zeros((8, W), F32)
     for i in range(NZ - 1):
@@ -359,18 +402,14 @@
         came = lax.ppermute(out, "tm", [(t, t - 8) for t in range(64) if t // 8 == 7 - i and t % 2])
     carried = carried + came
     came = lax.ppermute(carried, "tm", [(t, t - 1) for t in range(64) if t % 2])
-    sends = pl.pallas_call(
+    return pl.pallas_call(
         down_kernel,
-        out_shape=[shape(8, B)] * 2,
-        in_specs=[IN_VMEM] * 6,
-        out_specs=[IN_VMEM] * 2,
-        scratch_shapes=[pltpu.VMEM((8, W), F32)],
+        out_shape=shape(4, B),
+        in_specs=[IN_VMEM] * 7,
+        out_specs=IN_VMEM,
         compiler_params=PARAMS,
         name="down",
-    )(carried, came, step, twin, held_y, held_x)
-    even, odd = (move(send, COLLECT[r])[0:2] for r, send in enumerate(sends))
-    flip = lax.rem(lax.axis_index("state"), 2) == 1
-    return jnp.concatenate([jnp.where(flip, odd, even), jnp.where(flip, even, odd)], axis=0)
+    )(carried, came, *cuts, rows_map, pairs_map, held_x)
 
 
 def solution(mesh):

time: 128 us -> 122 us (0.953)
  starting transfers between devices: 43.1 us -> 37.5 us
  waiting for transfers between devices: 66.8 us -> 68.4 us
    ppermute x20, starting transfers between devices: 36.6 us -> 31 us  [move(): return lax.ppermute(value, AXES, pairs)]
    pallas_call x3 -> x4, Pallas kernels: 8.92 us -> 8.29 us  [the longest x2 6.62 us: chain(): pl.pallas_call(kernel, out_shape=[shape(4, 2, PAN, W), shape(3, FULL, W)...]
  transfers between devices with their start and end apart: 28 -> 28, of which waited for: 15 -> 16; matrix products, arithmetic and copies ran while one was open for 0% -> 0% of each run, Pallas kernels for 0% -> 0%
where the time goes in v4:
time: 122 us
  waiting for transfers between devices  68.4 us (56%)
  starting transfers between devices  37.5 us (31%)
  Pallas kernels  16.1 us (13%)
    ppermute x20, waiting for transfers between devices, move(): return lax.ppermute(value, AXES, pairs)  44.8 us
    ppermute x20, starting transfers between devices, move(): return lax.ppermute(value, AXES, pairs)  31 us
    ppermute x7, waiting for transfers between devices, on_device(): lax.ppermute(out, 'tm', [(t, t - 8) for t in range(64) if t // 8 == 7 - i...  22.8 us
    pallas_call x2, Pallas kernels, chain(): pl.pallas_call(kernel, out_shape=[shape(4, 2, PAN, W), shape(3, FULL, W)...  6.62 us
    ppermute x7, starting transfers between devices, on_device(): lax.ppermute(out, 'tm', [(t, t - 8) for t in range(64) if t // 8 == 7 - i...  5.26 us
    pallas_call x1, Pallas kernels, on_device(): pl.pallas_call(step_kernel, out_shape=shape(FULL, W), in_specs=[IN_VMEM]...  2.9 us
  transfers between devices with their start and end apart: 28, of which 16 were waited for; matrix products, arithmetic and copies ran while one was open for 0% of the time, Pallas kernels for 0%

profile of v4, /device:TPU:1, one launch (start us, length us, event | category | flops | bytes accessed | tf_op | source)
XLA Modules:
  0.0 122.2 jit_solution(1941177242231472078)
XLA Ops:
  0.0 2.0 %pack.1 = (f32[328,256]{1,0:T(8,128)S(1)}, f32[328,256]{1,0:T(8,128)S(1)}, f32[328,256]{1,0:T(8,128)S(1)}, f32[328,256]{1,0:T(8,128)S(1)}, f32[256,512]{1,0:T(8,128)S(1)}, /*index=5*/f32[256,512]{1,0:T(8,128)S(1)}) custom-call(f32[4,128,512]{2,1,0:T(8,128)} %p_ref.1, f32[4,128,512]{2,1,0:T(8,128)} %r_ref.1, f32[4,2,64,128]{3,2,1,0:T(8,128)} %t_ref.1, ...), custom_call_target="tpu_custom_call" | custom-call | tf_op jit(solution)/shard_map/pack/pallas_call | solution.py:346
  2.0 3.3 %collective-permute-start.4 = (f32[256,512]{1,0:T(8,128)S(1)}, f32[256,512]{1,0:T(8,128)S(1)}, u32[]{:S(2)}, u32[]{:S(2)}) collective-permute-start(f32[256,512]{1,0:T(8,128)S(1)} %get-tuple-element.43), channel_id=1, source_target_pairs={{0,4},{1,5},{2,6},{3,7},{4,0},{5,1},{6,2},{7,3},{8,12},{9,13},{10,... | collective-permute-start | bytes 1572872 | tf_op jit(solution)/shard_map/ppermute | solution.py:58
  5.4 1.9 %collective-permute-start = (f32[328,256]{1,0:T(8,128)S(1)}, f32[328,256]{1,0:T(8,128)S(1)}, u32[]{:S(2)}, u32[]{:S(2)}) collective-permute-start(f32[328,256]{1,0:T(8,128)S(1)} %get-tuple-element.38), channel_id=1, source_target_pairs={{0,0},{1,4},{2,2},{3,6},{4,1},{5,5},{6,3},{7,7},{8,8},{9,12},{10,1... | collective-permute-start | bytes 1007624 | tf_op jit(solution)/shard_map/ppermute | solution.py:58
  7.3 0.1 collective-permute-start.1
  7.4 1.7 %collective-permute-start.2 = (f32[328,256]{1,0:T(8,128)S(1)}, f32[328,256]{1,0:T(8,128)S(1)}, u32[]{:S(2)}, u32[]{:S(2)}) collective-permute-start(f32[328,256]{1,0:T(8,128)S(1)} %get-tuple-element.40), channel_id=1, source_target_pairs={{0,2},{1,6},{2,0},{3,4},{4,3},{5,7},{6,1},{7,5},{8,10},{9,14},{10,... | collective-permute-start | bytes 1007624 | tf_op jit(solution)/shard_map/ppermute | solution.py:58
  9.0 2.9 %collective-permute-start.3 = (f32[328,256]{1,0:T(8,128)S(1)}, f32[328,256]{1,0:T(8,128)S(1)}, u32[]{:S(2)}, u32[]{:S(2)}) collective-permute-start(f32[328,256]{1,0:T(8,128)S(1)} %get-tuple-element.41), channel_id=1, source_target_pairs={{0,6},{1,0},{2,4},{3,2},{4,7},{5,1},{6,5},{7,3},{8,14},{9,8},{10,1... | collective-permute-start | bytes 1007624 | tf_op jit(solution)/shard_map/ppermute | solution.py:58
  11.9 5.6 %collective-permute-done.pay0 = f32[328,256]{1,0:T(8,128)S(1)} collective-permute-done((f32[328,256]{1,0:T(8,128)S(1)}, f32[328,256]{1,0:T(8,128)S(1)}, u32[]{:S(2)}, u32[]{:S(2)}) %collective-permute-start) | collective-permute-done | bytes 335904 | tf_op jit(solution)/shard_map/ppermute | solution.py:58
  17.5 1.7 %collective-permute-done.1.pay1 = f32[328,256]{1,0:T(8,128)S(1)} collective-permute-done((f32[328,256]{1,0:T(8,128)S(1)}, f32[328,256]{1,0:T(8,128)S(1)}, u32[]{:S(2)}, u32[]{:S(2)}) %collective-permute-start.1) | collective-permute-done | bytes 335904 | tf_op jit(solution)/shard_map/ppermute | solution.py:58
  19.2 5.5 %collective-permute-done.2.pay2 = f32[328,256]{1,0:T(8,128)S(1)} collective-permute-done((f32[328,256]{1,0:T(8,128)S(1)}, f32[328,256]{1,0:T(8,128)S(1)}, u32[]{:S(2)}, u32[]{:S(2)}) %collective-permute-start.2) | collective-permute-done | bytes 335904 | tf_op jit(solution)/shard_map/ppermute | solution.py:58
  24.6 0.0 collective-permute-done.3.pay3
  24.6 0.0 collective-permute-done.4.other_ref
  24.6 2.9 %step.1.own_ref = f32[520,512]{1,0:T(8,128)S(1)} custom-call(f32[328,256]{1,0:T(8,128)S(1)} %collective-permute-done.pay0, f32[328,256]{1,0:T(8,128)S(1)} %collective-permute-done.1.pay1, f32[328,256]{1,0:T(8,128)S(1)} %collective-permute-done.2.pay2, f32[328,256]{1,0:T(8,128)S(1)} %collective-permute-done.3.pay3, ...), custom_call_target="tpu_custom_call" | custom-call | tf_op jit(solution)/shard_map/step/pallas_call | solution.py:361
  27.5 0.5 collective-permute-start.5
  28.0 2.3 %collective-permute-done.5.other_ref = f32[520,512]{1,0:T(8,128)S(1)} collective-permute-done((f32[520,512]{1,0:T(8,128)S(1)}, f32[520,512]{1,0:T(8,128)S(1)}, u32[]{:S(2)}, u32[]{:S(2)}) %collective-permute-start.5) | collective-permute-done | bytes 1064992 | tf_op jit(solution)/shard_map/ppermute | solution.py:58
  30.3 1.0 pair.1
  31.3 2.4 %collective-permute-start.6 = (f32[264,512]{1,0:T(8,128)S(1)}, f32[264,512]{1,0:T(8,128)S(1)}, u32[]{:S(2)}, u32[]{:S(2)}) collective-permute-start(f32[264,512]{1,0:T(8,128)S(1)} %get-tuple-element.44.refs_0_), channel_id=1, source_target_pairs={{0,1},{1,2},{2,3},{3,0},{4,7},{5,4},{6,5},{7,6},{8,9},{9,10},{10,1... | collective-permute-start | bytes 1622024 | tf_op jit(solution)/shard_map/ppermute | solution.py:58
  33.7 0.1 collective-permute-start.7
  33.8 6.2 %collective-permute-done.6.refs_2_ = f32[264,512]{1,0:T(8,128)S(1)} collective-permute-done((f32[264,512]{1,0:T(8,128)S(1)}, f32[264,512]{1,0:T(8,128)S(1)}, u32[]{:S(2)}, u32[]{:S(2)}) %collective-permute-start.6) | collective-permute-done | bytes 540704 | tf_op jit(solution)/shard_map/ppermute | solution.py:58
  40.0 3.1 %collective-permute-start.10 = (f32[264,512]{1,0:T(8,128)S(1)}, f32[264,512]{1,0:T(8,128)S(1)}, u32[]{:S(2)}, u32[]{:S(2)}) collective-permute-start(f32[264,512]{1,0:T(8,128)S(1)} %collective-permute-done.6.refs_2_), channel_id=1, source_target_pairs={{0,1},{1,2},{2,3},{3,0},{4,7},{5,4},{6,5},{7,6},{8,9},{9,10},{10,1... | collective-permute-start | bytes 1622024 | tf_op jit(solution)/shard_map/ppermute | solution.py:58
  43.2 0.0 collective-permute-start.8
  43.2 2.7 %collective-permute-done.7.refs_3_ = f32[264,512]{1,0:T(8,128)S(1)} collective-permute-done((f32[264,512]{1,0:T(8,128)S(1)}, f32[264,512]{1,0:T(8,128)S(1)}, u32[]{:S(2)}, u32[]{:S(2)}) %collective-permute-start.7) | collective-permute-done | bytes 540704 | tf_op jit(solution)/shard_map/ppermute | solution.py:58
  45.8 2.3 %collective-permute-start.9 = (f32[264,512]{1,0:T(8,128)S(1)}, f32[264,512]{1,0:T(8,128)S(1)}, u32[]{:S(2)}, u32[]{:S(2)}) collective-permute-start(f32[264,512]{1,0:T(8,128)S(1)} %collective-permute-done.7.refs_3_), channel_id=1, source_target_pairs={{0,4},{1,5},{2,6},{3,7},{4,0},{5,1},{6,2},{7,3},{8,12},{9,13},{10,... | collective-permute-start | bytes 1622024 | tf_op jit(solution)/shard_map/ppermute | solution.py:58
  48.1 3.5 %collective-permute-done.10.refs_6_ = f32[264,512]{1,0:T(8,128)S(1)} collective-permute-done((f32[264,512]{1,0:T(8,128)S(1)}, f32[264,512]{1,0:T(8,128)S(1)}, u32[]{:S(2)}, u32[]{:S(2)}) %collective-permute-start.10) | collective-permute-done | bytes 540704 | tf_op jit(solution)/shard_map/ppermute | solution.py:58
  51.6 2.3 %collective-permute-start.11 = (f32[264,512]{1,0:T(8,128)S(1)}, f32[264,512]{1,0:T(8,128)S(1)}, u32[]{:S(2)}, u32[]{:S(2)}) collective-permute-start(f32[264,512]{1,0:T(8,128)S(1)} %collective-permute-done.10.refs_6_), channel_id=1, source_target_pairs={{0,4},{1,5},{2,6},{3,7},{4,0},{5,1},{6,2},{7,3},{8,12},{9,13},{10,... | collective-permute-start | bytes 1622024 | tf_op jit(solution)/shard_map/ppermute | solution.py:58
  53.9 0.0 collective-permute-done.8.refs_4_
  53.9 1.6 %collective-permute-done.11.refs_7_ = f32[264,512]{1,0:T(8,128)S(1)} collective-permute-done((f32[264,512]{1,0:T(8,128)S(1)}, f32[264,512]{1,0:T(8,128)S(1)}, u32[]{:S(2)}, u32[]{:S(2)}) %collective-permute-start.11) | collective-permute-done | bytes 540704 | tf_op jit(solution)/shard_map/ppermute | solution.py:58
  55.5 3.3 %chain_x.1 = (f32[4,2,264,512]{3,2,1,0:T(8,128)S(1)}, f32[520,512]{1,0:T(8,128)S(1)}, f32[264,512]{1,0:T(8,128)S(1)}, f32[264,512]{1,0:T(8,128)S(1)}) custom-call(f32[264,512]{1,0:T(8,128)S(1)} %get-tuple-element.44.refs_0_, f32[264,512]{1,0:T(8,128)S(1)} %get-tuple-element.45.refs_1_, f32[264,512]{1,0:T(8,128)S(1)} %collective-permute-done.6.refs_2_, ...), custom_call_target="tpu_custom_call" | custom-call | tf_op jit(solution)/shard_map/chain_x/pallas_call | solution.py:329
  58.8 2.4 %collective-permute-start.12 = (f32[264,512]{1,0:T(8,128)S(1)}, f32[264,512]{1,0:T(8,128)S(1)}, u32[]{:S(2)}, u32[]{:S(2)}) collective-permute-start(f32[264,512]{1,0:T(8,128)S(1)} %get-tuple-element.46.after_ref.refs_0_), channel_id=1, source_target_pairs={{0,8},{1,9},{2,10},{3,11},{4,28},{5,29},{6,30},{7,31},{8,16},{9,17... | collective-permute-start | bytes 1622024 | tf_op jit(solution)/shard_map/ppermute | solution.py:58
  61.3 0.5 collective-permute-start.13
  61.7 5.8 %collective-permute-done.12.refs_2_ = f32[264,512]{1,0:T(8,128)S(1)} collective-permute-done((f32[264,512]{1,0:T(8,128)S(1)}, f32[264,512]{1,0:T(8,128)S(1)}, u32[]{:S(2)}, u32[]{:S(2)}) %collective-permute-start.12) | collective-permute-done | bytes 540704 | tf_op jit(solution)/shard_map/ppermute | solution.py:58
  67.6 3.1 %collective-permute-start.18 = (f32[264,512]{1,0:T(8,128)S(1)}, f32[264,512]{1,0:T(8,128)S(1)}, u32[]{:S(2)}, u32[]{:S(2)}) collective-permute-start(f32[264,512]{1,0:T(8,128)S(1)} %collective-permute-done.12.refs_2_), channel_id=1, source_target_pairs={{0,8},{1,9},{2,10},{3,11},{4,28},{5,29},{6,30},{7,31},{8,16},{9,17... | collective-permute-start | bytes 1622024 | tf_op jit(solution)/shard_map/ppermute | solution.py:58
  70.7 0.1 columns.1
  70.7 1.9 %collective-permute-start.14 = (f32[520,128]{1,0:T(8,128)S(1)}, f32[520,128]{1,0:T(8,128)S(1)}, u32[]{:S(2)}, u32[]{:S(2)}) collective-permute-start(f32[520,128]{1,0:T(8,128)S(1)} %get-tuple-element.48), channel_id=1, source_target_pairs={{0,0},{1,4},{2,1},{3,5},{4,2},{5,6},{6,3},{7,7},{8,8},{9,12},{10,9... | collective-permute-start | bytes 798728 | tf_op jit(solution)/shard_map/ppermute | solution.py:58
  72.7 2.0 %collective-permute-start.15 = (f32[520,128]{1,0:T(8,128)S(1)}, f32[520,128]{1,0:T(8,128)S(1)}, u32[]{:S(2)}, u32[]{:S(2)}) collective-permute-start(f32[520,128]{1,0:T(8,128)S(1)} %get-tuple-element.49), channel_id=1, source_target_pairs={{0,1},{1,5},{2,0},{3,4},{4,3},{5,7},{6,2},{7,6},{8,9},{9,13},{10,8... | collective-permute-start | bytes 798728 | tf_op jit(solution)/shard_map/ppermute | solution.py:58
  74.7 5.9 %collective-permute-done.14.cut0_ref = f32[520,128]{1,0:T(8,128)S(1)} collective-permute-done((f32[520,128]{1,0:T(8,128)S(1)}, f32[520,128]{1,0:T(8,128)S(1)}, u32[]{:S(2)}, u32[]{:S(2)}) %collective-permute-start.14) | collective-permute-done | bytes 266272 | tf_op jit(solution)/shard_map/ppermute | solution.py:58
  80.6 1.1 collective-permute-done.15.cut1_ref
  81.7 0.5 collective-permute-start.16
  82.2 0.0 collective-permute-done.18.refs_6_
  82.2 0.0 collective-permute-start.19
  82.2 1.4 %collective-permute-done.17.refs_5_ = f32[264,512]{1,0:T(8,128)S(1)} collective-permute-done((f32[264,512]{1,0:T(8,128)S(1)}, f32[264,512]{1,0:T(8,128)S(1)}, u32[]{:S(2)}, u32[]{:S(2)}) %collective-permute-start.17) | collective-permute-done | bytes 540704 | tf_op jit(solution)/shard_map/ppermute | solution.py:58
  83.6 0.8 collective-permute-done.16.refs_4_
  84.4 0.8 collective-permute-done.19.refs_7_
  85.2 3.3 %chain_y.1 = (f32[4,2,264,512]{3,2,1,0:T(8,128)}, f32[3,520,512]{2,1,0:T(8,128)S(1)}, f32[520,512]{1,0:T(8,128)S(1)}) custom-call(f32[264,512]{1,0:T(8,128)S(1)} %get-tuple-element.46.after_ref.refs_0_, f32[264,512]{1,0:T(8,128)S(1)} %get-tuple-element.47.refs_1_, f32[264,512]{1,0:T(8,128)S(1)} %collective-permute-done.12.refs_2_, ...), custom_call_target="tpu_custom_call" | custom-call | tf_op jit(solution)/shard_map/chain_y/pallas_call | solution.py:329
  88.5 0.3 plane.7
  88.8 0.7 collective-permute-start.20
  89.5 0.3 plane.8
  89.7 0.7 collective-permute-start.21
  90.4 0.0 collective-permute-done.21.came_ref
  90.4 0.3 plane.9
  90.7 0.7 collective-permute-start.22
  91.3 0.0 collective-permute-done.22.came_ref
  91.4 0.3 plane.10
  91.6 0.7 collective-permute-start.23
  92.3 0.3 plane.11
  92.6 0.7 collective-permute-start.24
  93.3 0.3 plane.12
  93.5 0.7 collective-permute-start.25
  94.2 0.0 collective-permute-done.25.came_ref
  94.2 0.3 plane.13
  94.5 1.3 %collective-permute-start.26 = (f32[8,512]{1,0:T(8,128)S(1)}, f32[8,512]{1,0:T(8,128)S(1)}, u32[]{:S(2)}, u32[]{:S(2)}) collective-permute-start(f32[8,512]{1,0:T(8,128)S(1)} %get-tuple-element.65), channel_id=1, source_target_pairs={{36,4},{44,12},{52,20},{60,28},{37,5},{45,13},{53,21},{61,29},{38,... | collective-permute-start | bytes 49160 | tf_op jit(solution)/shard_map/ppermute | solution.py:402
  95.8 22.7 %collective-permute-done.26 = f32[8,512]{1,0:T(8,128)S(1)} collective-permute-done((f32[8,512]{1,0:T(8,128)S(1)}, f32[8,512]{1,0:T(8,128)S(1)}, u32[]{:S(2)}, u32[]{:S(2)}) %collective-permute-start.26) | collective-permute-done | bytes 16416 | tf_op jit(solution)/shard_map/ppermute | solution.py:402
  118.5 1.3 %collective-permute-start.27 = (f32[8,512]{1,0:T(8,128)S(1)}, f32[8,512]{1,0:T(8,128)S(1)}, u32[]{:S(2)}, u32[]{:S(2)}) collective-permute-start(f32[8,512]{1,0:T(8,128)S(1)} %add.3.carried_ref), channel_id=1, source_target_pairs={{4,0},{12,8},{20,16},{28,24},{36,32},{44,40},{52,48},{60,56},{68,6... | collective-permute-start | bytes 49160 | tf_op jit(solution)/shard_map/ppermute | solution.py:404
  119.8 0.8 collective-permute-done.27.came_ref
  120.6 1.6 %down.1 = f32[4,128]{1,0:T(4,128)} custom-call(f32[8,512]{1,0:T(8,128)S(1)} %add.3.carried_ref, f32[8,512]{1,0:T(8,128)S(1)} %collective-permute-done.27.came_ref, f32[520,128]{1,0:T(8,128)S(1)} %collective-permute-done.14.cut0_ref, f32[520,128]{1,0:T(8,128)S(1)} %collective-permute-done.15.cut1_ref, f32[3,520,512]{2,1,0:T(8,128)S(1)} %get-tuple-element.68.rows_ref, ...), custom_call_target="tpu_custom_call" | custom-call | tf_op jit(solution)/shard_map/down/pallas_call | solution.py:405
  (8 shorter events, 0.0 us)
Async XLA Ops:
  2.0 22.6 %collective-permute-start.4 = (f32[256,512]{1,0:T(8,128)S(1)}, f32[256,512]{1,0:T(8,128)S(1)}, u32[]{:S(2)}, u32[]{:S(2)}) collective-permute-start(f32[256,512]{1,0:T(8,128)S(1)} %get-tuple-element.43), channel_id=1, source_target_pairs={{0,4},{1,5},{2,6},{3,7},{4,0},{5,1},{6,2},{7,3},{8,12},{9,13},{10,... | collective-permute-start | bytes 1572872 | tf_op jit(solution)/shard_map/ppermute | solution.py:58
  5.4 12.1 %collective-permute-start = (f32[328,256]{1,0:T(8,128)S(1)}, f32[328,256]{1,0:T(8,128)S(1)}, u32[]{:S(2)}, u32[]{:S(2)}) collective-permute-start(f32[328,256]{1,0:T(8,128)S(1)} %get-tuple-element.38), channel_id=1, source_target_pairs={{0,0},{1,4},{2,2},{3,6},{4,1},{5,5},{6,3},{7,7},{8,8},{9,12},{10,1... | collective-permute-start | bytes 1007624 | tf_op jit(solution)/shard_map/ppermute | solution.py:58
  7.3 11.9 %collective-permute-start.1 = (f32[328,256]{1,0:T(8,128)S(1)}, f32[328,256]{1,0:T(8,128)S(1)}, u32[]{:S(2)}, u32[]{:S(2)}) collective-permute-start(f32[328,256]{1,0:T(8,128)S(1)} %get-tuple-element.39), channel_id=1, source_target_pairs={{0,4},{1,2},{2,6},{3,0},{4,5},{5,3},{6,7},{7,1},{8,12},{9,10},{10,... | collective-permute-start | bytes 1007624 | tf_op jit(solution)/shard_map/ppermute | solution.py:58
  7.4 17.3 %collective-permute-start.2 = (f32[328,256]{1,0:T(8,128)S(1)}, f32[328,256]{1,0:T(8,128)S(1)}, u32[]{:S(2)}, u32[]{:S(2)}) collective-permute-start(f32[328,256]{1,0:T(8,128)S(1)} %get-tuple-element.40), channel_id=1, source_target_pairs={{0,2},{1,6},{2,0},{3,4},{4,3},{5,7},{6,1},{7,5},{8,10},{9,14},{10,... | collective-permute-start | bytes 1007624 | tf_op jit(solution)/shard_map/ppermute | solution.py:58
  9.0 15.6 %collective-permute-start.3 = (f32[328,256]{1,0:T(8,128)S(1)}, f32[328,256]{1,0:T(8,128)S(1)}, u32[]{:S(2)}, u32[]{:S(2)}) collective-permute-start(f32[328,256]{1,0:T(8,128)S(1)} %get-tuple-element.41), channel_id=1, source_target_pairs={{0,6},{1,0},{2,4},{3,2},{4,7},{5,1},{6,5},{7,3},{8,14},{9,8},{10,1... | collective-permute-start | bytes 1007624 | tf_op jit(solution)/shard_map/ppermute | solution.py:58
  27.5 2.8 %collective-permute-start.5 = (f32[520,512]{1,0:T(8,128)S(1)}, f32[520,512]{1,0:T(8,128)S(1)}, u32[]{:S(2)}, u32[]{:S(2)}) collective-permute-start(f32[520,512]{1,0:T(8,128)S(1)} %step.1.own_ref), channel_id=1, source_target_pairs={{0,4},{1,5},{2,6},{3,7},{4,0},{5,1},{6,2},{7,3},{8,12},{9,13},{10,... | collective-permute-start | bytes 3194888 | tf_op jit(solution)/shard_map/ppermute | solution.py:58
  31.3 8.7 %collective-permute-start.6 = (f32[264,512]{1,0:T(8,128)S(1)}, f32[264,512]{1,0:T(8,128)S(1)}, u32[]{:S(2)}, u32[]{:S(2)}) collective-permute-start(f32[264,512]{1,0:T(8,128)S(1)} %get-tuple-element.44.refs_0_), channel_id=1, source_target_pairs={{0,1},{1,2},{2,3},{3,0},{4,7},{5,4},{6,5},{7,6},{8,9},{9,10},{10,1... | collective-permute-start | bytes 1622024 | tf_op jit(solution)/shard_map/ppermute | solution.py:58
  33.7 12.1 %collective-permute-start.7 = (f32[264,512]{1,0:T(8,128)S(1)}, f32[264,512]{1,0:T(8,128)S(1)}, u32[]{:S(2)}, u32[]{:S(2)}) collective-permute-start(f32[264,512]{1,0:T(8,128)S(1)} %get-tuple-element.45.refs_1_), channel_id=1, source_target_pairs={{0,1},{1,2},{2,3},{3,0},{4,7},{5,4},{6,5},{7,6},{8,9},{9,10},{10,1... | collective-permute-start | bytes 1622024 | tf_op jit(solution)/shard_map/ppermute | solution.py:58
  40.0 11.6 %collective-permute-start.10 = (f32[264,512]{1,0:T(8,128)S(1)}, f32[264,512]{1,0:T(8,128)S(1)}, u32[]{:S(2)}, u32[]{:S(2)}) collective-permute-start(f32[264,512]{1,0:T(8,128)S(1)} %collective-permute-done.6.refs_2_), channel_id=1, source_target_pairs={{0,1},{1,2},{2,3},{3,0},{4,7},{5,4},{6,5},{7,6},{8,9},{9,10},{10,1... | collective-permute-start | bytes 1622024 | tf_op jit(solution)/shard_map/ppermute | solution.py:58
  43.2 10.8 %collective-permute-start.8 = (f32[264,512]{1,0:T(8,128)S(1)}, f32[264,512]{1,0:T(8,128)S(1)}, u32[]{:S(2)}, u32[]{:S(2)}) collective-permute-start(f32[264,512]{1,0:T(8,128)S(1)} %collective-permute-done.6.refs_2_), channel_id=1, source_target_pairs={{0,4},{1,5},{2,6},{3,7},{4,0},{5,1},{6,2},{7,3},{8,12},{9,13},{10,... | collective-permute-start | bytes 1622024 | tf_op jit(solution)/shard_map/ppermute | solution.py:58
  45.8 8.1 %collective-permute-start.9 = (f32[264,512]{1,0:T(8,128)S(1)}, f32[264,512]{1,0:T(8,128)S(1)}, u32[]{:S(2)}, u32[]{:S(2)}) collective-permute-start(f32[264,512]{1,0:T(8,128)S(1)} %collective-permute-done.7.refs_3_), channel_id=1, source_target_pairs={{0,4},{1,5},{2,6},{3,7},{4,0},{5,1},{6,2},{7,3},{8,12},{9,13},{10,... | collective-permute-start | bytes 1622024 | tf_op jit(solution)/shard_map/ppermute | solution.py:58
  51.6 3.9 %collective-permute-start.11 = (f32[264,512]{1,0:T(8,128)S(1)}, f32[264,512]{1,0:T(8,128)S(1)}, u32[]{:S(2)}, u32[]{:S(2)}) collective-permute-start(f32[264,512]{1,0:T(8,128)S(1)} %collective-permute-done.10.refs_6_), channel_id=1, source_target_pairs={{0,4},{1,5},{2,6},{3,7},{4,0},{5,1},{6,2},{7,3},{8,12},{9,13},{10,... | collective-permute-start | bytes 1622024 | tf_op jit(solution)/shard_map/ppermute | solution.py:58
  58.8 8.7 %collective-permute-start.12 = (f32[264,512]{1,0:T(8,128)S(1)}, f32[264,512]{1,0:T(8,128)S(1)}, u32[]{:S(2)}, u32[]{:S(2)}) collective-permute-start(f32[264,512]{1,0:T(8,128)S(1)} %get-tuple-element.46.after_ref.refs_0_), channel_id=1, source_target_pairs={{0,8},{1,9},{2,10},{3,11},{4,28},{5,29},{6,30},{7,31},{8,16},{9,17... | collective-permute-start | bytes 1622024 | tf_op jit(solution)/shard_map/ppermute | solution.py:58
  61.3 20.4 %collective-permute-start.13 = (f32[264,512]{1,0:T(8,128)S(1)}, f32[264,512]{1,0:T(8,128)S(1)}, u32[]{:S(2)}, u32[]{:S(2)}) collective-permute-start(f32[264,512]{1,0:T(8,128)S(1)} %get-tuple-element.47.refs_1_), channel_id=1, source_target_pairs={{0,8},{1,9},{2,10},{3,11},{4,28},{5,29},{6,30},{7,31},{8,16},{9,17... | collective-permute-start | bytes 1622024 | tf_op jit(solution)/shard_map/ppermute | solution.py:58
  67.6 14.6 %collective-permute-start.18 = (f32[264,512]{1,0:T(8,128)S(1)}, f32[264,512]{1,0:T(8,128)S(1)}, u32[]{:S(2)}, u32[]{:S(2)}) collective-permute-start(f32[264,512]{1,0:T(8,128)S(1)} %collective-permute-done.12.refs_2_), channel_id=1, source_target_pairs={{0,8},{1,9},{2,10},{3,11},{4,28},{5,29},{6,30},{7,31},{8,16},{9,17... | collective-permute-start | bytes 1622024 | tf_op jit(solution)/shard_map/ppermute | solution.py:58
  70.7 9.8 %collective-permute-start.14 = (f32[520,128]{1,0:T(8,128)S(1)}, f32[520,128]{1,0:T(8,128)S(1)}, u32[]{:S(2)}, u32[]{:S(2)}) collective-permute-start(f32[520,128]{1,0:T(8,128)S(1)} %get-tuple-element.48), channel_id=1, source_target_pairs={{0,0},{1,4},{2,1},{3,5},{4,2},{5,6},{6,3},{7,7},{8,8},{9,12},{10,9... | collective-permute-start | bytes 798728 | tf_op jit(solution)/shard_map/ppermute | solution.py:58
  72.7 9.0 %collective-permute-start.15 = (f32[520,128]{1,0:T(8,128)S(1)}, f32[520,128]{1,0:T(8,128)S(1)}, u32[]{:S(2)}, u32[]{:S(2)}) collective-permute-start(f32[520,128]{1,0:T(8,128)S(1)} %get-tuple-element.49), channel_id=1, source_target_pairs={{0,1},{1,5},{2,0},{3,4},{4,3},{5,7},{6,2},{7,6},{8,9},{9,13},{10,8... | collective-permute-start | bytes 798728 | tf_op jit(solution)/shard_map/ppermute | solution.py:58
  81.7 1.9 %collective-permute-start.17 = (f32[264,512]{1,0:T(8,128)S(1)}, f32[264,512]{1,0:T(8,128)S(1)}, u32[]{:S(2)}, u32[]{:S(2)}) collective-permute-start(f32[264,512]{1,0:T(8,128)S(1)} %collective-permute-done.13.refs_3_), channel_id=1, source_target_pairs={{0,4},{1,5},{2,6},{3,7},{4,0},{5,1},{6,2},{7,3},{8,12},{9,13},{10,... | collective-permute-start | bytes 1622024 | tf_op jit(solution)/shard_map/ppermute | solution.py:58
  81.7 2.7 %collective-permute-start.16 = (f32[264,512]{1,0:T(8,128)S(1)}, f32[264,512]{1,0:T(8,128)S(1)}, u32[]{:S(2)}, u32[]{:S(2)}) collective-permute-start(f32[264,512]{1,0:T(8,128)S(1)} %collective-permute-done.12.refs_2_), channel_id=1, source_target_pairs={{0,4},{1,5},{2,6},{3,7},{4,0},{5,1},{6,2},{7,3},{8,12},{9,13},{10,... | collective-permute-start | bytes 1622024 | tf_op jit(solution)/shard_map/ppermute | solution.py:58
  82.2 3.0 %collective-permute-start.19 = (f32[264,512]{1,0:T(8,128)S(1)}, f32[264,512]{1,0:T(8,128)S(1)}, u32[]{:S(2)}, u32[]{:S(2)}) collective-permute-start(f32[264,512]{1,0:T(8,128)S(1)} %collective-permute-done.18.refs_6_), channel_id=1, source_target_pairs={{0,4},{1,5},{2,6},{3,7},{4,0},{5,1},{6,2},{7,3},{8,12},{9,13},{10,... | collective-permute-start | bytes 1622024 | tf_op jit(solution)/shard_map/ppermute | solution.py:58
  88.8 0.7 collective-permute-start.20
  89.7 0.7 collective-permute-start.21
  90.7 0.7 collective-permute-start.22
  91.6 0.7 collective-permute-start.23
  92.6 0.7 collective-permute-start.24
  93.5 0.7 collective-permute-start.25
  94.5 24.0 %collective-permute-start.26 = (f32[8,512]{1,0:T(8,128)S(1)}, f32[8,512]{1,0:T(8,128)S(1)}, u32[]{:S(2)}, u32[]{:S(2)}) collective-permute-start(f32[8,512]{1,0:T(8,128)S(1)} %get-tuple-element.65), channel_id=1, source_target_pairs={{36,4},{44,12},{52,20},{60,28},{37,5},{45,13},{53,21},{61,29},{38,... | collective-permute-start | bytes 49160 | tf_op jit(solution)/shard_map/ppermute | solution.py:402
  118.5 2.1 %collective-permute-start.27 = (f32[8,512]{1,0:T(8,128)S(1)}, f32[8,512]{1,0:T(8,128)S(1)}, u32[]{:S(2)}, u32[]{:S(2)}) collective-permute-start(f32[8,512]{1,0:T(8,128)S(1)} %add.3.carried_ref), channel_id=1, source_target_pairs={{4,0},{12,8},{20,16},{28,24},{36,32},{44,40},{52,48},{60,56},{68,6... | collective-permute-start | bytes 49160 | tf_op jit(solution)/shard_map/ppermute | solution.py:404

commit v5 on v4

--- a/solution.py
+++ b/solution.py
@@ -224,11 +224,30 @@
     return copies
 
 
+def lead_kernel(*refs):
+    panels, held, lead_ref, sems = refs[:8], refs[8], refs[9], refs[10]
+    _, y, _, c = place()
+    for copy in fetch(panels, held, sems, y, c, False):
+        copy.wait()
+    row8 = held[3, 0, HALF:PAN, :]
+    for t in (2, 1, 0):
+        row8 = (
+            rows_times(row8[:, 0:HALF], held[t, 0, 0:HALF, :])
+            + rows_times(row8[:, HALF:W], held[t, 1, 0:HALF, :])
+            + held[t, 0, HALF:PAN, :]
+        )
+    lead_ref[...] = row8
+
+
 def chain_kernel(along, whole, *refs):
-    panels, held, prefix, outs, sems = refs[:8], refs[8], refs[9], refs[10:-1], refs[-1]
+    if whole:
+        held, prefix, outs = refs[0], refs[1], refs[2:]
+    else:
+        panels, held, prefix, outs, sems = refs[:8], refs[8], refs[9], refs[10:-1], refs[-1]
     x, y, _, c = place()
-    for copy in fetch(panels, held, sems, x if along == "x" else y, c, along == "x"):
-        copy.wait()
+    if not whole:
+        for copy in fetch(panels, held, sems, x, c, True):
+            copy.wait()
     tail = held[3, 0, HALF:PAN, :]
     begin = 0 if whole else c
     rows = jnp.concatenate([held[3, begin, 0:HALF, :], held[3, 1 - begin, 0:HALF, :], tail], axis=0)
@@ -322,20 +341,34 @@
     return panels, beside
 
 
-def chain(along, whole, panels):
+def lead(panels):
+    return pl.pallas_call(
+        lead_kernel,
+        out_shape=[shape(4, 2, PAN, W), shape(8, W)],
+        in_specs=[ANYWHERE] * 8,
+        out_specs=[IN_VMEM] * 2,
+        scratch_shapes=[pltpu.SemaphoreType.DMA((8,))],
+        compiler_params=PARAMS,
+        name="lead",
+    )(*panels)
+
+
+def chain(along, whole, operands):
     def kernel(*refs):
         chain_kernel(along, whole, *refs)
 
+    outs = [shape(4, 2, PAN, W), shape(FULL, W)] + [shape(PAN, W)] * 2
+    if whole:
+        outs = [shape(3, FULL, W), shape(FULL, W)]
     return pl.pallas_call(
         kernel,
-        out_shape=[shape(4, 2, PAN, W), shape(3, FULL, W) if whole else shape(FULL, W)]
-        + ([shape(FULL, W)] if whole else [shape(PAN, W)] * 2),
-        in_specs=[ANYWHERE] * 8,
-        out_specs=[IN_VMEM] * (3 if whole else 4),
-        scratch_shapes=[pltpu.SemaphoreType.DMA((8,))],
+        out_shape=outs,
+        in_specs=[IN_VMEM] if whole else [ANYWHERE] * 8,
+        out_specs=[IN_VMEM] * len(outs),
+        scratch_shapes=[] if whole else [pltpu.SemaphoreType.DMA((8,))],
         compiler_params=PARAMS,
         name="chain_" + along,
-    )(*panels)
+    )(*operands)
 
 
 def in_hbm(value):
@@ -387,18 +420,20 @@
     )(step, twin, row_map[0])
     cuts = [move(cut, COLLECT[r]) for r, cut in enumerate(cuts)]
     panels_y, cuts = gather_panels(*row_map, RING_Y, cuts)
-    _, rows_map, plane_map = chain("y", True, panels_y)
+    held_y, out = lead(panels_y)
+    rows_map, plane_map = chain("y", True, [held_y])
     carried = jnp.zeros((8, W), F32)
     came = jnp.zeros((8, W), F32)
     for i in range(NZ - 1):
-        carried, out = pl.pallas_call(
-            plane_kernel,
-            out_shape=[shape(8, W)] * 2,
-            in_specs=[IN_VMEM] * 3,
-            out_specs=[IN_VMEM] * 2,
-            compiler_params=PARAMS,
-            name="plane",
-        )(plane_map, carried, came)
+        if i > 0:
+            carried, out = pl.pallas_call(
+                plane_kernel,
+                out_shape=[shape(8, W)] * 2,
+                in_specs=[IN_VMEM] * 3,
+                out_specs=[IN_VMEM] * 2,
+                compiler_params=PARAMS,
+                name="plane",
+            )(plane_map, carried, came)
         came = lax.ppermute(out, "tm", [(t, t - 8) for t in range(64) if t // 8 == 7 - i and t % 2])
     carried = carried + came
     came = lax.ppermute(carried, "tm", [(t, t - 1) for t in range(64) if t % 2])

time: 122 us -> 120 us (0.984)
  waiting for transfers between devices: 68.4 us -> 65.9 us
    ppermute x7, waiting for transfers between devices: 22.8 us -> 20.3 us  [on_device(): lax.ppermute(out, 'tm', [(t, t - 8) for t in range(64) if t // 8 == 7 - i...]
    pallas_call x2 -> x3, Pallas kernels: 6.62 us -> 7.37 us  [the longest x2 6.07 us: chain(): pl.pallas_call(kernel, out_shape=outs, in_specs=[IN_VMEM] if whole else [...]
  transfers between devices with their start and end apart: 28 -> 28, of which waited for: 16 -> 16; matrix products, arithmetic and copies ran while one was open for 0% -> 0% of each run, Pallas kernels for 0% -> 2%
where the time goes in v5:
time: 120 us
  waiting for transfers between devices  65.9 us (55%)
  starting transfers between devices  37.5 us (31%)
  Pallas kernels  16.6 us (14%)
    ppermute x20, waiting for transfers between devices, move(): return lax.ppermute(value, AXES, pairs)  44.8 us
    ppermute x20, starting transfers between devices, move(): return lax.ppermute(value, AXES, pairs)  31 us
    ppermute x7, waiting for transfers between devices, on_device(): lax.ppermute(out, 'tm', [(t, t - 8) for t in range(64) if t // 8 == 7 - i...  20.3 us
    pallas_call x2, Pallas kernels, chain(): pl.pallas_call(kernel, out_shape=outs, in_specs=[IN_VMEM] if whole else [...  6.07 us
    ppermute x7, starting transfers between devices, on_device(): lax.ppermute(out, 'tm', [(t, t - 8) for t in range(64) if t // 8 == 7 - i...  5.26 us
    pallas_call x1, Pallas kernels, on_device(): pl.pallas_call(step_kernel, out_shape=shape(FULL, W), in_specs=[IN_VMEM]...  2.9 us
  transfers between devices with their start and end apart: 28, of which 16 were waited for; matrix products, arithmetic and copies ran while one was open for 0% of the time, Pallas kernels for 2%

profile of v5, /device:TPU:1, one launch (start us, length us, event | category | flops | bytes accessed | tf_op | source)
XLA Modules:
  0.0 120.2 jit_solution(5226373950242973185)
XLA Ops:
  0.0 2.0 %pack.1 = (f32[328,256]{1,0:T(8,128)S(1)}, f32[328,256]{1,0:T(8,128)S(1)}, f32[328,256]{1,0:T(8,128)S(1)}, f32[328,256]{1,0:T(8,128)S(1)}, f32[256,512]{1,0:T(8,128)S(1)}, /*index=5*/f32[256,512]{1,0:T(8,128)S(1)}) custom-call(f32[4,128,512]{2,1,0:T(8,128)} %p_ref.1, f32[4,128,512]{2,1,0:T(8,128)} %r_ref.1, f32[4,2,64,128]{3,2,1,0:T(8,128)} %t_ref.1, ...), custom_call_target="tpu_custom_call" | custom-call | tf_op jit(solution)/shard_map/pack/pallas_call | solution.py:379
  2.0 3.3 %collective-permute-start.4 = (f32[256,512]{1,0:T(8,128)S(1)}, f32[256,512]{1,0:T(8,128)S(1)}, u32[]{:S(2)}, u32[]{:S(2)}) collective-permute-start(f32[256,512]{1,0:T(8,128)S(1)} %get-tuple-element.43), channel_id=1, source_target_pairs={{0,4},{1,5},{2,6},{3,7},{4,0},{5,1},{6,2},{7,3},{8,12},{9,13},{10,... | collective-permute-start | bytes 1572872 | tf_op jit(solution)/shard_map/ppermute | solution.py:58
  5.4 1.9 %collective-permute-start = (f32[328,256]{1,0:T(8,128)S(1)}, f32[328,256]{1,0:T(8,128)S(1)}, u32[]{:S(2)}, u32[]{:S(2)}) collective-permute-start(f32[328,256]{1,0:T(8,128)S(1)} %get-tuple-element.38), channel_id=1, source_target_pairs={{0,0},{1,4},{2,2},{3,6},{4,1},{5,5},{6,3},{7,7},{8,8},{9,12},{10,1... | collective-permute-start | bytes 1007624 | tf_op jit(solution)/shard_map/ppermute | solution.py:58
  7.3 0.1 collective-permute-start.1
  7.4 1.7 %collective-permute-start.2 = (f32[328,256]{1,0:T(8,128)S(1)}, f32[328,256]{1,0:T(8,128)S(1)}, u32[]{:S(2)}, u32[]{:S(2)}) collective-permute-start(f32[328,256]{1,0:T(8,128)S(1)} %get-tuple-element.40), channel_id=1, source_target_pairs={{0,2},{1,6},{2,0},{3,4},{4,3},{5,7},{6,1},{7,5},{8,10},{9,14},{10,... | collective-permute-start | bytes 1007624 | tf_op jit(solution)/shard_map/ppermute | solution.py:58
  9.0 2.9 %collective-permute-start.3 = (f32[328,256]{1,0:T(8,128)S(1)}, f32[328,256]{1,0:T(8,128)S(1)}, u32[]{:S(2)}, u32[]{:S(2)}) collective-permute-start(f32[328,256]{1,0:T(8,128)S(1)} %get-tuple-element.41), channel_id=1, source_target_pairs={{0,6},{1,0},{2,4},{3,2},{4,7},{5,1},{6,5},{7,3},{8,14},{9,8},{10,1... | collective-permute-start | bytes 1007624 | tf_op jit(solution)/shard_map/ppermute | solution.py:58
  11.9 5.6 %collective-permute-done.pay0 = f32[328,256]{1,0:T(8,128)S(1)} collective-permute-done((f32[328,256]{1,0:T(8,128)S(1)}, f32[328,256]{1,0:T(8,128)S(1)}, u32[]{:S(2)}, u32[]{:S(2)}) %collective-permute-start) | collective-permute-done | bytes 335904 | tf_op jit(solution)/shard_map/ppermute | solution.py:58
  17.5 1.7 %collective-permute-done.1.pay1 = f32[328,256]{1,0:T(8,128)S(1)} collective-permute-done((f32[328,256]{1,0:T(8,128)S(1)}, f32[328,256]{1,0:T(8,128)S(1)}, u32[]{:S(2)}, u32[]{:S(2)}) %collective-permute-start.1) | collective-permute-done | bytes 335904 | tf_op jit(solution)/shard_map/ppermute | solution.py:58
  19.2 5.5 %collective-permute-done.2.pay2 = f32[328,256]{1,0:T(8,128)S(1)} collective-permute-done((f32[328,256]{1,0:T(8,128)S(1)}, f32[328,256]{1,0:T(8,128)S(1)}, u32[]{:S(2)}, u32[]{:S(2)}) %collective-permute-start.2) | collective-permute-done | bytes 335904 | tf_op jit(solution)/shard_map/ppermute | solution.py:58
  24.6 0.0 collective-permute-done.3.pay3
  24.6 0.0 collective-permute-done.4.other_ref
  24.6 2.9 %step.1.own_ref = f32[520,512]{1,0:T(8,128)S(1)} custom-call(f32[328,256]{1,0:T(8,128)S(1)} %collective-permute-done.pay0, f32[328,256]{1,0:T(8,128)S(1)} %collective-permute-done.1.pay1, f32[328,256]{1,0:T(8,128)S(1)} %collective-permute-done.2.pay2, f32[328,256]{1,0:T(8,128)S(1)} %collective-permute-done.3.pay3, ...), custom_call_target="tpu_custom_call" | custom-call | tf_op jit(solution)/shard_map/step/pallas_call | solution.py:394
  27.5 0.5 collective-permute-start.5
  28.0 2.3 %collective-permute-done.5.other_ref = f32[520,512]{1,0:T(8,128)S(1)} collective-permute-done((f32[520,512]{1,0:T(8,128)S(1)}, f32[520,512]{1,0:T(8,128)S(1)}, u32[]{:S(2)}, u32[]{:S(2)}) %collective-permute-start.5) | collective-permute-done | bytes 1064992 | tf_op jit(solution)/shard_map/ppermute | solution.py:58
  30.3 1.0 pair.1
  31.3 2.4 %collective-permute-start.6 = (f32[264,512]{1,0:T(8,128)S(1)}, f32[264,512]{1,0:T(8,128)S(1)}, u32[]{:S(2)}, u32[]{:S(2)}) collective-permute-start(f32[264,512]{1,0:T(8,128)S(1)} %get-tuple-element.44.refs_0_), channel_id=1, source_target_pairs={{0,1},{1,2},{2,3},{3,0},{4,7},{5,4},{6,5},{7,6},{8,9},{9,10},{10,1... | collective-permute-start | bytes 1622024 | tf_op jit(solution)/shard_map/ppermute | solution.py:58
  33.7 0.1 collective-permute-start.7
  33.8 6.2 %collective-permute-done.6.refs_2_ = f32[264,512]{1,0:T(8,128)S(1)} collective-permute-done((f32[264,512]{1,0:T(8,128)S(1)}, f32[264,512]{1,0:T(8,128)S(1)}, u32[]{:S(2)}, u32[]{:S(2)}) %collective-permute-start.6) | collective-permute-done | bytes 540704 | tf_op jit(solution)/shard_map/ppermute | solution.py:58
  40.0 3.1 %collective-permute-start.10 = (f32[264,512]{1,0:T(8,128)S(1)}, f32[264,512]{1,0:T(8,128)S(1)}, u32[]{:S(2)}, u32[]{:S(2)}) collective-permute-start(f32[264,512]{1,0:T(8,128)S(1)} %collective-permute-done.6.refs_2_), channel_id=1, source_target_pairs={{0,1},{1,2},{2,3},{3,0},{4,7},{5,4},{6,5},{7,6},{8,9},{9,10},{10,1... | collective-permute-start | bytes 1622024 | tf_op jit(solution)/shard_map/ppermute | solution.py:58
  43.2 0.0 collective-permute-start.8
  43.2 2.7 %collective-permute-done.7.refs_3_ = f32[264,512]{1,0:T(8,128)S(1)} collective-permute-done((f32[264,512]{1,0:T(8,128)S(1)}, f32[264,512]{1,0:T(8,128)S(1)}, u32[]{:S(2)}, u32[]{:S(2)}) %collective-permute-start.7) | collective-permute-done | bytes 540704 | tf_op jit(solution)/shard_map/ppermute | solution.py:58
  45.8 2.3 %collective-permute-start.9 = (f32[264,512]{1,0:T(8,128)S(1)}, f32[264,512]{1,0:T(8,128)S(1)}, u32[]{:S(2)}, u32[]{:S(2)}) collective-permute-start(f32[264,512]{1,0:T(8,128)S(1)} %collective-permute-done.7.refs_3_), channel_id=1, source_target_pairs={{0,4},{1,5},{2,6},{3,7},{4,0},{5,1},{6,2},{7,3},{8,12},{9,13},{10,... | collective-permute-start | bytes 1622024 | tf_op jit(solution)/shard_map/ppermute | solution.py:58
  48.1 3.5 %collective-permute-done.10.refs_6_ = f32[264,512]{1,0:T(8,128)S(1)} collective-permute-done((f32[264,512]{1,0:T(8,128)S(1)}, f32[264,512]{1,0:T(8,128)S(1)}, u32[]{:S(2)}, u32[]{:S(2)}) %collective-permute-start.10) | collective-permute-done | bytes 540704 | tf_op jit(solution)/shard_map/ppermute | solution.py:58
  51.6 2.3 %collective-permute-start.11 = (f32[264,512]{1,0:T(8,128)S(1)}, f32[264,512]{1,0:T(8,128)S(1)}, u32[]{:S(2)}, u32[]{:S(2)}) collective-permute-start(f32[264,512]{1,0:T(8,128)S(1)} %collective-permute-done.10.refs_6_), channel_id=1, source_target_pairs={{0,4},{1,5},{2,6},{3,7},{4,0},{5,1},{6,2},{7,3},{8,12},{9,13},{10,... | collective-permute-start | bytes 1622024 | tf_op jit(solution)/shard_map/ppermute | solution.py:58
  53.9 0.0 collective-permute-done.9.refs_5_
  53.9 1.6 %collective-permute-done.11.refs_7_ = f32[264,512]{1,0:T(8,128)S(1)} collective-permute-done((f32[264,512]{1,0:T(8,128)S(1)}, f32[264,512]{1,0:T(8,128)S(1)}, u32[]{:S(2)}, u32[]{:S(2)}) %collective-permute-start.11) | collective-permute-done | bytes 540704 | tf_op jit(solution)/shard_map/ppermute | solution.py:58
  55.5 3.3 %chain_x.1 = (f32[4,2,264,512]{3,2,1,0:T(8,128)S(1)}, f32[520,512]{1,0:T(8,128)S(1)}, f32[264,512]{1,0:T(8,128)S(1)}, f32[264,512]{1,0:T(8,128)S(1)}) custom-call(f32[264,512]{1,0:T(8,128)S(1)} %get-tuple-element.44.refs_0_, f32[264,512]{1,0:T(8,128)S(1)} %get-tuple-element.45.refs_1_, f32[264,512]{1,0:T(8,128)S(1)} %collective-permute-done.6.refs_2_, ...), custom_call_target="tpu_custom_call" | custom-call | tf_op jit(solution)/shard_map/chain_x/pallas_call | solution.py:363
  58.8 2.4 %collective-permute-start.12 = (f32[264,512]{1,0:T(8,128)S(1)}, f32[264,512]{1,0:T(8,128)S(1)}, u32[]{:S(2)}, u32[]{:S(2)}) collective-permute-start(f32[264,512]{1,0:T(8,128)S(1)} %get-tuple-element.46.after_ref.refs_0_), channel_id=1, source_target_pairs={{0,8},{1,9},{2,10},{3,11},{4,28},{5,29},{6,30},{7,31},{8,16},{9,17... | collective-permute-start | bytes 1622024 | tf_op jit(solution)/shard_map/ppermute | solution.py:58
  61.3 0.5 collective-permute-start.13
  61.7 5.8 %collective-permute-done.12.refs_2_ = f32[264,512]{1,0:T(8,128)S(1)} collective-permute-done((f32[264,512]{1,0:T(8,128)S(1)}, f32[264,512]{1,0:T(8,128)S(1)}, u32[]{:S(2)}, u32[]{:S(2)}) %collective-permute-start.12) | collective-permute-done | bytes 540704 | tf_op jit(solution)/shard_map/ppermute | solution.py:58
  67.6 3.1 %collective-permute-start.18 = (f32[264,512]{1,0:T(8,128)S(1)}, f32[264,512]{1,0:T(8,128)S(1)}, u32[]{:S(2)}, u32[]{:S(2)}) collective-permute-start(f32[264,512]{1,0:T(8,128)S(1)} %collective-permute-done.12.refs_2_), channel_id=1, source_target_pairs={{0,8},{1,9},{2,10},{3,11},{4,28},{5,29},{6,30},{7,31},{8,16},{9,17... | collective-permute-start | bytes 1622024 | tf_op jit(solution)/shard_map/ppermute | solution.py:58
  70.7 0.1 columns.1
  70.7 1.9 %collective-permute-start.14 = (f32[520,128]{1,0:T(8,128)S(1)}, f32[520,128]{1,0:T(8,128)S(1)}, u32[]{:S(2)}, u32[]{:S(2)}) collective-permute-start(f32[520,128]{1,0:T(8,128)S(1)} %get-tuple-element.48), channel_id=1, source_target_pairs={{0,0},{1,4},{2,1},{3,5},{4,2},{5,6},{6,3},{7,7},{8,8},{9,12},{10,9... | collective-permute-start | bytes 798728 | tf_op jit(solution)/shard_map/ppermute | solution.py:58
  72.7 2.0 %collective-permute-start.15 = (f32[520,128]{1,0:T(8,128)S(1)}, f32[520,128]{1,0:T(8,128)S(1)}, u32[]{:S(2)}, u32[]{:S(2)}) collective-permute-start(f32[520,128]{1,0:T(8,128)S(1)} %get-tuple-element.49), channel_id=1, source_target_pairs={{0,1},{1,5},{2,0},{3,4},{4,3},{5,7},{6,2},{7,6},{8,9},{9,13},{10,8... | collective-permute-start | bytes 798728 | tf_op jit(solution)/shard_map/ppermute | solution.py:58
  74.7 5.9 %collective-permute-done.14.cut0_ref = f32[520,128]{1,0:T(8,128)S(1)} collective-permute-done((f32[520,128]{1,0:T(8,128)S(1)}, f32[520,128]{1,0:T(8,128)S(1)}, u32[]{:S(2)}, u32[]{:S(2)}) %collective-permute-start.14) | collective-permute-done | bytes 266272 | tf_op jit(solution)/shard_map/ppermute | solution.py:58
  80.6 1.1 collective-permute-done.15.cut1_ref
  81.7 0.5 collective-permute-start.16
  82.2 0.0 collective-permute-start.19
  82.2 1.4 %collective-permute-done.17.refs_5_ = f32[264,512]{1,0:T(8,128)S(1)} collective-permute-done((f32[264,512]{1,0:T(8,128)S(1)}, f32[264,512]{1,0:T(8,128)S(1)}, u32[]{:S(2)}, u32[]{:S(2)}) %collective-permute-start.17) | collective-permute-done | bytes 540704 | tf_op jit(solution)/shard_map/ppermute | solution.py:58
  83.6 0.8 collective-permute-done.16.refs_4_
  84.4 0.8 collective-permute-done.19.refs_7_
  85.2 1.3 %lead.1 = (f32[4,2,264,512]{3,2,1,0:T(8,128)S(1)}, f32[8,512]{1,0:T(8,128)S(1)}) custom-call(f32[264,512]{1,0:T(8,128)S(1)} %get-tuple-element.46.after_ref.refs_0_, f32[264,512]{1,0:T(8,128)S(1)} %get-tuple-element.47.refs_1_, f32[264,512]{1,0:T(8,128)S(1)} %collective-permute-done.12.refs_2_, f32[264,512]{1,0:T(8,128)S(1)} %collective-permute-done.13.refs_3_, ...), custom_call_target="tpu_custom_call" | custom-call | tf_op jit(solution)/shard_map/lead/pallas_call | solution.py:345
  86.5 0.7 collective-permute-start.20
  87.1 2.8 %chain_y.1 = (f32[3,520,512]{2,1,0:T(8,128)S(1)}, f32[520,512]{1,0:T(8,128)S(1)}) custom-call(f32[4,2,264,512]{3,2,1,0:T(8,128)S(1)} %get-tuple-element.51.refs_0_), custom_call_target="tpu_custom_call" | custom-call | tf_op jit(solution)/shard_map/chain_y/pallas_call | solution.py:363
  89.9 0.0 collective-permute-done.20.came_ref
  89.9 0.3 plane.6
  90.2 0.7 collective-permute-start.21
  90.9 0.3 plane.7
  91.2 0.7 collective-permute-start.22
  91.8 0.0 collective-permute-done.22.came_ref
  91.8 0.3 plane.8
  92.1 0.7 collective-permute-start.23
  92.8 0.0 collective-permute-done.23.came_ref
  92.8 0.3 plane.9
  93.1 0.7 collective-permute-start.24
  93.7 0.3 plane.10
  94.0 0.7 collective-permute-start.25
  94.7 0.0 collective-permute-done.25.came_ref
  94.7 0.3 plane.11
  95.0 1.3 %collective-permute-start.26 = (f32[8,512]{1,0:T(8,128)S(1)}, f32[8,512]{1,0:T(8,128)S(1)}, u32[]{:S(2)}, u32[]{:S(2)}) collective-permute-start(f32[8,512]{1,0:T(8,128)S(1)} %get-tuple-element.65), channel_id=1, source_target_pairs={{36,4},{44,12},{52,20},{60,28},{37,5},{45,13},{53,21},{61,29},{38,... | collective-permute-start | bytes 49160 | tf_op jit(solution)/shard_map/ppermute | solution.py:437
  96.3 20.3 %collective-permute-done.26 = f32[8,512]{1,0:T(8,128)S(1)} collective-permute-done((f32[8,512]{1,0:T(8,128)S(1)}, f32[8,512]{1,0:T(8,128)S(1)}, u32[]{:S(2)}, u32[]{:S(2)}) %collective-permute-start.26) | collective-permute-done | bytes 16416 | tf_op jit(solution)/shard_map/ppermute | solution.py:437
  116.5 1.3 %collective-permute-start.27 = (f32[8,512]{1,0:T(8,128)S(1)}, f32[8,512]{1,0:T(8,128)S(1)}, u32[]{:S(2)}, u32[]{:S(2)}) collective-permute-start(f32[8,512]{1,0:T(8,128)S(1)} %add.3.carried_ref), channel_id=1, source_target_pairs={{4,0},{12,8},{20,16},{28,24},{36,32},{44,40},{52,48},{60,56},{68,6... | collective-permute-start | bytes 49160 | tf_op jit(solution)/shard_map/ppermute | solution.py:439
  117.8 0.8 collective-permute-done.27.came_ref
  118.6 1.6 %down.1 = f32[4,128]{1,0:T(4,128)} custom-call(f32[8,512]{1,0:T(8,128)S(1)} %add.3.carried_ref, f32[8,512]{1,0:T(8,128)S(1)} %collective-permute-done.27.came_ref, f32[520,128]{1,0:T(8,128)S(1)} %collective-permute-done.14.cut0_ref, f32[520,128]{1,0:T(8,128)S(1)} %collective-permute-done.15.cut1_ref, f32[3,520,512]{2,1,0:T(8,128)S(1)} %get-tuple-element.68.rows_ref, ...), custom_call_target="tpu_custom_call" | custom-call | tf_op jit(solution)/shard_map/down/pallas_call | solution.py:440
  (8 shorter events, 0.0 us)
Async XLA Ops:
  2.0 22.6 %collective-permute-start.4 = (f32[256,512]{1,0:T(8,128)S(1)}, f32[256,512]{1,0:T(8,128)S(1)}, u32[]{:S(2)}, u32[]{:S(2)}) collective-permute-start(f32[256,512]{1,0:T(8,128)S(1)} %get-tuple-element.43), channel_id=1, source_target_pairs={{0,4},{1,5},{2,6},{3,7},{4,0},{5,1},{6,2},{7,3},{8,12},{9,13},{10,... | collective-permute-start | bytes 1572872 | tf_op jit(solution)/shard_map/ppermute | solution.py:58
  5.4 12.1 %collective-permute-start = (f32[328,256]{1,0:T(8,128)S(1)}, f32[328,256]{1,0:T(8,128)S(1)}, u32[]{:S(2)}, u32[]{:S(2)}) collective-permute-start(f32[328,256]{1,0:T(8,128)S(1)} %get-tuple-element.38), channel_id=1, source_target_pairs={{0,0},{1,4},{2,2},{3,6},{4,1},{5,5},{6,3},{7,7},{8,8},{9,12},{10,1... | collective-permute-start | bytes 1007624 | tf_op jit(solution)/shard_map/ppermute | solution.py:58
  7.3 11.9 %collective-permute-start.1 = (f32[328,256]{1,0:T(8,128)S(1)}, f32[328,256]{1,0:T(8,128)S(1)}, u32[]{:S(2)}, u32[]{:S(2)}) collective-permute-start(f32[328,256]{1,0:T(8,128)S(1)} %get-tuple-element.39), channel_id=1, source_target_pairs={{0,4},{1,2},{2,6},{3,0},{4,5},{5,3},{6,7},{7,1},{8,12},{9,10},{10,... | collective-permute-start | bytes 1007624 | tf_op jit(solution)/shard_map/ppermute | solution.py:58
  7.4 17.3 %collective-permute-start.2 = (f32[328,256]{1,0:T(8,128)S(1)}, f32[328,256]{1,0:T(8,128)S(1)}, u32[]{:S(2)}, u32[]{:S(2)}) collective-permute-start(f32[328,256]{1,0:T(8,128)S(1)} %get-tuple-element.40), channel_id=1, source_target_pairs={{0,2},{1,6},{2,0},{3,4},{4,3},{5,7},{6,1},{7,5},{8,10},{9,14},{10,... | collective-permute-start | bytes 1007624 | tf_op jit(solution)/shard_map/ppermute | solution.py:58
  9.0 15.6 %collective-permute-start.3 = (f32[328,256]{1,0:T(8,128)S(1)}, f32[328,256]{1,0:T(8,128)S(1)}, u32[]{:S(2)}, u32[]{:S(2)}) collective-permute-start(f32[328,256]{1,0:T(8,128)S(1)} %get-tuple-element.41), channel_id=1, source_target_pairs={{0,6},{1,0},{2,4},{3,2},{4,7},{5,1},{6,5},{7,3},{8,14},{9,8},{10,1... | collective-permute-start | bytes 1007624 | tf_op jit(solution)/shard_map/ppermute | solution.py:58
  27.5 2.8 %collective-permute-start.5 = (f32[520,512]{1,0:T(8,128)S(1)}, f32[520,512]{1,0:T(8,128)S(1)}, u32[]{:S(2)}, u32[]{:S(2)}) collective-permute-start(f32[520,512]{1,0:T(8,128)S(1)} %step.1.own_ref), channel_id=1, source_target_pairs={{0,4},{1,5},{2,6},{3,7},{4,0},{5,1},{6,2},{7,3},{8,12},{9,13},{10,... | collective-permute-start | bytes 3194888 | tf_op jit(solution)/shard_map/ppermute | solution.py:58
  31.3 8.7 %collective-permute-start.6 = (f32[264,512]{1,0:T(8,128)S(1)}, f32[264,512]{1,0:T(8,128)S(1)}, u32[]{:S(2)}, u32[]{:S(2)}) collective-permute-start(f32[264,512]{1,0:T(8,128)S(1)} %get-tuple-element.44.refs_0_), channel_id=1, source_target_pairs={{0,1},{1,2},{2,3},{3,0},{4,7},{5,4},{6,5},{7,6},{8,9},{9,10},{10,1... | collective-permute-start | bytes 1622024 | tf_op jit(solution)/shard_map/ppermute | solution.py:58
  33.7 12.1 %collective-permute-start.7 = (f32[264,512]{1,0:T(8,128)S(1)}, f32[264,512]{1,0:T(8,128)S(1)}, u32[]{:S(2)}, u32[]{:S(2)}) collective-permute-start(f32[264,512]{1,0:T(8,128)S(1)} %get-tuple-element.45.refs_1_), channel_id=1, source_target_pairs={{0,1},{1,2},{2,3},{3,0},{4,7},{5,4},{6,5},{7,6},{8,9},{9,10},{10,1... | collective-permute-start | bytes 1622024 | tf_op jit(solution)/shard_map/ppermute | solution.py:58
  40.0 11.6 %collective-permute-start.10 = (f32[264,512]{1,0:T(8,128)S(1)}, f32[264,512]{1,0:T(8,128)S(1)}, u32[]{:S(2)}, u32[]{:S(2)}) collective-permute-start(f32[264,512]{1,0:T(8,128)S(1)} %collective-permute-done.6.refs_2_), channel_id=1, source_target_pairs={{0,1},{1,2},{2,3},{3,0},{4,7},{5,4},{6,5},{7,6},{8,9},{9,10},{10,1... | collective-permute-start | bytes 1622024 | tf_op jit(solution)/shard_map/ppermute | solution.py:58
  43.2 10.8 %collective-permute-start.8 = (f32[264,512]{1,0:T(8,128)S(1)}, f32[264,512]{1,0:T(8,128)S(1)}, u32[]{:S(2)}, u32[]{:S(2)}) collective-permute-start(f32[264,512]{1,0:T(8,128)S(1)} %collective-permute-done.6.refs_2_), channel_id=1, source_target_pairs={{0,4},{1,5},{2,6},{3,7},{4,0},{5,1},{6,2},{7,3},{8,12},{9,13},{10,... | collective-permute-start | bytes 1622024 | tf_op jit(solution)/shard_map/ppermute | solution.py:58
  45.8 8.1 %collective-permute-start.9 = (f32[264,512]{1,0:T(8,128)S(1)}, f32[264,512]{1,0:T(8,128)S(1)}, u32[]{:S(2)}, u32[]{:S(2)}) collective-permute-start(f32[264,512]{1,0:T(8,128)S(1)} %collective-permute-done.7.refs_3_), channel_id=1, source_target_pairs={{0,4},{1,5},{2,6},{3,7},{4,0},{5,1},{6,2},{7,3},{8,12},{9,13},{10,... | collective-permute-start | bytes 1622024 | tf_op jit(solution)/shard_map/ppermute | solution.py:58
  51.6 3.9 %collective-permute-start.11 = (f32[264,512]{1,0:T(8,128)S(1)}, f32[264,512]{1,0:T(8,128)S(1)}, u32[]{:S(2)}, u32[]{:S(2)}) collective-permute-start(f32[264,512]{1,0:T(8,128)S(1)} %collective-permute-done.10.refs_6_), channel_id=1, source_target_pairs={{0,4},{1,5},{2,6},{3,7},{4,0},{5,1},{6,2},{7,3},{8,12},{9,13},{10,... | collective-permute-start | bytes 1622024 | tf_op jit(solution)/shard_map/ppermute | solution.py:58
  58.8 8.7 %collective-permute-start.12 = (f32[264,512]{1,0:T(8,128)S(1)}, f32[264,512]{1,0:T(8,128)S(1)}, u32[]{:S(2)}, u32[]{:S(2)}) collective-permute-start(f32[264,512]{1,0:T(8,128)S(1)} %get-tuple-element.46.after_ref.refs_0_), channel_id=1, source_target_pairs={{0,8},{1,9},{2,10},{3,11},{4,28},{5,29},{6,30},{7,31},{8,16},{9,17... | collective-permute-start | bytes 1622024 | tf_op jit(solution)/shard_map/ppermute | solution.py:58
  61.3 20.4 %collective-permute-start.13 = (f32[264,512]{1,0:T(8,128)S(1)}, f32[264,512]{1,0:T(8,128)S(1)}, u32[]{:S(2)}, u32[]{:S(2)}) collective-permute-start(f32[264,512]{1,0:T(8,128)S(1)} %get-tuple-element.47.refs_1_), channel_id=1, source_target_pairs={{0,8},{1,9},{2,10},{3,11},{4,28},{5,29},{6,30},{7,31},{8,16},{9,17... | collective-permute-start | bytes 1622024 | tf_op jit(solution)/shard_map/ppermute | solution.py:58
  67.6 14.6 %collective-permute-start.18 = (f32[264,512]{1,0:T(8,128)S(1)}, f32[264,512]{1,0:T(8,128)S(1)}, u32[]{:S(2)}, u32[]{:S(2)}) collective-permute-start(f32[264,512]{1,0:T(8,128)S(1)} %collective-permute-done.12.refs_2_), channel_id=1, source_target_pairs={{0,8},{1,9},{2,10},{3,11},{4,28},{5,29},{6,30},{7,31},{8,16},{9,17... | collective-permute-start | bytes 1622024 | tf_op jit(solution)/shard_map/ppermute | solution.py:58
  70.7 9.8 %collective-permute-start.14 = (f32[520,128]{1,0:T(8,128)S(1)}, f32[520,128]{1,0:T(8,128)S(1)}, u32[]{:S(2)}, u32[]{:S(2)}) collective-permute-start(f32[520,128]{1,0:T(8,128)S(1)} %get-tuple-element.48), channel_id=1, source_target_pairs={{0,0},{1,4},{2,1},{3,5},{4,2},{5,6},{6,3},{7,7},{8,8},{9,12},{10,9... | collective-permute-start | bytes 798728 | tf_op jit(solution)/shard_map/ppermute | solution.py:58
  72.7 9.0 %collective-permute-start.15 = (f32[520,128]{1,0:T(8,128)S(1)}, f32[520,128]{1,0:T(8,128)S(1)}, u32[]{:S(2)}, u32[]{:S(2)}) collective-permute-start(f32[520,128]{1,0:T(8,128)S(1)} %get-tuple-element.49), channel_id=1, source_target_pairs={{0,1},{1,5},{2,0},{3,4},{4,3},{5,7},{6,2},{7,6},{8,9},{9,13},{10,8... | collective-permute-start | bytes 798728 | tf_op jit(solution)/shard_map/ppermute | solution.py:58
  81.7 1.9 %collective-permute-start.17 = (f32[264,512]{1,0:T(8,128)S(1)}, f32[264,512]{1,0:T(8,128)S(1)}, u32[]{:S(2)}, u32[]{:S(2)}) collective-permute-start(f32[264,512]{1,0:T(8,128)S(1)} %collective-permute-done.13.refs_3_), channel_id=1, source_target_pairs={{0,4},{1,5},{2,6},{3,7},{4,0},{5,1},{6,2},{7,3},{8,12},{9,13},{10,... | collective-permute-start | bytes 1622024 | tf_op jit(solution)/shard_map/ppermute | solution.py:58
  81.7 2.7 %collective-permute-start.16 = (f32[264,512]{1,0:T(8,128)S(1)}, f32[264,512]{1,0:T(8,128)S(1)}, u32[]{:S(2)}, u32[]{:S(2)}) collective-permute-start(f32[264,512]{1,0:T(8,128)S(1)} %collective-permute-done.12.refs_2_), channel_id=1, source_target_pairs={{0,4},{1,5},{2,6},{3,7},{4,0},{5,1},{6,2},{7,3},{8,12},{9,13},{10,... | collective-permute-start | bytes 1622024 | tf_op jit(solution)/shard_map/ppermute | solution.py:58
  82.2 3.0 %collective-permute-start.19 = (f32[264,512]{1,0:T(8,128)S(1)}, f32[264,512]{1,0:T(8,128)S(1)}, u32[]{:S(2)}, u32[]{:S(2)}) collective-permute-start(f32[264,512]{1,0:T(8,128)S(1)} %collective-permute-done.18.refs_6_), channel_id=1, source_target_pairs={{0,4},{1,5},{2,6},{3,7},{4,0},{5,1},{6,2},{7,3},{8,12},{9,13},{10,... | collective-permute-start | bytes 1622024 | tf_op jit(solution)/shard_map/ppermute | solution.py:58
  86.5 3.4 %collective-permute-start.20 = (f32[8,512]{1,0:T(8,128)S(1)}, f32[8,512]{1,0:T(8,128)S(1)}, u32[]{:S(2)}, u32[]{:S(2)}) collective-permute-start(f32[8,512]{1,0:T(8,128)S(1)} %get-tuple-element.53), channel_id=1, source_target_pairs={{228,196},{236,204},{244,212},{252,220},{229,197},{237,205},{245,2... | collective-permute-start | bytes 49160 | tf_op jit(solution)/shard_map/ppermute | solution.py:437
  90.2 0.7 collective-permute-start.21
  91.2 0.7 collective-permute-start.22
  92.1 0.7 collective-permute-start.23
  93.1 0.7 collective-permute-start.24
  94.0 0.7 collective-permute-start.25
  95.0 21.6 %collective-permute-start.26 = (f32[8,512]{1,0:T(8,128)S(1)}, f32[8,512]{1,0:T(8,128)S(1)}, u32[]{:S(2)}, u32[]{:S(2)}) collective-permute-start(f32[8,512]{1,0:T(8,128)S(1)} %get-tuple-element.65), channel_id=1, source_target_pairs={{36,4},{44,12},{52,20},{60,28},{37,5},{45,13},{53,21},{61,29},{38,... | collective-permute-start | bytes 49160 | tf_op jit(solution)/shard_map/ppermute | solution.py:437
  116.5 2.1 %collective-permute-start.27 = (f32[8,512]{1,0:T(8,128)S(1)}, f32[8,512]{1,0:T(8,128)S(1)}, u32[]{:S(2)}, u32[]{:S(2)}) collective-permute-start(f32[8,512]{1,0:T(8,128)S(1)} %add.3.carried_ref), channel_id=1, source_target_pairs={{4,0},{12,8},{20,16},{28,24},{36,32},{44,40},{52,48},{60,56},{68,6... | collective-permute-start | bytes 49160 | tf_op jit(solution)/shard_map/ppermute | solution.py:439

commit v6 on v5

--- a/solution.py
+++ b/solution.py
@@ -213,24 +213,27 @@
 def fetch(panels, held, sems, index, c, turned):
     forth, back, far = index + 3 - 2 * c, index + 1 + 2 * c, index + 2
     homes = ((index, c), (index, 1 - c), (forth, c), (forth, 1 - c), (back, 1 - c), (back, c), (far, c), (far, 1 - c))
-    copies = []
-    for n, (ref, (source, half)) in enumerate(zip(panels, homes)):
+    for ref, (source, half) in zip(panels, homes):
         slot = lax.rem(source, 4)
         if turned:
             slot = 2 * lax.rem(slot, 2) + slot // 2
-        copy = pltpu.make_async_copy(ref, held.at[slot, half], sems.at[n])
+        copy = pltpu.make_async_copy(ref, held.at[slot, half], sems.at[slot, half])
         copy.start()
-        copies.append(copy)
-    return copies
+
+
+def arrive(panels, held, sems, t):
+    for half in range(2):
+        pltpu.make_async_copy(panels[0], held.at[t, half], sems.at[t, half]).wait()
 
 
 def lead_kernel(*refs):
     panels, held, lead_ref, sems = refs[:8], refs[8], refs[9], refs[10]
     _, y, _, c = place()
-    for copy in fetch(panels, held, sems, y, c, False):
-        copy.wait()
+    fetch(panels, held, sems, y, c, False)
+    arrive(panels, held, sems, 3)
     row8 = held[3, 0, HALF:PAN, :]
     for t in (2, 1, 0):
+        arrive(panels, held, sems, t)
         row8 = (
             rows_times(row8[:, 0:HALF], held[t, 0, 0:HALF, :])
             + rows_times(row8[:, HALF:W], held[t, 1, 0:HALF, :])
@@ -246,8 +249,8 @@
         panels, held, prefix, outs, sems = refs[:8], refs[8], refs[9], refs[10:-1], refs[-1]
     x, y, _, c = place()
     if not whole:
-        for copy in fetch(panels, held, sems, x, c, True):
-            copy.wait()
+        fetch(panels, held, sems, x, c, True)
+        arrive(panels, held, sems, 3)
     tail = held[3, 0, HALF:PAN, :]
     begin = 0 if whole else c
     rows = jnp.concatenate([held[3, begin, 0:HALF, :], held[3, 1 - begin, 0:HALF, :], tail], axis=0)
@@ -255,6 +258,8 @@
     if whole:
         prefix[2] = rows
     for t in (2, 1, 0):
+        if not whole:
+            arrive(panels, held, sems, t)
         left = split(rows)
         top = split(held[t, 0, 0:HALF, :])
         bottom = split(held[t, 1, 0:HALF, :])
@@ -347,7 +352,7 @@
         out_shape=[shape(4, 2, PAN, W), shape(8, W)],
         in_specs=[ANYWHERE] * 8,
         out_specs=[IN_VMEM] * 2,
-        scratch_shapes=[pltpu.SemaphoreType.DMA((8,))],
+        scratch_shapes=[pltpu.SemaphoreType.DMA((4, 2))],
         compiler_params=PARAMS,
         name="lead",
     )(*panels)
@@ -365,7 +370,7 @@
         out_shape=outs,
         in_specs=[IN_VMEM] if whole else [ANYWHERE] * 8,
         out_specs=[IN_VMEM] * len(outs),
-        scratch_shapes=[] if whole else [pltpu.SemaphoreType.DMA((8,))],
+        scratch_shapes=[] if whole else [pltpu.SemaphoreType.DMA((4, 2))],
         compiler_params=PARAMS,
         name="chain_" + along,
     )(*operands)

time: 120 us -> 121 us (level)
  no operation moved by 1% of the time
where the time goes in v6:
time: 121 us
  waiting for transfers between devices  65.9 us (54%)
  starting transfers between devices  37.5 us (31%)
  Pallas kernels  17.1 us (14%)
    ppermute x20, waiting for transfers between devices, move(): return lax.ppermute(value, AXES, pairs)  44.8 us
    ppermute x20, starting transfers between devices, move(): return lax.ppermute(value, AXES, pairs)  31 us
    ppermute x7, waiting for transfers between devices, on_device(): lax.ppermute(out, 'tm', [(t, t - 8) for t in range(64) if t // 8 == 7 - i...  20.3 us
    pallas_call x2, Pallas kernels, chain(): pl.pallas_call(kernel, out_shape=outs, in_specs=[IN_VMEM] if whole else [...  6.53 us
    ppermute x7, starting transfers between devices, on_device(): lax.ppermute(out, 'tm', [(t, t - 8) for t in range(64) if t // 8 == 7 - i...  5.26 us
    pallas_call x1, Pallas kernels, on_device(): pl.pallas_call(step_kernel, out_shape=shape(FULL, W), in_specs=[IN_VMEM]...  2.9 us
  transfers between devices with their start and end apart: 28, of which 16 were waited for; matrix products, arithmetic and copies ran while one was open for 0% of the time, Pallas kernels for 2%

profile of v6, /device:TPU:1, one launch (start us, length us, event | category | flops | bytes accessed | tf_op | source)
XLA Modules:
  0.0 120.7 jit_solution(17122920965640284803)
XLA Ops:
  0.0 2.0 %pack.1 = (f32[328,256]{1,0:T(8,128)S(1)}, f32[328,256]{1,0:T(8,128)S(1)}, f32[328,256]{1,0:T(8,128)S(1)}, f32[328,256]{1,0:T(8,128)S(1)}, f32[256,512]{1,0:T(8,128)S(1)}, /*index=5*/f32[256,512]{1,0:T(8,128)S(1)}) custom-call(f32[4,128,512]{2,1,0:T(8,128)} %p_ref.1, f32[4,128,512]{2,1,0:T(8,128)} %r_ref.1, f32[4,2,64,128]{3,2,1,0:T(8,128)} %t_ref.1, ...), custom_call_target="tpu_custom_call" | custom-call | tf_op jit(solution)/shard_map/pack/pallas_call | solution.py:384
  2.0 3.3 %collective-permute-start.4 = (f32[256,512]{1,0:T(8,128)S(1)}, f32[256,512]{1,0:T(8,128)S(1)}, u32[]{:S(2)}, u32[]{:S(2)}) collective-permute-start(f32[256,512]{1,0:T(8,128)S(1)} %get-tuple-element.43), channel_id=1, source_target_pairs={{0,4},{1,5},{2,6},{3,7},{4,0},{5,1},{6,2},{7,3},{8,12},{9,13},{10,... | collective-permute-start | bytes 1572872 | tf_op jit(solution)/shard_map/ppermute | solution.py:58
  5.4 1.9 %collective-permute-start = (f32[328,256]{1,0:T(8,128)S(1)}, f32[328,256]{1,0:T(8,128)S(1)}, u32[]{:S(2)}, u32[]{:S(2)}) collective-permute-start(f32[328,256]{1,0:T(8,128)S(1)} %get-tuple-element.38), channel_id=1, source_target_pairs={{0,0},{1,4},{2,2},{3,6},{4,1},{5,5},{6,3},{7,7},{8,8},{9,12},{10,1... | collective-permute-start | bytes 1007624 | tf_op jit(solution)/shard_map/ppermute | solution.py:58
  7.3 0.1 collective-permute-start.1
  7.4 1.7 %collective-permute-start.2 = (f32[328,256]{1,0:T(8,128)S(1)}, f32[328,256]{1,0:T(8,128)S(1)}, u32[]{:S(2)}, u32[]{:S(2)}) collective-permute-start(f32[328,256]{1,0:T(8,128)S(1)} %get-tuple-element.40), channel_id=1, source_target_pairs={{0,2},{1,6},{2,0},{3,4},{4,3},{5,7},{6,1},{7,5},{8,10},{9,14},{10,... | collective-permute-start | bytes 1007624 | tf_op jit(solution)/shard_map/ppermute | solution.py:58
  9.0 2.9 %collective-permute-start.3 = (f32[328,256]{1,0:T(8,128)S(1)}, f32[328,256]{1,0:T(8,128)S(1)}, u32[]{:S(2)}, u32[]{:S(2)}) collective-permute-start(f32[328,256]{1,0:T(8,128)S(1)} %get-tuple-element.41), channel_id=1, source_target_pairs={{0,6},{1,0},{2,4},{3,2},{4,7},{5,1},{6,5},{7,3},{8,14},{9,8},{10,1... | collective-permute-start | bytes 1007624 | tf_op jit(solution)/shard_map/ppermute | solution.py:58
  11.9 5.6 %collective-permute-done.pay0 = f32[328,256]{1,0:T(8,128)S(1)} collective-permute-done((f32[328,256]{1,0:T(8,128)S(1)}, f32[328,256]{1,0:T(8,128)S(1)}, u32[]{:S(2)}, u32[]{:S(2)}) %collective-permute-start) | collective-permute-done | bytes 335904 | tf_op jit(solution)/shard_map/ppermute | solution.py:58
  17.5 1.7 %collective-permute-done.1.pay1 = f32[328,256]{1,0:T(8,128)S(1)} collective-permute-done((f32[328,256]{1,0:T(8,128)S(1)}, f32[328,256]{1,0:T(8,128)S(1)}, u32[]{:S(2)}, u32[]{:S(2)}) %collective-permute-start.1) | collective-permute-done | bytes 335904 | tf_op jit(solution)/shard_map/ppermute | solution.py:58
  19.2 5.5 %collective-permute-done.2.pay2 = f32[328,256]{1,0:T(8,128)S(1)} collective-permute-done((f32[328,256]{1,0:T(8,128)S(1)}, f32[328,256]{1,0:T(8,128)S(1)}, u32[]{:S(2)}, u32[]{:S(2)}) %collective-permute-start.2) | collective-permute-done | bytes 335904 | tf_op jit(solution)/shard_map/ppermute | solution.py:58
  24.6 0.0 collective-permute-done.3.pay3
  24.6 0.0 collective-permute-done.4.other_ref
  24.6 2.9 %step.1.own_ref = f32[520,512]{1,0:T(8,128)S(1)} custom-call(f32[328,256]{1,0:T(8,128)S(1)} %collective-permute-done.pay0, f32[328,256]{1,0:T(8,128)S(1)} %collective-permute-done.1.pay1, f32[328,256]{1,0:T(8,128)S(1)} %collective-permute-done.2.pay2, f32[328,256]{1,0:T(8,128)S(1)} %collective-permute-done.3.pay3, ...), custom_call_target="tpu_custom_call" | custom-call | tf_op jit(solution)/shard_map/step/pallas_call | solution.py:399
  27.5 0.5 collective-permute-start.5
  28.0 2.3 %collective-permute-done.5.other_ref = f32[520,512]{1,0:T(8,128)S(1)} collective-permute-done((f32[520,512]{1,0:T(8,128)S(1)}, f32[520,512]{1,0:T(8,128)S(1)}, u32[]{:S(2)}, u32[]{:S(2)}) %collective-permute-start.5) | collective-permute-done | bytes 1064992 | tf_op jit(solution)/shard_map/ppermute | solution.py:58
  30.3 1.0 pair.1
  31.3 2.4 %collective-permute-start.6 = (f32[264,512]{1,0:T(8,128)S(1)}, f32[264,512]{1,0:T(8,128)S(1)}, u32[]{:S(2)}, u32[]{:S(2)}) collective-permute-start(f32[264,512]{1,0:T(8,128)S(1)} %get-tuple-element.44.refs_0_), channel_id=1, source_target_pairs={{0,1},{1,2},{2,3},{3,0},{4,7},{5,4},{6,5},{7,6},{8,9},{9,10},{10,1... | collective-permute-start | bytes 1622024 | tf_op jit(solution)/shard_map/ppermute | solution.py:58
  33.7 0.1 collective-permute-start.7
  33.8 6.2 %collective-permute-done.6.refs_2_ = f32[264,512]{1,0:T(8,128)S(1)} collective-permute-done((f32[264,512]{1,0:T(8,128)S(1)}, f32[264,512]{1,0:T(8,128)S(1)}, u32[]{:S(2)}, u32[]{:S(2)}) %collective-permute-start.6) | collective-permute-done | bytes 540704 | tf_op jit(solution)/shard_map/ppermute | solution.py:58
  40.0 3.1 %collective-permute-start.10 = (f32[264,512]{1,0:T(8,128)S(1)}, f32[264,512]{1,0:T(8,128)S(1)}, u32[]{:S(2)}, u32[]{:S(2)}) collective-permute-start(f32[264,512]{1,0:T(8,128)S(1)} %collective-permute-done.6.refs_2_), channel_id=1, source_target_pairs={{0,1},{1,2},{2,3},{3,0},{4,7},{5,4},{6,5},{7,6},{8,9},{9,10},{10,1... | collective-permute-start | bytes 1622024 | tf_op jit(solution)/shard_map/ppermute | solution.py:58
  43.2 0.0 collective-permute-start.8
  43.2 2.7 %collective-permute-done.7.refs_3_ = f32[264,512]{1,0:T(8,128)S(1)} collective-permute-done((f32[264,512]{1,0:T(8,128)S(1)}, f32[264,512]{1,0:T(8,128)S(1)}, u32[]{:S(2)}, u32[]{:S(2)}) %collective-permute-start.7) | collective-permute-done | bytes 540704 | tf_op jit(solution)/shard_map/ppermute | solution.py:58
  45.8 2.3 %collective-permute-start.9 = (f32[264,512]{1,0:T(8,128)S(1)}, f32[264,512]{1,0:T(8,128)S(1)}, u32[]{:S(2)}, u32[]{:S(2)}) collective-permute-start(f32[264,512]{1,0:T(8,128)S(1)} %collective-permute-done.7.refs_3_), channel_id=1, source_target_pairs={{0,4},{1,5},{2,6},{3,7},{4,0},{5,1},{6,2},{7,3},{8,12},{9,13},{10,... | collective-permute-start | bytes 1622024 | tf_op jit(solution)/shard_map/ppermute | solution.py:58
  48.1 3.5 %collective-permute-done.10.refs_6_ = f32[264,512]{1,0:T(8,128)S(1)} collective-permute-done((f32[264,512]{1,0:T(8,128)S(1)}, f32[264,512]{1,0:T(8,128)S(1)}, u32[]{:S(2)}, u32[]{:S(2)}) %collective-permute-start.10) | collective-permute-done | bytes 540704 | tf_op jit(solution)/shard_map/ppermute | solution.py:58
  51.6 2.3 %collective-permute-start.11 = (f32[264,512]{1,0:T(8,128)S(1)}, f32[264,512]{1,0:T(8,128)S(1)}, u32[]{:S(2)}, u32[]{:S(2)}) collective-permute-start(f32[264,512]{1,0:T(8,128)S(1)} %collective-permute-done.10.refs_6_), channel_id=1, source_target_pairs={{0,4},{1,5},{2,6},{3,7},{4,0},{5,1},{6,2},{7,3},{8,12},{9,13},{10,... | collective-permute-start | bytes 1622024 | tf_op jit(solution)/shard_map/ppermute | solution.py:58
  53.9 1.6 %collective-permute-done.11.refs_7_ = f32[264,512]{1,0:T(8,128)S(1)} collective-permute-done((f32[264,512]{1,0:T(8,128)S(1)}, f32[264,512]{1,0:T(8,128)S(1)}, u32[]{:S(2)}, u32[]{:S(2)}) %collective-permute-start.11) | collective-permute-done | bytes 540704 | tf_op jit(solution)/shard_map/ppermute | solution.py:58
  55.5 3.8 %chain_x.1 = (f32[4,2,264,512]{3,2,1,0:T(8,128)S(1)}, f32[520,512]{1,0:T(8,128)S(1)}, f32[264,512]{1,0:T(8,128)S(1)}, f32[264,512]{1,0:T(8,128)S(1)}) custom-call(f32[264,512]{1,0:T(8,128)S(1)} %get-tuple-element.44.refs_0_, f32[264,512]{1,0:T(8,128)S(1)} %get-tuple-element.45.refs_1_, f32[264,512]{1,0:T(8,128)S(1)} %collective-permute-done.6.refs_2_, ...), custom_call_target="tpu_custom_call" | custom-call | tf_op jit(solution)/shard_map/chain_x/pallas_call | solution.py:368
  59.3 2.4 %collective-permute-start.12 = (f32[264,512]{1,0:T(8,128)S(1)}, f32[264,512]{1,0:T(8,128)S(1)}, u32[]{:S(2)}, u32[]{:S(2)}) collective-permute-start(f32[264,512]{1,0:T(8,128)S(1)} %get-tuple-element.46.after_ref.refs_0_), channel_id=1, source_target_pairs={{0,8},{1,9},{2,10},{3,11},{4,28},{5,29},{6,30},{7,31},{8,16},{9,17... | collective-permute-start | bytes 1622024 | tf_op jit(solution)/shard_map/ppermute | solution.py:58
  61.7 0.5 collective-permute-start.13
  62.2 5.8 %collective-permute-done.12.refs_2_ = f32[264,512]{1,0:T(8,128)S(1)} collective-permute-done((f32[264,512]{1,0:T(8,128)S(1)}, f32[264,512]{1,0:T(8,128)S(1)}, u32[]{:S(2)}, u32[]{:S(2)}) %collective-permute-start.12) | collective-permute-done | bytes 540704 | tf_op jit(solution)/shard_map/ppermute | solution.py:58
  68.0 3.1 %collective-permute-start.18 = (f32[264,512]{1,0:T(8,128)S(1)}, f32[264,512]{1,0:T(8,128)S(1)}, u32[]{:S(2)}, u32[]{:S(2)}) collective-permute-start(f32[264,512]{1,0:T(8,128)S(1)} %collective-permute-done.12.refs_2_), channel_id=1, source_target_pairs={{0,8},{1,9},{2,10},{3,11},{4,28},{5,29},{6,30},{7,31},{8,16},{9,17... | collective-permute-start | bytes 1622024 | tf_op jit(solution)/shard_map/ppermute | solution.py:58
  71.1 0.1 columns.1
  71.2 1.9 %collective-permute-start.14 = (f32[520,128]{1,0:T(8,128)S(1)}, f32[520,128]{1,0:T(8,128)S(1)}, u32[]{:S(2)}, u32[]{:S(2)}) collective-permute-start(f32[520,128]{1,0:T(8,128)S(1)} %get-tuple-element.48), channel_id=1, source_target_pairs={{0,0},{1,4},{2,1},{3,5},{4,2},{5,6},{6,3},{7,7},{8,8},{9,12},{10,9... | collective-permute-start | bytes 798728 | tf_op jit(solution)/shard_map/ppermute | solution.py:58
  73.1 2.0 %collective-permute-start.15 = (f32[520,128]{1,0:T(8,128)S(1)}, f32[520,128]{1,0:T(8,128)S(1)}, u32[]{:S(2)}, u32[]{:S(2)}) collective-permute-start(f32[520,128]{1,0:T(8,128)S(1)} %get-tuple-element.49), channel_id=1, source_target_pairs={{0,1},{1,5},{2,0},{3,4},{4,3},{5,7},{6,2},{7,6},{8,9},{9,13},{10,8... | collective-permute-start | bytes 798728 | tf_op jit(solution)/shard_map/ppermute | solution.py:58
  75.1 5.9 %collective-permute-done.14.cut0_ref = f32[520,128]{1,0:T(8,128)S(1)} collective-permute-done((f32[520,128]{1,0:T(8,128)S(1)}, f32[520,128]{1,0:T(8,128)S(1)}, u32[]{:S(2)}, u32[]{:S(2)}) %collective-permute-start.14) | collective-permute-done | bytes 266272 | tf_op jit(solution)/shard_map/ppermute | solution.py:58
  81.0 1.1 collective-permute-done.15.cut1_ref
  82.1 0.0 collective-permute-done.13.refs_3_
  82.1 0.5 collective-permute-start.16
  82.6 0.0 collective-permute-done.18.refs_6_
  82.6 0.0 collective-permute-start.19
  82.7 1.4 %collective-permute-done.17.refs_5_ = f32[264,512]{1,0:T(8,128)S(1)} collective-permute-done((f32[264,512]{1,0:T(8,128)S(1)}, f32[264,512]{1,0:T(8,128)S(1)}, u32[]{:S(2)}, u32[]{:S(2)}) %collective-permute-start.17) | collective-permute-done | bytes 540704 | tf_op jit(solution)/shard_map/ppermute | solution.py:58
  84.1 0.8 collective-permute-done.16.refs_4_
  84.8 0.8 collective-permute-done.19.refs_7_
  85.6 1.4 %lead.1 = (f32[4,2,264,512]{3,2,1,0:T(8,128)S(1)}, f32[8,512]{1,0:T(8,128)S(1)}) custom-call(f32[264,512]{1,0:T(8,128)S(1)} %get-tuple-element.46.after_ref.refs_0_, f32[264,512]{1,0:T(8,128)S(1)} %get-tuple-element.47.refs_1_, f32[264,512]{1,0:T(8,128)S(1)} %collective-permute-done.12.refs_2_, f32[264,512]{1,0:T(8,128)S(1)} %collective-permute-done.13.refs_3_, ...), custom_call_target="tpu_custom_call" | custom-call | tf_op jit(solution)/shard_map/lead/pallas_call | solution.py:350
  87.0 0.7 collective-permute-start.20
  87.7 2.8 %chain_y.1 = (f32[3,520,512]{2,1,0:T(8,128)S(1)}, f32[520,512]{1,0:T(8,128)S(1)}) custom-call(f32[4,2,264,512]{3,2,1,0:T(8,128)S(1)} %get-tuple-element.51.refs_0_), custom_call_target="tpu_custom_call" | custom-call | tf_op jit(solution)/shard_map/chain_y/pallas_call | solution.py:368
  90.4 0.3 plane.6
  90.7 0.7 collective-permute-start.21
  91.4 0.0 collective-permute-done.21.came_ref
  91.4 0.3 plane.7
  91.7 0.7 collective-permute-start.22
  92.3 0.3 plane.8
  92.6 0.7 collective-permute-start.23
  93.3 0.0 collective-permute-done.23.came_ref
  93.3 0.3 plane.9
  93.6 0.7 collective-permute-start.24
  94.2 0.0 collective-permute-done.24.came_ref
  94.2 0.3 plane.10
  94.5 0.7 collective-permute-start.25
  95.2 0.3 plane.11
  95.5 1.3 %collective-permute-start.26 = (f32[8,512]{1,0:T(8,128)S(1)}, f32[8,512]{1,0:T(8,128)S(1)}, u32[]{:S(2)}, u32[]{:S(2)}) collective-permute-start(f32[8,512]{1,0:T(8,128)S(1)} %get-tuple-element.65), channel_id=1, source_target_pairs={{36,4},{44,12},{52,20},{60,28},{37,5},{45,13},{53,21},{61,29},{38,... | collective-permute-start | bytes 49160 | tf_op jit(solution)/shard_map/ppermute | solution.py:442
  96.8 20.3 %collective-permute-done.26 = f32[8,512]{1,0:T(8,128)S(1)} collective-permute-done((f32[8,512]{1,0:T(8,128)S(1)}, f32[8,512]{1,0:T(8,128)S(1)}, u32[]{:S(2)}, u32[]{:S(2)}) %collective-permute-start.26) | collective-permute-done | bytes 16416 | tf_op jit(solution)/shard_map/ppermute | solution.py:442
  117.0 1.3 %collective-permute-start.27 = (f32[8,512]{1,0:T(8,128)S(1)}, f32[8,512]{1,0:T(8,128)S(1)}, u32[]{:S(2)}, u32[]{:S(2)}) collective-permute-start(f32[8,512]{1,0:T(8,128)S(1)} %add.3.carried_ref), channel_id=1, source_target_pairs={{4,0},{12,8},{20,16},{28,24},{36,32},{44,40},{52,48},{60,56},{68,6... | collective-permute-start | bytes 49160 | tf_op jit(solution)/shard_map/ppermute | solution.py:444
  118.3 0.8 collective-permute-done.27.came_ref
  119.1 1.6 %down.1 = f32[4,128]{1,0:T(4,128)} custom-call(f32[8,512]{1,0:T(8,128)S(1)} %add.3.carried_ref, f32[8,512]{1,0:T(8,128)S(1)} %collective-permute-done.27.came_ref, f32[520,128]{1,0:T(8,128)S(1)} %collective-permute-done.14.cut0_ref, f32[520,128]{1,0:T(8,128)S(1)} %collective-permute-done.15.cut1_ref, f32[3,520,512]{2,1,0:T(8,128)S(1)} %get-tuple-element.68.rows_ref, ...), custom_call_target="tpu_custom_call" | custom-call | tf_op jit(solution)/shard_map/down/pallas_call | solution.py:445
  (8 shorter events, 0.0 us)
Async XLA Ops:
  2.0 22.6 %collective-permute-start.4 = (f32[256,512]{1,0:T(8,128)S(1)}, f32[256,512]{1,0:T(8,128)S(1)}, u32[]{:S(2)}, u32[]{:S(2)}) collective-permute-start(f32[256,512]{1,0:T(8,128)S(1)} %get-tuple-element.43), channel_id=1, source_target_pairs={{0,4},{1,5},{2,6},{3,7},{4,0},{5,1},{6,2},{7,3},{8,12},{9,13},{10,... | collective-permute-start | bytes 1572872 | tf_op jit(solution)/shard_map/ppermute | solution.py:58
  5.4 12.1 %collective-permute-start = (f32[328,256]{1,0:T(8,128)S(1)}, f32[328,256]{1,0:T(8,128)S(1)}, u32[]{:S(2)}, u32[]{:S(2)}) collective-permute-start(f32[328,256]{1,0:T(8,128)S(1)} %get-tuple-element.38), channel_id=1, source_target_pairs={{0,0},{1,4},{2,2},{3,6},{4,1},{5,5},{6,3},{7,7},{8,8},{9,12},{10,1... | collective-permute-start | bytes 1007624 | tf_op jit(solution)/shard_map/ppermute | solution.py:58
  7.3 11.9 %collective-permute-start.1 = (f32[328,256]{1,0:T(8,128)S(1)}, f32[328,256]{1,0:T(8,128)S(1)}, u32[]{:S(2)}, u32[]{:S(2)}) collective-permute-start(f32[328,256]{1,0:T(8,128)S(1)} %get-tuple-element.39), channel_id=1, source_target_pairs={{0,4},{1,2},{2,6},{3,0},{4,5},{5,3},{6,7},{7,1},{8,12},{9,10},{10,... | collective-permute-start | bytes 1007624 | tf_op jit(solution)/shard_map/ppermute | solution.py:58
  7.4 17.3 %collective-permute-start.2 = (f32[328,256]{1,0:T(8,128)S(1)}, f32[328,256]{1,0:T(8,128)S(1)}, u32[]{:S(2)}, u32[]{:S(2)}) collective-permute-start(f32[328,256]{1,0:T(8,128)S(1)} %get-tuple-element.40), channel_id=1, source_target_pairs={{0,2},{1,6},{2,0},{3,4},{4,3},{5,7},{6,1},{7,5},{8,10},{9,14},{10,... | collective-permute-start | bytes 1007624 | tf_op jit(solution)/shard_map/ppermute | solution.py:58
  9.0 15.6 %collective-permute-start.3 = (f32[328,256]{1,0:T(8,128)S(1)}, f32[328,256]{1,0:T(8,128)S(1)}, u32[]{:S(2)}, u32[]{:S(2)}) collective-permute-start(f32[328,256]{1,0:T(8,128)S(1)} %get-tuple-element.41), channel_id=1, source_target_pairs={{0,6},{1,0},{2,4},{3,2},{4,7},{5,1},{6,5},{7,3},{8,14},{9,8},{10,1... | collective-permute-start | bytes 1007624 | tf_op jit(solution)/shard_map/ppermute | solution.py:58
  27.5 2.8 %collective-permute-start.5 = (f32[520,512]{1,0:T(8,128)S(1)}, f32[520,512]{1,0:T(8,128)S(1)}, u32[]{:S(2)}, u32[]{:S(2)}) collective-permute-start(f32[520,512]{1,0:T(8,128)S(1)} %step.1.own_ref), channel_id=1, source_target_pairs={{0,4},{1,5},{2,6},{3,7},{4,0},{5,1},{6,2},{7,3},{8,12},{9,13},{10,... | collective-permute-start | bytes 3194888 | tf_op jit(solution)/shard_map/ppermute | solution.py:58
  31.3 8.7 %collective-permute-start.6 = (f32[264,512]{1,0:T(8,128)S(1)}, f32[264,512]{1,0:T(8,128)S(1)}, u32[]{:S(2)}, u32[]{:S(2)}) collective-permute-start(f32[264,512]{1,0:T(8,128)S(1)} %get-tuple-element.44.refs_0_), channel_id=1, source_target_pairs={{0,1},{1,2},{2,3},{3,0},{4,7},{5,4},{6,5},{7,6},{8,9},{9,10},{10,1... | collective-permute-start | bytes 1622024 | tf_op jit(solution)/shard_map/ppermute | solution.py:58
  33.7 12.1 %collective-permute-start.7 = (f32[264,512]{1,0:T(8,128)S(1)}, f32[264,512]{1,0:T(8,128)S(1)}, u32[]{:S(2)}, u32[]{:S(2)}) collective-permute-start(f32[264,512]{1,0:T(8,128)S(1)} %get-tuple-element.45.refs_1_), channel_id=1, source_target_pairs={{0,1},{1,2},{2,3},{3,0},{4,7},{5,4},{6,5},{7,6},{8,9},{9,10},{10,1... | collective-permute-start | bytes 1622024 | tf_op jit(solution)/shard_map/ppermute | solution.py:58
  40.0 11.6 %collective-permute-start.10 = (f32[264,512]{1,0:T(8,128)S(1)}, f32[264,512]{1,0:T(8,128)S(1)}, u32[]{:S(2)}, u32[]{:S(2)}) collective-permute-start(f32[264,512]{1,0:T(8,128)S(1)} %collective-permute-done.6.refs_2_), channel_id=1, source_target_pairs={{0,1},{1,2},{2,3},{3,0},{4,7},{5,4},{6,5},{7,6},{8,9},{9,10},{10,1... | collective-permute-start | bytes 1622024 | tf_op jit(solution)/shard_map/ppermute | solution.py:58
  43.2 10.8 %collective-permute-start.8 = (f32[264,512]{1,0:T(8,128)S(1)}, f32[264,512]{1,0:T(8,128)S(1)}, u32[]{:S(2)}, u32[]{:S(2)}) collective-permute-start(f32[264,512]{1,0:T(8,128)S(1)} %collective-permute-done.6.refs_2_), channel_id=1, source_target_pairs={{0,4},{1,5},{2,6},{3,7},{4,0},{5,1},{6,2},{7,3},{8,12},{9,13},{10,... | collective-permute-start | bytes 1622024 | tf_op jit(solution)/shard_map/ppermute | solution.py:58
  45.8 8.1 %collective-permute-start.9 = (f32[264,512]{1,0:T(8,128)S(1)}, f32[264,512]{1,0:T(8,128)S(1)}, u32[]{:S(2)}, u32[]{:S(2)}) collective-permute-start(f32[264,512]{1,0:T(8,128)S(1)} %collective-permute-done.7.refs_3_), channel_id=1, source_target_pairs={{0,4},{1,5},{2,6},{3,7},{4,0},{5,1},{6,2},{7,3},{8,12},{9,13},{10,... | collective-permute-start | bytes 1622024 | tf_op jit(solution)/shard_map/ppermute | solution.py:58
  51.6 3.9 %collective-permute-start.11 = (f32[264,512]{1,0:T(8,128)S(1)}, f32[264,512]{1,0:T(8,128)S(1)}, u32[]{:S(2)}, u32[]{:S(2)}) collective-permute-start(f32[264,512]{1,0:T(8,128)S(1)} %collective-permute-done.10.refs_6_), channel_id=1, source_target_pairs={{0,4},{1,5},{2,6},{3,7},{4,0},{5,1},{6,2},{7,3},{8,12},{9,13},{10,... | collective-permute-start | bytes 1622024 | tf_op jit(solution)/shard_map/ppermute | solution.py:58
  59.3 8.7 %collective-permute-start.12 = (f32[264,512]{1,0:T(8,128)S(1)}, f32[264,512]{1,0:T(8,128)S(1)}, u32[]{:S(2)}, u32[]{:S(2)}) collective-permute-start(f32[264,512]{1,0:T(8,128)S(1)} %get-tuple-element.46.after_ref.refs_0_), channel_id=1, source_target_pairs={{0,8},{1,9},{2,10},{3,11},{4,28},{5,29},{6,30},{7,31},{8,16},{9,17... | collective-permute-start | bytes 1622024 | tf_op jit(solution)/shard_map/ppermute | solution.py:58
  61.7 20.4 %collective-permute-start.13 = (f32[264,512]{1,0:T(8,128)S(1)}, f32[264,512]{1,0:T(8,128)S(1)}, u32[]{:S(2)}, u32[]{:S(2)}) collective-permute-start(f32[264,512]{1,0:T(8,128)S(1)} %get-tuple-element.47.refs_1_), channel_id=1, source_target_pairs={{0,8},{1,9},{2,10},{3,11},{4,28},{5,29},{6,30},{7,31},{8,16},{9,17... | collective-permute-start | bytes 1622024 | tf_op jit(solution)/shard_map/ppermute | solution.py:58
  68.0 14.6 %collective-permute-start.18 = (f32[264,512]{1,0:T(8,128)S(1)}, f32[264,512]{1,0:T(8,128)S(1)}, u32[]{:S(2)}, u32[]{:S(2)}) collective-permute-start(f32[264,512]{1,0:T(8,128)S(1)} %collective-permute-done.12.refs_2_), channel_id=1, source_target_pairs={{0,8},{1,9},{2,10},{3,11},{4,28},{5,29},{6,30},{7,31},{8,16},{9,17... | collective-permute-start | bytes 1622024 | tf_op jit(solution)/shard_map/ppermute | solution.py:58
  71.2 9.8 %collective-permute-start.14 = (f32[520,128]{1,0:T(8,128)S(1)}, f32[520,128]{1,0:T(8,128)S(1)}, u32[]{:S(2)}, u32[]{:S(2)}) collective-permute-start(f32[520,128]{1,0:T(8,128)S(1)} %get-tuple-element.48), channel_id=1, source_target_pairs={{0,0},{1,4},{2,1},{3,5},{4,2},{5,6},{6,3},{7,7},{8,8},{9,12},{10,9... | collective-permute-start | bytes 798728 | tf_op jit(solution)/shard_map/ppermute | solution.py:58
  73.1 9.0 %collective-permute-start.15 = (f32[520,128]{1,0:T(8,128)S(1)}, f32[520,128]{1,0:T(8,128)S(1)}, u32[]{:S(2)}, u32[]{:S(2)}) collective-permute-start(f32[520,128]{1,0:T(8,128)S(1)} %get-tuple-element.49), channel_id=1, source_target_pairs={{0,1},{1,5},{2,0},{3,4},{4,3},{5,7},{6,2},{7,6},{8,9},{9,13},{10,8... | collective-permute-start | bytes 798728 | tf_op jit(solution)/shard_map/ppermute | solution.py:58
  82.1 1.9 %collective-permute-start.17 = (f32[264,512]{1,0:T(8,128)S(1)}, f32[264,512]{1,0:T(8,128)S(1)}, u32[]{:S(2)}, u32[]{:S(2)}) collective-permute-start(f32[264,512]{1,0:T(8,128)S(1)} %collective-permute-done.13.refs_3_), channel_id=1, source_target_pairs={{0,4},{1,5},{2,6},{3,7},{4,0},{5,1},{6,2},{7,3},{8,12},{9,13},{10,... | collective-permute-start | bytes 1622024 | tf_op jit(solution)/shard_map/ppermute | solution.py:58
  82.1 2.7 %collective-permute-start.16 = (f32[264,512]{1,0:T(8,128)S(1)}, f32[264,512]{1,0:T(8,128)S(1)}, u32[]{:S(2)}, u32[]{:S(2)}) collective-permute-start(f32[264,512]{1,0:T(8,128)S(1)} %collective-permute-done.12.refs_2_), channel_id=1, source_target_pairs={{0,4},{1,5},{2,6},{3,7},{4,0},{5,1},{6,2},{7,3},{8,12},{9,13},{10,... | collective-permute-start | bytes 1622024 | tf_op jit(solution)/shard_map/ppermute | solution.py:58
  82.6 3.0 %collective-permute-start.19 = (f32[264,512]{1,0:T(8,128)S(1)}, f32[264,512]{1,0:T(8,128)S(1)}, u32[]{:S(2)}, u32[]{:S(2)}) collective-permute-start(f32[264,512]{1,0:T(8,128)S(1)} %collective-permute-done.18.refs_6_), channel_id=1, source_target_pairs={{0,4},{1,5},{2,6},{3,7},{4,0},{5,1},{6,2},{7,3},{8,12},{9,13},{10,... | collective-permute-start | bytes 1622024 | tf_op jit(solution)/shard_map/ppermute | solution.py:58
  87.0 3.4 %collective-permute-start.20 = (f32[8,512]{1,0:T(8,128)S(1)}, f32[8,512]{1,0:T(8,128)S(1)}, u32[]{:S(2)}, u32[]{:S(2)}) collective-permute-start(f32[8,512]{1,0:T(8,128)S(1)} %get-tuple-element.53), channel_id=1, source_target_pairs={{228,196},{236,204},{244,212},{252,220},{229,197},{237,205},{245,2... | collective-permute-start | bytes 49160 | tf_op jit(solution)/shard_map/ppermute | solution.py:442
  90.7 0.7 collective-permute-start.21
  91.7 0.7 collective-permute-start.22
  92.6 0.7 collective-permute-start.23
  93.6 0.7 collective-permute-start.24
  94.5 0.7 collective-permute-start.25
  95.5 21.6 %collective-permute-start.26 = (f32[8,512]{1,0:T(8,128)S(1)}, f32[8,512]{1,0:T(8,128)S(1)}, u32[]{:S(2)}, u32[]{:S(2)}) collective-permute-start(f32[8,512]{1,0:T(8,128)S(1)} %get-tuple-element.65), channel_id=1, source_target_pairs={{36,4},{44,12},{52,20},{60,28},{37,5},{45,13},{53,21},{61,29},{38,... | collective-permute-start | bytes 49160 | tf_op jit(solution)/shard_map/ppermute | solution.py:442
  117.0 2.1 %collective-permute-start.27 = (f32[8,512]{1,0:T(8,128)S(1)}, f32[8,512]{1,0:T(8,128)S(1)}, u32[]{:S(2)}, u32[]{:S(2)}) collective-permute-start(f32[8,512]{1,0:T(8,128)S(1)} %add.3.carried_ref), channel_id=1, source_target_pairs={{4,0},{12,8},{20,16},{28,24},{36,32},{44,40},{52,48},{60,56},{68,6... | collective-permute-start | bytes 49160 | tf_op jit(solution)/shard_map/ppermute | solution.py:444
